TPU v7x, 32 devices: a whole 2x2x4 slice. The times are simulated.
32 devices in a mesh: groups: 2 (over y), section: 16 (over z, x, core).
Axes of the slice: x: 2, y: 2, z: 4, core: 2. Of those that a mesh axis runs over, the one named last changes fastest.
Arguments:
- held: bfloat16 [16, 128, 4096], P('section', 'groups'), parts along dimension 1, may hold values from 0 to 2
- tile_values: bfloat16 [4608, 128, 128], P('section'), may hold values from -0.25 to 0.25
- tile_rows: int32 [4608], P('section'), may hold values from 0 to 255
- tile_cols: int32 [4608], P('section'), may hold values from 0 to 31
- tile_count: int32 [16], P('section'), may hold values from 1 to 288, as said below
- bias: float32 [65536], P('section'), may hold values from -0.5 to -0.2
Outputs:
- settled: bfloat16 [16, 128, 4096], P('section', 'groups'), parts along dimension 1
There are 2 independent parts, one for each index of `groups`. A program takes and returns all parts, laid end to end along the dimension named above; an argument that names none is the same for every part. Nothing has to cross between parts.
Inputs may be any that keep to these rules, and one draw needn't show every extreme that they name: `tile_count`: slots at or after a list's count are ignored; in every draw some list has all 288 slots live. `tile_rows`: pairs of tile row and tile column may repeat within a list; repeated tiles add.
All inputs are finite; a program needn't handle non-finite values.
Results may differ from a plain program's by a relative error of at most 0.0053.
Values may be sent and summed in bfloat16 or wider, within the bound.
No kernel may reach another device: no remote copies, remote signals or barrier semaphores. Data moves between devices by JAX's collectives and lax.ppermute only.
A program may use at most 64 MiB of HBM per device.

v0:
```python
import jax
import jax.numpy as jnp
from jax import lax
from jax.sharding import PartitionSpec as P

TILE = 128
NTILES = 256
SPLIT = 8
TICKS = 2
COLT = 32


def swapped(array, axis, bit):
    return lax.ppermute(array, axis, [(i, i ^ 1 << bit) for i in range(lax.axis_size(axis))])


def from_behind(array, axis, by):
    peers = lax.axis_size(axis)
    return lax.ppermute(array, axis, [(i, (i + by) % peers) for i in range(peers)])


def layer_slab(full_input, rows_list, cols_list, live_count, values_list, bias_slab):
    batch_rows = full_input.shape[0]
    slots = rows_list.shape[0]
    blocks = full_input.reshape(batch_rows, NTILES, TILE)
    live = jnp.arange(slots, dtype=jnp.int32) < live_count
    picked = jnp.take(blocks, rows_list, axis=1)
    picked = jnp.where(live[None, :, None], picked, jnp.zeros_like(picked))
    products = jnp.einsum("bck,ckj->cbj", picked, values_list, preferred_element_type=jnp.float32)
    summed = jax.ops.segment_sum(products, cols_list, num_segments=COLT)
    summed = summed.transpose(1, 0, 2).reshape(batch_rows, COLT * TILE)
    return jnp.maximum(summed + bias_slab[None, :], 0.0).astype(jnp.bfloat16)


def assemble(slab_part):
    position = lax.axis_index("section") % SPLIT
    joined = slab_part
    for bit_index in range(SPLIT.bit_length() - 1):
        partner = swapped(joined, "section", bit_index)
        upper_half = (position >> bit_index) % 2 == 1
        joined = jnp.where(
            upper_half,
            jnp.concatenate([partner, joined], axis=1),
            jnp.concatenate([joined, partner], axis=1),
        )
    return joined


def on_device(held, tile_values, tile_rows, tile_cols, tile_count, bias):
    live_count = tile_count[0]
    full_input = assemble(held[0])
    result = held[0]
    for tick_index in range(TICKS):
        result = layer_slab(full_input, tile_rows, tile_cols, live_count, tile_values, bias)
        if tick_index + 1 < TICKS:
            whole_output = assemble(result)
            full_input = from_behind(whole_output, "section", SPLIT)
    return result[None]


def solution(mesh):
    return jax.shard_map(
        on_device,
        mesh=mesh,
        in_specs=(
            P("section", "groups", None),
            P("section", None, None),
            P("section"),
            P("section"),
            P("section"),
            P("section"),
        ),
        out_specs=P("section", "groups", None),
        check_vma=False,
    )
```

profile of v0, /device:TPU:0, one launch (start us, length us, event | category | flops | bytes accessed | tf_op | source)
XLA Modules:
  0.0 440.8 jit_solution(5128049430844454706)
XLA Ops:
  0.0 0.0 copy-start
  0.0 0.5 collective-permute-start
  0.5 0.0 copy-start.3
  0.5 1.7 collective-permute-done
  2.2 1.5 maximum_select_fusion.5
  3.7 2.9 collective-permute-start.1
  6.6 23.5 %collective-permute-done.1 = bf16[64,8192]{1,0:T(8,128)(2,1)S(1)} collective-permute-done((bf16[64,8192]{1,0:T(8,128)(2,1)S(1)}, bf16[64,8192]{1,0:T(8,128)(2,1)S(1)}, u32[]{:S(2)}, u32[]{:S(2)}) %collective-permute-start.1) | collective-permute-done | bytes 1048608 | tf_op jit(solution)/shard_map/ppermute | solution.py:14
  30.0 1.8 maximum_select_fusion.2
  31.9 1.8 collective-permute-start.2
  33.7 0.0 copy-done
  33.7 0.1 copy.23
  33.8 0.2 copy.8
  34.7 0.0 copy-done.3
  34.7 0.1 copy_bitcast_fusion.3
  34.9 0.2 maximum_select_fusion.6
  35.0 0.3 copy_bitcast_fusion.2
  35.3 0.3 maximum_select_fusion.3
  35.7 43.7 %collective-permute-done.2 = bf16[64,16384]{1,0:T(8,128)(2,1)} collective-permute-done((bf16[64,16384]{1,0:T(8,128)(2,1)}, bf16[64,16384]{1,0:T(8,128)(2,1)}, u32[]{:S(2)}, u32[]{:S(2)}) %collective-permute-start.2) | collective-permute-done | bytes 2097184 | tf_op jit(solution)/shard_map/ppermute | solution.py:14
  79.4 2.2 copy_bitcast_fusion.1
  81.5 2.6 maximum_select_fusion
  84.2 5.7 %gather_fusion = bf16[288,64,128]{2,1,0:T(8,128)(2,1)} fusion(bf16[64,256,128]{2,0,1:T(8,128)(2,1)} %maximum_select_fusion, s32[1024]{0:T(1024)S(1)} %pad_clamp_fusion), kind=kCustom, calls=%fused_computation.clone | custom fusion | bytes 9438336 | tf_op jit(solution)/shard_map/jit(_take)/gather | solution.py:27
  89.9 0.0 copy-start.2
  89.9 11.4 %fusion.1 = f32[288,64,128]{2,1,0:T(8,128)} fusion(bf16[288,128,128]{2,1,0:T(8,128)(2,1)} %param.9, bf16[288,64,128]{2,1,0:T(8,128)(2,1)} %gather_fusion, pred[288]{0:T(512)(128)(4,1)S(1)} %get-tuple-element.7, pred[288]{0:T(512)(128)(4,1)S(1)} %get-tuple-element.6), kind=kOutput, calls=%fused_computation.7 | convolution fusion | flops 608698368 | bytes 23593536 | tf_op jit(solution)/shard_map/bck,ckj->cbj/dot_general | solution.py:29
  101.3 0.1 broadcast.56.clone
  101.4 0.0 copy-done.2
  101.4 0.0 copy-start.1
  101.5 29.8 %scatter_fusion = f32[32,64,128]{2,1,0:T(8,128)S(1)} fusion(f32[32,64,128]{2,1,0:T(8,128)S(1)} %broadcast.56.clone, s32[288]{0:T(512)S(1)} %copy-done.2, f32[288,64,128]{2,1,0:T(8,128)} %fusion.1), kind=kCustom, calls=%fused_computation.2 | custom fusion | flops 2359296 | bytes 28312704 | tf_op jit(solution)/shard_map/scatter-add | solution.py:30
  131.3 0.0 copy-done.1
  131.3 0.1 fusion.13
  131.4 0.1 collective-permute-start.3
  131.4 1.9 collective-permute-done.3
  133.3 0.2 maximum_select_fusion.7
  133.6 1.5 collective-permute-start.4
  135.1 23.8 %collective-permute-done.4 = bf16[64,8192]{1,0:T(8,128)(2,1)S(1)} collective-permute-done((bf16[64,8192]{1,0:T(8,128)(2,1)S(1)}, bf16[64,8192]{1,0:T(8,128)(2,1)S(1)}, u32[]{:S(2)}, u32[]{:S(2)}) %collective-permute-start.4) | collective-permute-done | bytes 1048608 | tf_op jit(solution)/shard_map/ppermute | solution.py:14
  158.9 0.5 maximum_select_fusion.4
  159.3 1.6 collective-permute-start.5
  160.9 45.3 %collective-permute-done.5 = bf16[64,16384]{1,0:T(8,128)(2,1)S(1)} collective-permute-done((bf16[64,16384]{1,0:T(8,128)(2,1)S(1)}, bf16[64,16384]{1,0:T(8,128)(2,1)S(1)}, u32[]{:S(2)}, u32[]{:S(2)}) %collective-permute-start.5) | collective-permute-done | bytes 2097184 | tf_op jit(solution)/shard_map/ppermute | solution.py:14
  206.2 1.0 maximum_select_fusion.1
  207.2 2.6 collective-permute-start.6
  209.8 179.1 %collective-permute-done.6 = bf16[64,32768]{1,0:T(8,128)(2,1)S(1)} collective-permute-done((bf16[64,32768]{1,0:T(8,128)(2,1)S(1)}, bf16[64,32768]{1,0:T(8,128)(2,1)S(1)}, u32[]{:S(2)}, u32[]{:S(2)}) %collective-permute-start.6) | collective-permute-done | bytes 4194336 | tf_op jit(solution)/shard_map/ppermute | solution.py:19
  388.9 3.2 copy_bitcast_fusion
  392.1 5.7 %gather_fusion.1 = bf16[288,64,128]{2,1,0:T(8,128)(2,1)} fusion(bf16[64,256,128]{2,0,1:T(8,128)(2,1)} %copy_bitcast_fusion, s32[1024]{0:T(1024)S(1)} %pad_clamp_fusion), kind=kCustom, calls=%fused_computation.1.clone | custom fusion | bytes 9438336 | tf_op jit(solution)/shard_map/jit(_take)/gather | solution.py:27
  397.8 11.4 %fusion = f32[288,64,128]{2,1,0:T(8,128)} fusion(bf16[288,128,128]{2,1,0:T(8,128)(2,1)} %param.9, bf16[288,64,128]{2,1,0:T(8,128)(2,1)} %gather_fusion.1, pred[288]{0:T(512)(128)(4,1)S(1)} %get-tuple-element.7, pred[288]{0:T(512)(128)(4,1)S(1)} %get-tuple-element.6), kind=kOutput, calls=%fused_computation.5 | convolution fusion | flops 608698368 | bytes 23593536 | tf_op jit(solution)/shard_map/bck,ckj->cbj/dot_general | solution.py:29
  409.2 0.1 broadcast.56
  409.3 29.8 %scatter_fusion.1 = f32[32,64,128]{2,1,0:T(8,128)S(1)} fusion(f32[32,64,128]{2,1,0:T(8,128)S(1)} %broadcast.56, s32[288]{0:T(512)S(1)} %copy-done.2, f32[288,64,128]{2,1,0:T(8,128)} %fusion), kind=kCustom, calls=%fused_computation.3 | custom fusion | flops 2359296 | bytes 28312704 | tf_op jit(solution)/shard_map/scatter-add | solution.py:30
  439.1 0.6 copy.17
  439.8 0.2 reshape.72
  440.0 0.9 maximum_convert_fusion
  (3 shorter events, 0.0 us)
Async XLA Ops:
  0.0 33.7 %copy-start = (bf16[1,64,4096]{2,1,0:T(8,128)(2,1)S(1)}, bf16[1,64,4096]{2,1,0:T(8,128)(2,1)}, u32[]{:S(2)}) copy-start(bf16[1,64,4096]{2,1,0:T(8,128)(2,1)} %param.8) | copy-start | bytes 1572868
  0.0 2.2 collective-permute-start
  0.5 34.2 %copy-start.3 = (s32[288]{0:T(512)S(1)}, s32[288]{0:T(512)}, u32[]{:S(2)}) copy-start(s32[288]{0:T(512)} %param.10) | copy-start | bytes 3460
  3.7 26.4 %collective-permute-start.1 = (bf16[64,8192]{1,0:T(8,128)(2,1)S(1)}, bf16[64,8192]{1,0:T(8,128)(2,1)S(1)}, u32[]{:S(2)}, u32[]{:S(2)}) collective-permute-start(bf16[64,8192]{1,0:T(8,128)(2,1)S(1)} %maximum_select_fusion.5), channel_id=1, source_target_pairs={{0,2},{1,3},{2,0},{3,1},{4,6},{5,7},{6,4},{7,5},{8,10},{9,11},{10,... | collective-permute-start | bytes 3145736 | tf_op jit(solution)/shard_map/ppermute | solution.py:14
  31.9 47.5 %collective-permute-start.2 = (bf16[64,16384]{1,0:T(8,128)(2,1)}, bf16[64,16384]{1,0:T(8,128)(2,1)}, u32[]{:S(2)}, u32[]{:S(2)}) collective-permute-start(bf16[64,16384]{1,0:T(8,128)(2,1)} %maximum_select_fusion.2), channel_id=1, source_target_pairs={{0,4},{1,5},{2,6},{3,7},{4,0},{5,1},{6,2},{7,3},{8,12},{9,13},{10,... | collective-permute-start | bytes 6291464 | tf_op jit(solution)/shard_map/ppermute | solution.py:14
  89.9 11.5 %copy-start.2 = (s32[288]{0:T(512)S(1)}, s32[288]{0:T(512)}, u32[]{:S(2)}) copy-start(s32[288]{0:T(512)} %param.11) | copy-start | bytes 3460
  101.4 29.8 %copy-start.1 = (f32[4096]{0:T(1024)S(1)}, f32[4096]{0:T(1024)}, u32[]{:S(2)}) copy-start(f32[4096]{0:T(1024)} %param.13) | copy-start | bytes 49156
  131.4 2.0 collective-permute-start.3
  133.6 25.3 %collective-permute-start.4 = (bf16[64,8192]{1,0:T(8,128)(2,1)S(1)}, bf16[64,8192]{1,0:T(8,128)(2,1)S(1)}, u32[]{:S(2)}, u32[]{:S(2)}) collective-permute-start(bf16[64,8192]{1,0:T(8,128)(2,1)S(1)} %maximum_select_fusion.7), channel_id=1, source_target_pairs={{0,2},{1,3},{2,0},{3,1},{4,6},{5,7},{6,4},{7,5},{8,10},{9,11},{10,... | collective-permute-start | bytes 3145736 | tf_op jit(solution)/shard_map/ppermute | solution.py:14
  159.3 46.9 %collective-permute-start.5 = (bf16[64,16384]{1,0:T(8,128)(2,1)S(1)}, bf16[64,16384]{1,0:T(8,128)(2,1)S(1)}, u32[]{:S(2)}, u32[]{:S(2)}) collective-permute-start(bf16[64,16384]{1,0:T(8,128)(2,1)S(1)} %maximum_select_fusion.4), channel_id=1, source_target_pairs={{0,4},{1,5},{2,6},{3,7},{4,0},{5,1},{6,2},{7,3},{8,12},{9,13},{10,... | collective-permute-start | bytes 6291464 | tf_op jit(solution)/shard_map/ppermute | solution.py:14
  207.2 181.7 %collective-permute-start.6 = (bf16[64,32768]{1,0:T(8,128)(2,1)S(1)}, bf16[64,32768]{1,0:T(8,128)(2,1)S(1)}, u32[]{:S(2)}, u32[]{:S(2)}) collective-permute-start(bf16[64,32768]{1,0:T(8,128)(2,1)S(1)} %maximum_select_fusion.1), channel_id=1, source_target_pairs={{0,8},{1,9},{2,10},{3,11},{4,12},{5,13},{6,14},{7,15},{8,0},{9,1},... | collective-permute-start | bytes 12582920 | tf_op jit(solution)/shard_map/ppermute | solution.py:19
where the time goes:
time: 443 us; the launch traced here: 441 us
  waiting for transfers between devices  319 us (72%)
  other arithmetic  68.7 us (16%)
  matrix products  22.8 us (5%)
  local copies, waits for them, and re-layouts  18.6 us (4%)
  starting transfers between devices  10.9 us (2%)
    ppermute x1, waiting for transfers between devices, from_behind(): lax.ppermute(array, axis, [(i, (i + by) % peers) for i in range(peers)])  179 us
    ppermute x6, waiting for transfers between devices, swapped(): lax.ppermute(array, axis, [(i, i ^ 1 << bit) for i in range(lax.axis_size...  140 us
    scatter-add x2, other arithmetic, layer_slab(): summed = jax.ops.segment_sum(products, cols_list, num_segments=COLT)  59.6 us
    dot_general x2, matrix products, layer_slab(): jnp.einsum('bck,ckj->cbj', picked, values_list, preferred_element_type=jn...  22.8 us
    gather x2, local copies, waits for them, and re-layouts, layer_slab(): picked = jnp.take(blocks, rows_list, axis=1)  11.5 us
  transfers between devices with their start and end apart: 7, of which 7 were waited for; matrix products, arithmetic and copies ran while one was open for 0% of the time, Pallas kernels for 0%

commit v1 on v0

v1 whole, which is shorter than its diff:
```python
import functools

import jax
import jax.numpy as jnp
from jax import lax
from jax.experimental import pallas as pl
from jax.experimental.pallas import tpu as pltpu
from jax.sharding import PartitionSpec as P

TILE = 128
SPLIT = 8
TICKS = 2
UNROLL = 8


def flipped(array, bit):
    peers = lax.axis_size("section")
    return lax.ppermute(array, "section", [(i, i ^ bit) for i in range(peers)])


def from_behind(array):
    peers = lax.axis_size("section")
    return lax.ppermute(array, "section", [(i, (i + SPLIT) % peers) for i in range(peers)])


def slot_lists(rows, cols, count, position, slab_tiles, trash):
    slots = rows.shape[0]
    index = jnp.arange(slots, dtype=jnp.int32)
    live = index < count
    group = jnp.where(live, (rows // slab_tiles) ^ position, SPLIT)
    member = group[:, None] == jnp.arange(SPLIT, dtype=jnp.int32)[None, :]
    steps = (jnp.sum(member, axis=0, dtype=jnp.int32) + UNROLL - 1) // UNROLL
    lower = jnp.arange(SPLIT + 1)[:, None] > jnp.arange(SPLIT)[None, :]
    starts = jnp.sum(jnp.where(lower, steps[None, :], 0), axis=1, dtype=jnp.int32)
    before = (group[None, :] == group[:, None]) & (index[None, :] < index[:, None])
    rank = jnp.sum(before, axis=1, dtype=jnp.int32)
    base = jnp.sum(jnp.where(member, starts[None, :SPLIT] * UNROLL, 0), axis=1, dtype=jnp.int32)
    place = jnp.where(live, base + rank, -1)
    length = slots + SPLIT * UNROLL
    hit = place[None, :] == jnp.arange(length, dtype=jnp.int32)[:, None]
    empty = trash
    word = (index * 64 + rows % slab_tiles) * 64 + cols
    packed = jnp.sum(jnp.where(hit, (word - empty)[None, :], 0), axis=1, dtype=jnp.int32) + empty
    return starts, packed


def slab_kernel(groups, first, last, starts_ref, list_ref, w_ref, *refs):
    refs = list(refs)
    acc_in = None if first else refs.pop(0)
    bias_ref = refs.pop(0) if last else None
    pieces = [[refs.pop(0) for _ in range(n)] for _, n in groups]
    out_ref = refs.pop(0)
    acc = refs.pop(0) if last else out_ref
    if first:
        acc[...] = jnp.zeros_like(acc)
    else:
        acc[...] = acc_in[...]
    for (group, _), parts in zip(groups, pieces):

        def step(it, carry, parts=parts):
            products = []
            places = []
            for u in range(UNROLL):
                word = list_ref[it * UNROLL + u]
                at = pl.ds(pl.multiple_of(((word >> 6) & 63) * TILE, TILE), TILE)
                rows = [part[:, at] for part in parts]
                x = rows[0] if len(rows) == 1 else jnp.concatenate(rows, axis=0)
                products.append(jnp.dot(x, w_ref[word >> 12], preferred_element_type=jnp.float32))
                places.append(word & 63)
            for place, product in zip(places, products):
                acc[place] = acc[place] + product
            return carry

        lax.fori_loop(starts_ref[group], starts_ref[group + 1], step, 0)
    if last:
        for c in range(out_ref.shape[1] // TILE):
            at = slice(c * TILE, (c + 1) * TILE)
            out_ref[:, at] = jnp.maximum(acc[c] + bias_ref[:, at], 0.0).astype(out_ref.dtype)


def slab_step(groups, starts, packed, weights, acc, bias, pieces):
    first, last = acc is None, bias is not None
    tall = sum(piece.shape[0] for piece in pieces[0])
    wide = pieces[0][0].shape[1]
    smem = pl.BlockSpec(memory_space=pltpu.SMEM)
    vmem = pl.BlockSpec(memory_space=pltpu.VMEM)
    operands = [starts, packed, weights]
    if not first:
        operands.append(acc)
    if last:
        operands.append(bias)
    for parts in pieces:
        operands.extend(parts)
    shape = (wide // TILE + 1, tall, TILE)
    if last:
        out = jax.ShapeDtypeStruct((tall, wide), jnp.bfloat16)
        scratch = [pltpu.VMEM(shape, jnp.float32)]
    else:
        out = jax.ShapeDtypeStruct(shape, jnp.float32)
        scratch = []
    layout = tuple((g, len(parts)) for g, parts in zip(groups, pieces))
    share = len(groups) / SPLIT
    return pl.pallas_call(
        functools.partial(slab_kernel, layout, first, last),
        out_shape=out,
        in_specs=[smem, smem] + [vmem] * (len(operands) - 2),
        out_specs=vmem,
        scratch_shapes=scratch,
        compiler_params=pltpu.CompilerParams(vmem_limit_bytes=4 << 20),
        cost_estimate=pl.CostEstimate(
            flops=int(share * 2 * weights.size * tall * 8),
            bytes_accessed=int(share * weights.size * 2),
            transcendentals=0,
        ),
        name="slab_" + "".join(str(g) for g in groups),
    )(*operands)


def on_device(held, tile_values, tile_rows, tile_cols, tile_count, bias):
    position = lax.axis_index("section") % SPLIT
    wide = held.shape[2]
    starts, packed = slot_lists(tile_rows, tile_cols, tile_count[0], position, wide // TILE, wide // TILE)
    bias_row = bias[None, :]
    own = held[0]
    half = own.shape[0] // 2

    def finish(pieces):
        early = [0, 1, 2, 3, 4, 5]
        late = [6, 7]
        acc = slab_step(early, starts, packed, tile_values, None, None, [pieces[g] for g in early])
        return slab_step(late, starts, packed, tile_values, acc, bias_row, [pieces[g] for g in late])

    outs = []
    for own_half in (own[:half], own[half:]):
        quarter = own_half.shape[0] // 2
        core = flipped(own_half, 1)
        x = flipped(own_half, 2)
        z = flipped(own_half, 4)
        d0 = flipped(x[:quarter], 4)
        d1 = flipped(z[quarter:], 2)
        xc = flipped(x, 1)
        zc = flipped(z, 1)
        d0c = flipped(d0, 1)
        d1c = flipped(d1, 1)
        outs.append(finish([[own_half], [core], [x], [xc], [z], [zc], [d0, d1], [d0c, d1c]]))
    results = []
    for out in outs:
        mine = from_behind(out)
        core = flipped(mine, 1)
        z = flipped(mine, 4)
        x = flipped(mine, 2)
        d = flipped(z, 2)
        zc = flipped(z, 1)
        xc = flipped(x, 1)
        dc = flipped(d, 1)
        results.append(finish([[mine], [core], [x], [xc], [z], [zc], [d], [dc]]))
    return jnp.concatenate(results, axis=0)[None]


def solution(mesh):
    return jax.shard_map(
        on_device,
        mesh=mesh,
        in_specs=(
            P("section", "groups", None),
            P("section", None, None),
            P("section"),
            P("section"),
            P("section"),
            P("section"),
        ),
        out_specs=P("section", "groups", None),
        check_vma=False,
    )
```

time: 443 us -> 100 us (0.23)
  the two profiles are of different devices: /device:TPU:0 before, /device:TPU:25 now
where the time goes in v1:
time: 100 us; the launch traced here: 98.8 us
  Pallas kernels  35.6 us (36%)
  waiting for transfers between devices  35.5 us (36%)
  starting transfers between devices  19.8 us (20%)
  local copies, waits for them, and re-layouts  4.8 us (5%)
  other arithmetic  2.23 us (2%)
    pallas_call x8, Pallas kernels, slab_step(): pl.pallas_call(functools.partial(slab_kernel, layout, first, last), out_s...  35.6 us
    ppermute x32, waiting for transfers between devices, flipped(): return lax.ppermute(array, 'section', [(i, i ^ bit) for i in range(peers)])  22.2 us
    ppermute x32, starting transfers between devices, flipped(): return lax.ppermute(array, 'section', [(i, i ^ bit) for i in range(peers)])  19.6 us
    ppermute x2, waiting for transfers between devices, from_behind(): lax.ppermute(array, 'section', [(i, (i + SPLIT) % peers) for i in range(p...  13.3 us
    unnamed x4, local copies, waits for them, and re-layouts  3.68 us
  transfers between devices with their start and end apart: 34, of which 11 were waited for; matrix products, arithmetic and copies ran while one was open for 1% of the time, Pallas kernels for 33%

profile of v1, /device:TPU:25, one launch (start us, length us, event | category | flops | bytes accessed | tf_op | source)
XLA Modules:
  0.0 98.8 jit_solution(6082709424326279997)
XLA Ops:
  0.0 1.1 %slice_bitcast_fusion.1 = (bf16[32,4096]{1,0:T(8,128)(2,1)S(1)}, bf16[32,4096]{1,0:T(8,128)(2,1)S(1)}) fusion(bf16[1,64,4096]{2,1,0:T(8,128)(2,1)} %param.6), kind=kLoop, calls=%fused_computation.7 | loop fusion | bytes 1048576 | tf_op jit(solution)/shard_map/slice | solution.py:134
  1.1 1.3 %collective-permute-start.1 = (bf16[32,4096]{1,0:T(8,128)(2,1)S(1)}, bf16[32,4096]{1,0:T(8,128)(2,1)S(1)}, u32[]{:S(2)}, u32[]{:S(2)}) collective-permute-start(bf16[32,4096]{1,0:T(8,128)(2,1)S(1)} %get-tuple-element.5.refs_0_), channel_id=1, source_target_pairs={{0,2},{1,3},{2,0},{3,1},{4,6},{5,7},{6,4},{7,5},{8,10},{9,11},{10,... | collective-permute-start | bytes 786440 | tf_op jit(solution)/shard_map/ppermute | solution.py:18
  2.4 0.2 collective-permute-start.3
  2.5 1.2 %collective-permute-start = (bf16[32,4096]{1,0:T(8,128)(2,1)S(1)}, bf16[32,4096]{1,0:T(8,128)(2,1)S(1)}, u32[]{:S(2)}, u32[]{:S(2)}) collective-permute-start(bf16[32,4096]{1,0:T(8,128)(2,1)S(1)} %get-tuple-element.5.refs_0_), channel_id=1, source_target_pairs={{0,1},{1,0},{2,3},{3,2},{4,5},{5,4},{6,7},{7,6},{8,9},{9,8},{10,11... | collective-permute-start | bytes 786440 | tf_op jit(solution)/shard_map/ppermute | solution.py:18
  3.8 0.3 collective-permute-start.18
  4.0 1.3 %collective-permute-start.20 = (bf16[32,4096]{1,0:T(8,128)(2,1)S(1)}, bf16[32,4096]{1,0:T(8,128)(2,1)S(1)}, u32[]{:S(2)}, u32[]{:S(2)}) collective-permute-start(bf16[32,4096]{1,0:T(8,128)(2,1)S(1)} %get-tuple-element.6.refs_0_), channel_id=1, source_target_pairs={{0,4},{1,5},{2,6},{3,7},{4,0},{5,1},{6,2},{7,3},{8,12},{9,13},{10,... | collective-permute-start | bytes 786440 | tf_op jit(solution)/shard_map/ppermute | solution.py:18
  6.0 0.7 fusion.6
  6.7 0.1 convert_reduce_fusion.1
  6.8 0.1 select_reduce_fusion.2.starts_ref
  6.9 0.2 convert_reduce_fusion
  7.1 0.1 select_reduce_fusion.1
  7.2 1.1 %collective-permute-done.1.refs_2_ = bf16[32,4096]{1,0:T(8,128)(2,1)S(1)} collective-permute-done((bf16[32,4096]{1,0:T(8,128)(2,1)S(1)}, bf16[32,4096]{1,0:T(8,128)(2,1)S(1)}, u32[]{:S(2)}, u32[]{:S(2)}) %collective-permute-start.1) | collective-permute-done | bytes 262176 | tf_op jit(solution)/shard_map/ppermute | solution.py:18
  8.3 0.2 collective-permute-start.5
  8.6 0.6 collective-permute-done.3.refs_4_
  9.2 0.6 collective-permute-start.6
  9.9 4.1 %collective-permute-done.18.refs_2_ = bf16[32,4096]{1,0:T(8,128)(2,1)S(1)} collective-permute-done((bf16[32,4096]{1,0:T(8,128)(2,1)S(1)}, bf16[32,4096]{1,0:T(8,128)(2,1)S(1)}, u32[]{:S(2)}, u32[]{:S(2)}) %collective-permute-start.18) | collective-permute-done | bytes 262176 | tf_op jit(solution)/shard_map/ppermute | solution.py:18
  14.0 0.2 collective-permute-start.22
  14.2 0.6 collective-permute-done.20.refs_4_
  14.8 0.6 collective-permute-start.23
  15.5 3.3 %collective-permute-start.2 = (bf16[32,4096]{1,0:T(8,128)(2,1)S(1)}, bf16[32,4096]{1,0:T(8,128)(2,1)S(1)}, u32[]{:S(2)}, u32[]{:S(2)}) collective-permute-start(bf16[32,4096]{1,0:T(8,128)(2,1)S(1)} %collective-permute-done.1.refs_2_), channel_id=1, source_target_pairs={{0,1},{1,0},{2,3},{3,2},{4,5},{5,4},{6,7},{7,6},{8,9},{9,8},{10,11... | collective-permute-start | bytes 786440 | tf_op jit(solution)/shard_map/ppermute | solution.py:18
  18.7 0.0 collective-permute-done.5.refs_2_
  18.7 2.2 %collective-permute-start.4 = (bf16[32,4096]{1,0:T(8,128)(2,1)S(1)}, bf16[32,4096]{1,0:T(8,128)(2,1)S(1)}, u32[]{:S(2)}, u32[]{:S(2)}) collective-permute-start(bf16[32,4096]{1,0:T(8,128)(2,1)S(1)} %collective-permute-done.3.refs_4_), channel_id=1, source_target_pairs={{0,1},{1,0},{2,3},{3,2},{4,5},{5,4},{6,7},{7,6},{8,9},{9,8},{10,11... | collective-permute-start | bytes 786440 | tf_op jit(solution)/shard_map/ppermute | solution.py:18
  20.9 0.2 select_reduce_fusion
  21.1 0.0 collective-permute-done.6.refs_3_
  21.1 0.1 collective-permute-start.17
  21.2 0.0 collective-permute-done.22.refs_2_
  21.2 1.1 %collective-permute-start.19 = (bf16[32,4096]{1,0:T(8,128)(2,1)S(1)}, bf16[32,4096]{1,0:T(8,128)(2,1)S(1)}, u32[]{:S(2)}, u32[]{:S(2)}) collective-permute-start(bf16[32,4096]{1,0:T(8,128)(2,1)S(1)} %collective-permute-done.18.refs_2_), channel_id=1, source_target_pairs={{0,1},{1,0},{2,3},{3,2},{4,5},{5,4},{6,7},{7,6},{8,9},{9,8},{10,11... | collective-permute-start | bytes 786440 | tf_op jit(solution)/shard_map/ppermute | solution.py:18
  22.3 0.0 collective-permute-done.23.refs_3_
  22.3 0.9 collective-permute-start.21
  23.2 0.1 collective-permute-start.7
  23.3 0.0 collective-permute-done.4.refs_5_
  23.3 0.4 collective-permute-start.8
  23.7 3.7 %copy-done = bf16[288,128,128]{2,1,0:T(8,128)(2,1)S(1)} copy-done((bf16[288,128,128]{2,1,0:T(8,128)(2,1)S(1)}, bf16[288,128,128]{2,1,0:T(8,128)(2,1)}, u32[]{:S(2)}) %copy-start) | copy-done | bytes 9437208
  27.4 6.3 %slab_012345.4.refs_0_ = f32[33,32,128]{2,1,0:T(8,128)S(1)} custom-call(s32[9]{0:T(128)S(1)} %select_reduce_fusion.2.starts_ref, s32[352]{0:T(512)S(1)} %broadcast_add_fusion.list_ref, bf16[288,128,128]{2,1,0:T(8,128)(2,1)S(1)} %copy-done, bf16[32,4096]{1,0:T(8,128)(2,1)S(1)} %get-tuple-element.5.refs_0_, bf16[32,4096]{1,0:T(8,128)(2,1)S(1)} %collective-permute-done.refs_1_, ...), custom_call_target="tpu_custom_call" | custom-call | flops 1811939328 | bytes 7077888 | tf_op jit(solution)/shard_map/slab_012345/pallas_call | solution.py:103
  33.7 0.1 collective-permute-start.24
  33.8 0.5 collective-permute-start.25
  34.3 2.6 %slab_67.4 = bf16[32,4096]{1,0:T(8,128)(2,1)S(1)} custom-call(s32[9]{0:T(128)S(1)} %select_reduce_fusion.2.starts_ref, s32[352]{0:T(512)S(1)} %broadcast_add_fusion.list_ref, bf16[288,128,128]{2,1,0:T(8,128)(2,1)S(1)} %copy-done, f32[33,32,128]{2,1,0:T(8,128)S(1)} %slab_012345.4.refs_0_, f32[1,4096]{1,0:T(1,128)S(1)} %bitcast.10, ...), custom_call_target="tpu_custom_call" | custom-call | flops 603979776 | bytes 2359296 | tf_op jit(solution)/shard_map/slab_67/pallas_call | solution.py:103
  36.9 0.0 collective-permute-done.17.refs_1_
  36.9 0.1 collective-permute-start.9
  37.0 0.0 collective-permute-done.19.refs_3_
  37.0 0.0 collective-permute-done.21.refs_5_
  37.0 6.3 %slab_012345.6.refs_0_ = f32[33,32,128]{2,1,0:T(8,128)S(1)} custom-call(s32[9]{0:T(128)S(1)} %select_reduce_fusion.2.starts_ref, s32[352]{0:T(512)S(1)} %broadcast_add_fusion.list_ref, bf16[288,128,128]{2,1,0:T(8,128)(2,1)S(1)} %copy-done, bf16[32,4096]{1,0:T(8,128)(2,1)S(1)} %get-tuple-element.6.refs_0_, ...), custom_call_target="tpu_custom_call" | custom-call | flops 1811939328 | bytes 7077888 | tf_op jit(solution)/shard_map/slab_012345/pallas_call | solution.py:103
  43.3 2.6 %slab_67.6 = bf16[32,4096]{1,0:T(8,128)(2,1)S(1)} custom-call(s32[9]{0:T(128)S(1)} %select_reduce_fusion.2.starts_ref, s32[352]{0:T(512)S(1)} %broadcast_add_fusion.list_ref, bf16[288,128,128]{2,1,0:T(8,128)(2,1)S(1)} %copy-done, f32[33,32,128]{2,1,0:T(8,128)S(1)} %slab_012345.6.refs_0_, f32[1,4096]{1,0:T(1,128)S(1)} %bitcast.11, ...), custom_call_target="tpu_custom_call" | custom-call | flops 603979776 | bytes 2359296 | tf_op jit(solution)/shard_map/slab_67/pallas_call | solution.py:103
  45.9 0.1 collective-permute-start.26
  46.0 8.1 %collective-permute-done.9.refs_0_ = bf16[32,4096]{1,0:T(8,128)(2,1)S(1)} collective-permute-done((bf16[32,4096]{1,0:T(8,128)(2,1)S(1)}, bf16[32,4096]{1,0:T(8,128)(2,1)S(1)}, u32[]{:S(2)}, u32[]{:S(2)}) %collective-permute-start.9) | collective-permute-done | bytes 262176 | tf_op jit(solution)/shard_map/ppermute | solution.py:23
  54.1 0.3 collective-permute-start.10
  54.4 5.3 %collective-permute-done.26.refs_0_ = bf16[32,4096]{1,0:T(8,128)(2,1)S(1)} collective-permute-done((bf16[32,4096]{1,0:T(8,128)(2,1)S(1)}, bf16[32,4096]{1,0:T(8,128)(2,1)S(1)}, u32[]{:S(2)}, u32[]{:S(2)}) %collective-permute-start.26) | collective-permute-done | bytes 262176 | tf_op jit(solution)/shard_map/ppermute | solution.py:23
  59.7 2.0 %collective-permute-done.11.refs_2_ = bf16[32,4096]{1,0:T(8,128)(2,1)S(1)} collective-permute-done((bf16[32,4096]{1,0:T(8,128)(2,1)S(1)}, bf16[32,4096]{1,0:T(8,128)(2,1)S(1)}, u32[]{:S(2)}, u32[]{:S(2)}) %collective-permute-start.11) | collective-permute-done | bytes 262176 | tf_op jit(solution)/shard_map/ppermute | solution.py:18
  61.6 1.1 %collective-permute-start.12 = (bf16[32,4096]{1,0:T(8,128)(2,1)S(1)}, bf16[32,4096]{1,0:T(8,128)(2,1)S(1)}, u32[]{:S(2)}, u32[]{:S(2)}) collective-permute-start(bf16[32,4096]{1,0:T(8,128)(2,1)S(1)} %collective-permute-done.11.refs_2_), channel_id=1, source_target_pairs={{0,1},{1,0},{2,3},{3,2},{4,5},{5,4},{6,7},{7,6},{8,9},{9,8},{10,11... | collective-permute-start | bytes 786440 | tf_op jit(solution)/shard_map/ppermute | solution.py:18
  62.8 2.4 %collective-permute-done.13.refs_4_ = bf16[32,4096]{1,0:T(8,128)(2,1)S(1)} collective-permute-done((bf16[32,4096]{1,0:T(8,128)(2,1)S(1)}, bf16[32,4096]{1,0:T(8,128)(2,1)S(1)}, u32[]{:S(2)}, u32[]{:S(2)}) %collective-permute-start.13) | collective-permute-done | bytes 262176 | tf_op jit(solution)/shard_map/ppermute | solution.py:18
  65.2 0.5 collective-permute-start.14
  65.7 5.1 %collective-permute-done.30.refs_4_ = bf16[32,4096]{1,0:T(8,128)(2,1)S(1)} collective-permute-done((bf16[32,4096]{1,0:T(8,128)(2,1)S(1)}, bf16[32,4096]{1,0:T(8,128)(2,1)S(1)}, u32[]{:S(2)}, u32[]{:S(2)}) %collective-permute-start.30) | collective-permute-done | bytes 262176 | tf_op jit(solution)/shard_map/ppermute | solution.py:18
  70.8 0.5 collective-permute-start.27
  71.3 0.1 collective-permute-start.29
  71.4 0.4 collective-permute-start.31
  71.8 1.9 %collective-permute-done.15.refs_2_ = bf16[32,4096]{1,0:T(8,128)(2,1)S(1)} collective-permute-done((bf16[32,4096]{1,0:T(8,128)(2,1)S(1)}, bf16[32,4096]{1,0:T(8,128)(2,1)S(1)}, u32[]{:S(2)}, u32[]{:S(2)}) %collective-permute-start.15) | collective-permute-done | bytes 262176 | tf_op jit(solution)/shard_map/ppermute | solution.py:18
  73.7 1.2 %collective-permute-start.16 = (bf16[32,4096]{1,0:T(8,128)(2,1)S(1)}, bf16[32,4096]{1,0:T(8,128)(2,1)S(1)}, u32[]{:S(2)}, u32[]{:S(2)}) collective-permute-start(bf16[32,4096]{1,0:T(8,128)(2,1)S(1)} %collective-permute-done.15.refs_2_), channel_id=1, source_target_pairs={{0,1},{1,0},{2,3},{3,2},{4,5},{5,4},{6,7},{7,6},{8,9},{9,8},{10,11... | collective-permute-start | bytes 786440 | tf_op jit(solution)/shard_map/ppermute | solution.py:18
  74.8 4.4 %collective-permute-done.32.refs_2_ = bf16[32,4096]{1,0:T(8,128)(2,1)S(1)} collective-permute-done((bf16[32,4096]{1,0:T(8,128)(2,1)S(1)}, bf16[32,4096]{1,0:T(8,128)(2,1)S(1)}, u32[]{:S(2)}, u32[]{:S(2)}) %collective-permute-start.32) | collective-permute-done | bytes 262176 | tf_op jit(solution)/shard_map/ppermute | solution.py:18
  79.2 0.8 collective-permute-start.33
  80.1 6.3 %slab_012345.5.refs_0_ = f32[33,32,128]{2,1,0:T(8,128)S(1)} custom-call(s32[9]{0:T(128)S(1)} %select_reduce_fusion.2.starts_ref, s32[352]{0:T(512)S(1)} %broadcast_add_fusion.list_ref, bf16[288,128,128]{2,1,0:T(8,128)(2,1)S(1)} %copy-done, bf16[32,4096]{1,0:T(8,128)(2,1)S(1)} %collective-permute-done.9.refs_0_, ...), custom_call_target="tpu_custom_call" | custom-call | flops 1811939328 | bytes 7077888 | tf_op jit(solution)/shard_map/slab_012345/pallas_call | solution.py:103
  86.4 6.3 %slab_012345.7.refs_0_ = f32[33,32,128]{2,1,0:T(8,128)S(1)} custom-call(s32[9]{0:T(128)S(1)} %select_reduce_fusion.2.starts_ref, s32[352]{0:T(512)S(1)} %broadcast_add_fusion.list_ref, bf16[288,128,128]{2,1,0:T(8,128)(2,1)S(1)} %copy-done, bf16[32,4096]{1,0:T(8,128)(2,1)S(1)} %collective-permute-done.26.refs_0_, ...), custom_call_target="tpu_custom_call" | custom-call | flops 1811939328 | bytes 7077888 | tf_op jit(solution)/shard_map/slab_012345/pallas_call | solution.py:103
  92.8 2.6 %slab_67.5 = bf16[32,4096]{1,0:T(8,128)(2,1)S(1)} custom-call(s32[9]{0:T(128)S(1)} %select_reduce_fusion.2.starts_ref, s32[352]{0:T(512)S(1)} %broadcast_add_fusion.list_ref, bf16[288,128,128]{2,1,0:T(8,128)(2,1)S(1)} %copy-done, f32[33,32,128]{2,1,0:T(8,128)S(1)} %slab_012345.5.refs_0_, f32[1,4096]{1,0:T(1,128)S(1)} %bitcast.12, ...), custom_call_target="tpu_custom_call" | custom-call | flops 603979776 | bytes 2359296 | tf_op jit(solution)/shard_map/slab_67/pallas_call | solution.py:103
  95.3 2.6 %slab_67.7 = bf16[32,4096]{1,0:T(8,128)(2,1)S(1)} custom-call(s32[9]{0:T(128)S(1)} %select_reduce_fusion.2.starts_ref, s32[352]{0:T(512)S(1)} %broadcast_add_fusion.list_ref, bf16[288,128,128]{2,1,0:T(8,128)(2,1)S(1)} %copy-done, f32[33,32,128]{2,1,0:T(8,128)S(1)} %slab_012345.7.refs_0_, f32[1,4096]{1,0:T(1,128)S(1)} %bitcast.13, ...), custom_call_target="tpu_custom_call" | custom-call | flops 603979776 | bytes 2359296 | tf_op jit(solution)/shard_map/slab_67/pallas_call | solution.py:103
  97.9 0.8 maximum_bitcast_fusion
  (32 shorter events, 0.1 us)
Async XLA Ops:
  0.0 34.3 %copy-start.1 = (f32[4096]{0:T(1024)S(1)}, f32[4096]{0:T(1024)}, u32[]{:S(2)}) copy-start(f32[4096]{0:T(1024)} %param.11) | copy-start | bytes 49156
  1.1 7.2 %collective-permute-start.1 = (bf16[32,4096]{1,0:T(8,128)(2,1)S(1)}, bf16[32,4096]{1,0:T(8,128)(2,1)S(1)}, u32[]{:S(2)}, u32[]{:S(2)}) collective-permute-start(bf16[32,4096]{1,0:T(8,128)(2,1)S(1)} %get-tuple-element.5.refs_0_), channel_id=1, source_target_pairs={{0,2},{1,3},{2,0},{3,1},{4,6},{5,7},{6,4},{7,5},{8,10},{9,11},{10,... | collective-permute-start | bytes 786440 | tf_op jit(solution)/shard_map/ppermute | solution.py:18
  2.4 6.9 %collective-permute-start.3 = (bf16[32,4096]{1,0:T(8,128)(2,1)S(1)}, bf16[32,4096]{1,0:T(8,128)(2,1)S(1)}, u32[]{:S(2)}, u32[]{:S(2)}) collective-permute-start(bf16[32,4096]{1,0:T(8,128)(2,1)S(1)} %get-tuple-element.5.refs_0_), channel_id=1, source_target_pairs={{0,4},{1,5},{2,6},{3,7},{4,0},{5,1},{6,2},{7,3},{8,12},{9,13},{10,... | collective-permute-start | bytes 786440 | tf_op jit(solution)/shard_map/ppermute | solution.py:18
  2.5 13.0 %collective-permute-start = (bf16[32,4096]{1,0:T(8,128)(2,1)S(1)}, bf16[32,4096]{1,0:T(8,128)(2,1)S(1)}, u32[]{:S(2)}, u32[]{:S(2)}) collective-permute-start(bf16[32,4096]{1,0:T(8,128)(2,1)S(1)} %get-tuple-element.5.refs_0_), channel_id=1, source_target_pairs={{0,1},{1,0},{2,3},{3,2},{4,5},{5,4},{6,7},{7,6},{8,9},{9,8},{10,11... | collective-permute-start | bytes 786440 | tf_op jit(solution)/shard_map/ppermute | solution.py:18
  3.8 10.2 %collective-permute-start.18 = (bf16[32,4096]{1,0:T(8,128)(2,1)S(1)}, bf16[32,4096]{1,0:T(8,128)(2,1)S(1)}, u32[]{:S(2)}, u32[]{:S(2)}) collective-permute-start(bf16[32,4096]{1,0:T(8,128)(2,1)S(1)} %get-tuple-element.6.refs_0_), channel_id=1, source_target_pairs={{0,2},{1,3},{2,0},{3,1},{4,6},{5,7},{6,4},{7,5},{8,10},{9,11},{10,... | collective-permute-start | bytes 786440 | tf_op jit(solution)/shard_map/ppermute | solution.py:18
  4.0 10.8 %collective-permute-start.20 = (bf16[32,4096]{1,0:T(8,128)(2,1)S(1)}, bf16[32,4096]{1,0:T(8,128)(2,1)S(1)}, u32[]{:S(2)}, u32[]{:S(2)}) collective-permute-start(bf16[32,4096]{1,0:T(8,128)(2,1)S(1)} %get-tuple-element.6.refs_0_), channel_id=1, source_target_pairs={{0,4},{1,5},{2,6},{3,7},{4,0},{5,1},{6,2},{7,3},{8,12},{9,13},{10,... | collective-permute-start | bytes 786440 | tf_op jit(solution)/shard_map/ppermute | solution.py:18
  8.3 10.4 %collective-permute-start.5 = (bf16[16,4096]{1,0:T(8,128)(2,1)S(1)}, bf16[16,4096]{1,0:T(8,128)(2,1)S(1)}, u32[]{:S(2)}, u32[]{:S(2)}) collective-permute-start(bf16[16,4096]{1,0:T(8,128)(2,1)S(1)} %slice.36), channel_id=1, source_target_pairs={{0,4},{1,5},{2,6},{3,7},{4,0},{5,1},{6,2},{7,3},{8,12},{9,13},{10,... | collective-permute-start | bytes 393224 | tf_op jit(solution)/shard_map/ppermute | solution.py:18
  9.2 11.8 %collective-permute-start.6 = (bf16[16,4096]{1,0:T(8,128)(2,1)S(1)}, bf16[16,4096]{1,0:T(8,128)(2,1)S(1)}, u32[]{:S(2)}, u32[]{:S(2)}) collective-permute-start(bf16[16,4096]{1,0:T(8,128)(2,1)S(1)} %slice.37), channel_id=1, source_target_pairs={{0,2},{1,3},{2,0},{3,1},{4,6},{5,7},{6,4},{7,5},{8,10},{9,11},{10,... | collective-permute-start | bytes 393224 | tf_op jit(solution)/shard_map/ppermute | solution.py:18
  14.0 7.2 %collective-permute-start.22 = (bf16[16,4096]{1,0:T(8,128)(2,1)S(1)}, bf16[16,4096]{1,0:T(8,128)(2,1)S(1)}, u32[]{:S(2)}, u32[]{:S(2)}) collective-permute-start(bf16[16,4096]{1,0:T(8,128)(2,1)S(1)} %slice.38), channel_id=1, source_target_pairs={{0,4},{1,5},{2,6},{3,7},{4,0},{5,1},{6,2},{7,3},{8,12},{9,13},{10,... | collective-permute-start | bytes 393224 | tf_op jit(solution)/shard_map/ppermute | solution.py:18
  14.8 7.5 %collective-permute-start.23 = (bf16[16,4096]{1,0:T(8,128)(2,1)S(1)}, bf16[16,4096]{1,0:T(8,128)(2,1)S(1)}, u32[]{:S(2)}, u32[]{:S(2)}) collective-permute-start(bf16[16,4096]{1,0:T(8,128)(2,1)S(1)} %slice.39), channel_id=1, source_target_pairs={{0,2},{1,3},{2,0},{3,1},{4,6},{5,7},{6,4},{7,5},{8,10},{9,11},{10,... | collective-permute-start | bytes 393224 | tf_op jit(solution)/shard_map/ppermute | solution.py:18
  15.5 7.7 %collective-permute-start.2 = (bf16[32,4096]{1,0:T(8,128)(2,1)S(1)}, bf16[32,4096]{1,0:T(8,128)(2,1)S(1)}, u32[]{:S(2)}, u32[]{:S(2)}) collective-permute-start(bf16[32,4096]{1,0:T(8,128)(2,1)S(1)} %collective-permute-done.1.refs_2_), channel_id=1, source_target_pairs={{0,1},{1,0},{2,3},{3,2},{4,5},{5,4},{6,7},{7,6},{8,9},{9,8},{10,11... | collective-permute-start | bytes 786440 | tf_op jit(solution)/shard_map/ppermute | solution.py:18
  18.7 4.5 %collective-permute-start.4 = (bf16[32,4096]{1,0:T(8,128)(2,1)S(1)}, bf16[32,4096]{1,0:T(8,128)(2,1)S(1)}, u32[]{:S(2)}, u32[]{:S(2)}) collective-permute-start(bf16[32,4096]{1,0:T(8,128)(2,1)S(1)} %collective-permute-done.3.refs_4_), channel_id=1, source_target_pairs={{0,1},{1,0},{2,3},{3,2},{4,5},{5,4},{6,7},{7,6},{8,9},{9,8},{10,11... | collective-permute-start | bytes 786440 | tf_op jit(solution)/shard_map/ppermute | solution.py:18
  21.1 15.8 %collective-permute-start.17 = (bf16[32,4096]{1,0:T(8,128)(2,1)S(1)}, bf16[32,4096]{1,0:T(8,128)(2,1)S(1)}, u32[]{:S(2)}, u32[]{:S(2)}) collective-permute-start(bf16[32,4096]{1,0:T(8,128)(2,1)S(1)} %get-tuple-element.6.refs_0_), channel_id=1, source_target_pairs={{0,1},{1,0},{2,3},{3,2},{4,5},{5,4},{6,7},{7,6},{8,9},{9,8},{10,11... | collective-permute-start | bytes 786440 | tf_op jit(solution)/shard_map/ppermute | solution.py:18
  21.2 15.8 %collective-permute-start.19 = (bf16[32,4096]{1,0:T(8,128)(2,1)S(1)}, bf16[32,4096]{1,0:T(8,128)(2,1)S(1)}, u32[]{:S(2)}, u32[]{:S(2)}) collective-permute-start(bf16[32,4096]{1,0:T(8,128)(2,1)S(1)} %collective-permute-done.18.refs_2_), channel_id=1, source_target_pairs={{0,1},{1,0},{2,3},{3,2},{4,5},{5,4},{6,7},{7,6},{8,9},{9,8},{10,11... | collective-permute-start | bytes 786440 | tf_op jit(solution)/shard_map/ppermute | solution.py:18
  22.3 14.7 %collective-permute-start.21 = (bf16[32,4096]{1,0:T(8,128)(2,1)S(1)}, bf16[32,4096]{1,0:T(8,128)(2,1)S(1)}, u32[]{:S(2)}, u32[]{:S(2)}) collective-permute-start(bf16[32,4096]{1,0:T(8,128)(2,1)S(1)} %collective-permute-done.20.refs_4_), channel_id=1, source_target_pairs={{0,1},{1,0},{2,3},{3,2},{4,5},{5,4},{6,7},{7,6},{8,9},{9,8},{10,11... | collective-permute-start | bytes 786440 | tf_op jit(solution)/shard_map/ppermute | solution.py:18
  23.2 10.5 %collective-permute-start.7 = (bf16[16,4096]{1,0:T(8,128)(2,1)S(1)}, bf16[16,4096]{1,0:T(8,128)(2,1)S(1)}, u32[]{:S(2)}, u32[]{:S(2)}) collective-permute-start(bf16[16,4096]{1,0:T(8,128)(2,1)S(1)} %collective-permute-done.5.refs_2_), channel_id=1, source_target_pairs={{0,1},{1,0},{2,3},{3,2},{4,5},{5,4},{6,7},{7,6},{8,9},{9,8},{10,11... | collective-permute-start | bytes 393224 | tf_op jit(solution)/shard_map/ppermute | solution.py:18
  23.3 10.5 %collective-permute-start.8 = (bf16[16,4096]{1,0:T(8,128)(2,1)S(1)}, bf16[16,4096]{1,0:T(8,128)(2,1)S(1)}, u32[]{:S(2)}, u32[]{:S(2)}) collective-permute-start(bf16[16,4096]{1,0:T(8,128)(2,1)S(1)} %collective-permute-done.6.refs_3_), channel_id=1, source_target_pairs={{0,1},{1,0},{2,3},{3,2},{4,5},{5,4},{6,7},{7,6},{8,9},{9,8},{10,11... | collective-permute-start | bytes 393224 | tf_op jit(solution)/shard_map/ppermute | solution.py:18
  23.7 3.7 %copy-start = (bf16[288,128,128]{2,1,0:T(8,128)(2,1)S(1)}, bf16[288,128,128]{2,1,0:T(8,128)(2,1)}, u32[]{:S(2)}) copy-start(bf16[288,128,128]{2,1,0:T(8,128)(2,1)} %w_ref.15) | copy-start | bytes 28311556
  33.7 9.6 %collective-permute-start.24 = (bf16[16,4096]{1,0:T(8,128)(2,1)S(1)}, bf16[16,4096]{1,0:T(8,128)(2,1)S(1)}, u32[]{:S(2)}, u32[]{:S(2)}) collective-permute-start(bf16[16,4096]{1,0:T(8,128)(2,1)S(1)} %collective-permute-done.22.refs_2_), channel_id=1, source_target_pairs={{0,1},{1,0},{2,3},{3,2},{4,5},{5,4},{6,7},{7,6},{8,9},{9,8},{10,11... | collective-permute-start | bytes 393224 | tf_op jit(solution)/shard_map/ppermute | solution.py:18
  33.8 9.5 %collective-permute-start.25 = (bf16[16,4096]{1,0:T(8,128)(2,1)S(1)}, bf16[16,4096]{1,0:T(8,128)(2,1)S(1)}, u32[]{:S(2)}, u32[]{:S(2)}) collective-permute-start(bf16[16,4096]{1,0:T(8,128)(2,1)S(1)} %collective-permute-done.23.refs_3_), channel_id=1, source_target_pairs={{0,1},{1,0},{2,3},{3,2},{4,5},{5,4},{6,7},{7,6},{8,9},{9,8},{10,11... | collective-permute-start | bytes 393224 | tf_op jit(solution)/shard_map/ppermute | solution.py:18
  36.9 17.2 %collective-permute-start.9 = (bf16[32,4096]{1,0:T(8,128)(2,1)S(1)}, bf16[32,4096]{1,0:T(8,128)(2,1)S(1)}, u32[]{:S(2)}, u32[]{:S(2)}) collective-permute-start(bf16[32,4096]{1,0:T(8,128)(2,1)S(1)} %slab_67.4), channel_id=1, source_target_pairs={{0,8},{1,9},{2,10},{3,11},{4,12},{5,13},{6,14},{7,15},{8,0},{9,1},... | collective-permute-start | bytes 786440 | tf_op jit(solution)/shard_map/ppermute | solution.py:23
  45.9 13.7 %collective-permute-start.26 = (bf16[32,4096]{1,0:T(8,128)(2,1)S(1)}, bf16[32,4096]{1,0:T(8,128)(2,1)S(1)}, u32[]{:S(2)}, u32[]{:S(2)}) collective-permute-start(bf16[32,4096]{1,0:T(8,128)(2,1)S(1)} %slab_67.6), channel_id=1, source_target_pairs={{0,8},{1,9},{2,10},{3,11},{4,12},{5,13},{6,14},{7,15},{8,0},{9,1},... | collective-permute-start | bytes 786440 | tf_op jit(solution)/shard_map/ppermute | solution.py:23
  54.1 7.6 %collective-permute-start.11 = (bf16[32,4096]{1,0:T(8,128)(2,1)S(1)}, bf16[32,4096]{1,0:T(8,128)(2,1)S(1)}, u32[]{:S(2)}, u32[]{:S(2)}) collective-permute-start(bf16[32,4096]{1,0:T(8,128)(2,1)S(1)} %collective-permute-done.9.refs_0_), channel_id=1, source_target_pairs={{0,2},{1,3},{2,0},{3,1},{4,6},{5,7},{6,4},{7,5},{8,10},{9,11},{10,... | collective-permute-start | bytes 786440 | tf_op jit(solution)/shard_map/ppermute | solution.py:18
  54.1 11.1 %collective-permute-start.13 = (bf16[32,4096]{1,0:T(8,128)(2,1)S(1)}, bf16[32,4096]{1,0:T(8,128)(2,1)S(1)}, u32[]{:S(2)}, u32[]{:S(2)}) collective-permute-start(bf16[32,4096]{1,0:T(8,128)(2,1)S(1)} %collective-permute-done.9.refs_0_), channel_id=1, source_target_pairs={{0,4},{1,5},{2,6},{3,7},{4,0},{5,1},{6,2},{7,3},{8,12},{9,13},{10,... | collective-permute-start | bytes 786440 | tf_op jit(solution)/shard_map/ppermute | solution.py:18
  54.1 11.7 %collective-permute-start.10 = (bf16[32,4096]{1,0:T(8,128)(2,1)S(1)}, bf16[32,4096]{1,0:T(8,128)(2,1)S(1)}, u32[]{:S(2)}, u32[]{:S(2)}) collective-permute-start(bf16[32,4096]{1,0:T(8,128)(2,1)S(1)} %collective-permute-done.9.refs_0_), channel_id=1, source_target_pairs={{0,1},{1,0},{2,3},{3,2},{4,5},{5,4},{6,7},{7,6},{8,9},{9,8},{10,11... | collective-permute-start | bytes 786440 | tf_op jit(solution)/shard_map/ppermute | solution.py:18
  59.7 11.2 %collective-permute-start.30 = (bf16[32,4096]{1,0:T(8,128)(2,1)S(1)}, bf16[32,4096]{1,0:T(8,128)(2,1)S(1)}, u32[]{:S(2)}, u32[]{:S(2)}) collective-permute-start(bf16[32,4096]{1,0:T(8,128)(2,1)S(1)} %collective-permute-done.26.refs_0_), channel_id=1, source_target_pairs={{0,4},{1,5},{2,6},{3,7},{4,0},{5,1},{6,2},{7,3},{8,12},{9,13},{10,... | collective-permute-start | bytes 786440 | tf_op jit(solution)/shard_map/ppermute | solution.py:18
  59.7 11.2 %collective-permute-start.28 = (bf16[32,4096]{1,0:T(8,128)(2,1)S(1)}, bf16[32,4096]{1,0:T(8,128)(2,1)S(1)}, u32[]{:S(2)}, u32[]{:S(2)}) collective-permute-start(bf16[32,4096]{1,0:T(8,128)(2,1)S(1)} %collective-permute-done.26.refs_0_), channel_id=1, source_target_pairs={{0,2},{1,3},{2,0},{3,1},{4,6},{5,7},{6,4},{7,5},{8,10},{9,11},{10,... | collective-permute-start | bytes 786440 | tf_op jit(solution)/shard_map/ppermute | solution.py:18
  61.6 9.7 %collective-permute-start.12 = (bf16[32,4096]{1,0:T(8,128)(2,1)S(1)}, bf16[32,4096]{1,0:T(8,128)(2,1)S(1)}, u32[]{:S(2)}, u32[]{:S(2)}) collective-permute-start(bf16[32,4096]{1,0:T(8,128)(2,1)S(1)} %collective-permute-done.11.refs_2_), channel_id=1, source_target_pairs={{0,1},{1,0},{2,3},{3,2},{4,5},{5,4},{6,7},{7,6},{8,9},{9,8},{10,11... | collective-permute-start | bytes 786440 | tf_op jit(solution)/shard_map/ppermute | solution.py:18
  65.2 6.2 %collective-permute-start.14 = (bf16[32,4096]{1,0:T(8,128)(2,1)S(1)}, bf16[32,4096]{1,0:T(8,128)(2,1)S(1)}, u32[]{:S(2)}, u32[]{:S(2)}) collective-permute-start(bf16[32,4096]{1,0:T(8,128)(2,1)S(1)} %collective-permute-done.13.refs_4_), channel_id=1, source_target_pairs={{0,1},{1,0},{2,3},{3,2},{4,5},{5,4},{6,7},{7,6},{8,9},{9,8},{10,11... | collective-permute-start | bytes 786440 | tf_op jit(solution)/shard_map/ppermute | solution.py:18
  65.7 7.9 %collective-permute-start.15 = (bf16[32,4096]{1,0:T(8,128)(2,1)S(1)}, bf16[32,4096]{1,0:T(8,128)(2,1)S(1)}, u32[]{:S(2)}, u32[]{:S(2)}) collective-permute-start(bf16[32,4096]{1,0:T(8,128)(2,1)S(1)} %collective-permute-done.13.refs_4_), channel_id=1, source_target_pairs={{0,2},{1,3},{2,0},{3,1},{4,6},{5,7},{6,4},{7,5},{8,10},{9,11},{10,... | collective-permute-start | bytes 786440 | tf_op jit(solution)/shard_map/ppermute | solution.py:18
  70.8 8.4 %collective-permute-start.32 = (bf16[32,4096]{1,0:T(8,128)(2,1)S(1)}, bf16[32,4096]{1,0:T(8,128)(2,1)S(1)}, u32[]{:S(2)}, u32[]{:S(2)}) collective-permute-start(bf16[32,4096]{1,0:T(8,128)(2,1)S(1)} %collective-permute-done.30.refs_4_), channel_id=1, source_target_pairs={{0,2},{1,3},{2,0},{3,1},{4,6},{5,7},{6,4},{7,5},{8,10},{9,11},{10,... | collective-permute-start | bytes 786440 | tf_op jit(solution)/shard_map/ppermute | solution.py:18
  70.8 15.6 %collective-permute-start.27 = (bf16[32,4096]{1,0:T(8,128)(2,1)S(1)}, bf16[32,4096]{1,0:T(8,128)(2,1)S(1)}, u32[]{:S(2)}, u32[]{:S(2)}) collective-permute-start(bf16[32,4096]{1,0:T(8,128)(2,1)S(1)} %collective-permute-done.26.refs_0_), channel_id=1, source_target_pairs={{0,1},{1,0},{2,3},{3,2},{4,5},{5,4},{6,7},{7,6},{8,9},{9,8},{10,11... | collective-permute-start | bytes 786440 | tf_op jit(solution)/shard_map/ppermute | solution.py:18
  71.3 15.1 %collective-permute-start.29 = (bf16[32,4096]{1,0:T(8,128)(2,1)S(1)}, bf16[32,4096]{1,0:T(8,128)(2,1)S(1)}, u32[]{:S(2)}, u32[]{:S(2)}) collective-permute-start(bf16[32,4096]{1,0:T(8,128)(2,1)S(1)} %collective-permute-done.28.refs_2_), channel_id=1, source_target_pairs={{0,1},{1,0},{2,3},{3,2},{4,5},{5,4},{6,7},{7,6},{8,9},{9,8},{10,11... | collective-permute-start | bytes 786440 | tf_op jit(solution)/shard_map/ppermute | solution.py:18
  71.4 15.0 %collective-permute-start.31 = (bf16[32,4096]{1,0:T(8,128)(2,1)S(1)}, bf16[32,4096]{1,0:T(8,128)(2,1)S(1)}, u32[]{:S(2)}, u32[]{:S(2)}) collective-permute-start(bf16[32,4096]{1,0:T(8,128)(2,1)S(1)} %collective-permute-done.30.refs_4_), channel_id=1, source_target_pairs={{0,1},{1,0},{2,3},{3,2},{4,5},{5,4},{6,7},{7,6},{8,9},{9,8},{10,11... | collective-permute-start | bytes 786440 | tf_op jit(solution)/shard_map/ppermute | solution.py:18
  73.7 19.1 %collective-permute-start.16 = (bf16[32,4096]{1,0:T(8,128)(2,1)S(1)}, bf16[32,4096]{1,0:T(8,128)(2,1)S(1)}, u32[]{:S(2)}, u32[]{:S(2)}) collective-permute-start(bf16[32,4096]{1,0:T(8,128)(2,1)S(1)} %collective-permute-done.15.refs_2_), channel_id=1, source_target_pairs={{0,1},{1,0},{2,3},{3,2},{4,5},{5,4},{6,7},{7,6},{8,9},{9,8},{10,11... | collective-permute-start | bytes 786440 | tf_op jit(solution)/shard_map/ppermute | solution.py:18
  79.2 16.1 %collective-permute-start.33 = (bf16[32,4096]{1,0:T(8,128)(2,1)S(1)}, bf16[32,4096]{1,0:T(8,128)(2,1)S(1)}, u32[]{:S(2)}, u32[]{:S(2)}) collective-permute-start(bf16[32,4096]{1,0:T(8,128)(2,1)S(1)} %collective-permute-done.32.refs_2_), channel_id=1, source_target_pairs={{0,1},{1,0},{2,3},{3,2},{4,5},{5,4},{6,7},{7,6},{8,9},{9,8},{10,11... | collective-permute-start | bytes 786440 | tf_op jit(solution)/shard_map/ppermute | solution.py:18

commit v2 on v0

v2 whole, which is shorter than its diff:
```python
import functools

import jax
import jax.numpy as jnp
from jax import lax
from jax.experimental import pallas as pl
from jax.experimental.pallas import tpu as pltpu
from jax.sharding import PartitionSpec as P

TILE = 128
SPLIT = 8
TICKS = 2
UNROLL = 16
CHUNKS = 2

CORE, X, Z = 1, 2, 4


def sent(array, target):
    peers = lax.axis_size("section")
    return lax.ppermute(array, "section", [(i, target(i, peers)) for i in range(peers)])


def across_core(array):
    return sent(array, lambda i, n: i ^ CORE)


def across_first(array):
    return sent(array, lambda i, n: i ^ (Z if i & CORE else X))


def across_second(array):
    return sent(array, lambda i, n: i ^ (X if i & CORE else Z))


def from_behind(array):
    return sent(array, lambda i, n: (i + SPLIT) % n)


def after(array, *others):
    return lax.optimization_barrier((array, *others))[0]


PLACE = ((0, 1, 2, 5, 3, 4, 6, 7), (0, 1, 3, 4, 2, 5, 6, 7))


def slab_place(source, position):
    difference = source ^ position
    odd = (position & CORE) == 1
    even_place = sum(jnp.where(difference == j, PLACE[0][j], 0) for j in range(SPLIT))
    odd_place = sum(jnp.where(difference == j, PLACE[1][j], 0) for j in range(SPLIT))
    return jnp.where(odd, odd_place, even_place)


def slot_lists(phases, place, chunk, tile, cols, live, spare):
    slots = cols.shape[0]
    index = jnp.arange(slots, dtype=jnp.int32)
    count = len(phases)
    phase = jnp.full((slots,), count, jnp.int32)
    block = jnp.zeros((slots,), jnp.int32)
    for k, blocks in enumerate(phases):
        for at, (p, c) in enumerate(blocks):
            hit = live & (place == p) & (chunk == c)
            phase = jnp.where(hit, k, phase)
            block = jnp.where(hit, at, block)
    member = phase[:, None] == jnp.arange(count, dtype=jnp.int32)[None, :]
    steps = (jnp.sum(member, axis=0, dtype=jnp.int32) + UNROLL - 1) // UNROLL
    lower = jnp.arange(count + 1)[:, None] > jnp.arange(count)[None, :]
    starts = jnp.sum(jnp.where(lower, steps[None, :], 0), axis=1, dtype=jnp.int32)
    before = (phase[None, :] == phase[:, None]) & (index[None, :] < index[:, None])
    rank = jnp.sum(before, axis=1, dtype=jnp.int32)
    base = jnp.sum(jnp.where(member, starts[None, :count] * UNROLL, 0), axis=1, dtype=jnp.int32)
    spot = jnp.where(live, base + rank, -1)
    hit = spot[None, :] == jnp.arange(slots + count * UNROLL, dtype=jnp.int32)[:, None]
    word = ((index * 32 + block) * 64 + tile) * 64 + cols
    packed = jnp.sum(jnp.where(hit, (word - spare)[None, :], 0), axis=1, dtype=jnp.int32) + spare
    return starts, packed


def phase_kernel(phase, pieces, first, last, starts_ref, list_ref, w_ref, *refs):
    refs = list(refs)
    acc_in = None if first else refs.pop(0)
    bias_ref = refs.pop(0) if last else None
    piece_refs = [refs.pop(0) for _ in range(pieces)]
    outs = [refs.pop(0) for _ in range(last)] if last else []
    acc = None if last else refs.pop(0)
    held = refs.pop(0)
    if last:
        acc = refs.pop(0)
    for at, piece in enumerate(piece_refs):
        held[at] = piece[...]
    acc[...] = jnp.zeros_like(acc) if first else acc_in[...]

    def step(it, carry):
        products = []
        places = []
        for u in range(UNROLL):
            word = list_ref[it * UNROLL + u]
            at = pl.ds(pl.multiple_of(((word >> 6) & 63) * TILE, TILE), TILE)
            x = held[(word >> 12) & 31, :, at]
            products.append(jnp.dot(x, w_ref[word >> 17], preferred_element_type=jnp.float32))
            places.append(word & 63)
        for place, product in zip(places, products):
            acc[place] = acc[place] + product
        return carry

    lax.fori_loop(starts_ref[phase], starts_ref[phase + 1], step, 0)
    c = 0
    for out in outs:
        for k in range(out.shape[1] // TILE):
            at = slice(c * TILE, (c + 1) * TILE)
            out[:, k * TILE:(k + 1) * TILE] = jnp.maximum(acc[c] + bias_ref[:, at], 0.0).astype(out.dtype)
            c += 1


def run_phase(phase, lists, weights, acc, pieces, wide, bias=None, chunks=0):
    first, last = acc is None, bias is not None
    tall, piece_wide = pieces[0].shape
    smem = pl.BlockSpec(memory_space=pltpu.SMEM)
    vmem = pl.BlockSpec(memory_space=pltpu.VMEM)
    operands = [*lists, weights] + ([] if first else [acc]) + ([bias] if last else []) + list(pieces)
    shape = (wide // TILE + 1, tall, TILE)
    scratch = [pltpu.VMEM((len(pieces), tall, piece_wide), jnp.bfloat16)]
    aliases = {}
    if last:
        out = [jax.ShapeDtypeStruct((tall, wide // chunks), jnp.bfloat16)] * chunks
        scratch.append(pltpu.VMEM(shape, jnp.float32))
    else:
        out = [jax.ShapeDtypeStruct(shape, jnp.float32)]
        if not first:
            aliases = {3: 0}
    results = pl.pallas_call(
        functools.partial(phase_kernel, phase, len(pieces), first, chunks if last else 0),
        out_shape=out,
        in_specs=[smem, smem] + [vmem] * (len(operands) - 2),
        out_specs=[vmem] * len(out),
        scratch_shapes=scratch,
        input_output_aliases=aliases,
        compiler_params=pltpu.CompilerParams(vmem_limit_bytes=12 << 20),
        cost_estimate=pl.CostEstimate(flops=2_000_000_000, bytes_accessed=6_000_000, transcendentals=0),
        name=f"phase_{phase}",
    )(*operands)
    return results if last else results[0]


FIRST_PHASES = (
    ((0, 0), (1, 0)),
    ((2, 0), (3, 0), (4, 0), (5, 0)),
    ((6, 0), (7, 0)),
)
LATER_PHASES = (
    tuple((p, 0) for p in range(8)),
    tuple((p, 1) for p in range(6)),
    ((6, 1), (7, 1)),
)


def first_layer(own, lists, weights, bias):
    wide = own.shape[1]
    a = across_first(own)
    core = across_core(own)
    b = across_second(own)
    acc = run_phase(0, lists, weights, None, [own, core], wide)
    a = after(a, acc)
    e = across_second(a)
    pieces = [a, b, across_core(a), across_core(b)]
    acc = run_phase(1, lists, weights, acc, pieces, wide)
    e = after(e, acc)
    return run_phase(2, lists, weights, acc, [e, across_core(e)], wide, bias, CHUNKS)


def later_layer(parts, lists, weights, bias, wide, chunks):
    parts = [from_behind(part) for part in parts]
    acc = None
    for at, own in enumerate(parts):
        a = across_first(own)
        b = across_second(own)
        core = across_core(own)
        e = across_second(a)
        pieces = [own, core, a, b, across_core(a), across_core(b)]
        if at == 0:
            acc = run_phase(0, lists, weights, None, [*pieces, e, across_core(e)], wide)
        else:
            e = after(e, acc)
            acc = run_phase(1, lists, weights, acc, pieces, wide)
            return run_phase(2, lists, weights, acc, [e, across_core(e)], wide, bias, chunks)


def on_device(held, tile_values, tile_rows, tile_cols, tile_count, bias):
    position = lax.axis_index("section") % SPLIT
    own = held[0]
    wide = own.shape[1]
    tiles = wide // TILE
    live = jnp.arange(tile_rows.shape[0], dtype=jnp.int32) < tile_count[0]
    place = slab_place(tile_rows // tiles, position)
    tile = tile_rows % tiles
    part = tiles // CHUNKS
    first_lists = slot_lists(FIRST_PHASES, place, jnp.zeros_like(tile), tile, tile_cols, live, tiles)
    later_lists = slot_lists(LATER_PHASES, place, tile // part, tile % part, tile_cols, live, tiles)
    bias_row = bias[None, :]
    slab = first_layer(own, first_lists, tile_values, bias_row)
    for tick in range(1, TICKS):
        last = tick + 1 == TICKS
        slab = later_layer(slab, later_lists, tile_values, bias_row, wide, 1 if last else CHUNKS)
    return slab[0][None]


def solution(mesh):
    return jax.shard_map(
        on_device,
        mesh=mesh,
        in_specs=(
            P("section", "groups", None),
            P("section", None, None),
            P("section"),
            P("section"),
            P("section"),
            P("section"),
        ),
        out_specs=P("section", "groups", None),
        check_vma=False,
    )
```

time: 443 us -> 78.5 us (0.18)
  waiting for transfers between devices: 319 us -> 36.5 us
  other arithmetic: 68.7 us -> 2.92 us
  matrix products: 22.8 us -> 0 us
  Pallas kernels: 0 us -> 16.5 us
  local copies, waits for them, and re-layouts: 18.6 us -> 4.74 us
  starting transfers between devices: 10.9 us -> 17.1 us
    ppermute x7 -> x23, waiting for transfers between devices: 319 us -> 36.5 us  [sent(): lax.ppermute(array, 'section', [(i, target(i, peers)) for i in range(peer...]
    scatter-add x2 -> x0, other arithmetic: 59.6 us -> none  [layer_slab(): summed = jax.ops.segment_sum(products, cols_list, num_segments=COLT)]
    dot_general x2 -> x0, matrix products: 22.8 us -> none  [layer_slab(): jnp.einsum('bck,ckj->cbj', picked, values_list, preferred_element_type=jn...]
    pallas_call x0 -> x6, Pallas kernels: none -> 16.5 us  [run_phase(): pl.pallas_call(functools.partial(phase_kernel, phase, len(pieces), first,...]
    gather x2 -> x0, local copies, waits for them, and re-layouts: 11.5 us -> none  [layer_slab(): picked = jnp.take(blocks, rows_list, axis=1)]
    select_n x9 -> x5, other arithmetic: 8.1 us -> 0.06 us  [the longest x2 0.03 us: slot_lists(): phase = jnp.where(hit, k, phase)]
    ppermute x7 -> x23, starting transfers between devices: 10.9 us -> 17.1 us  [sent(): lax.ppermute(array, 'section', [(i, target(i, peers)) for i in range(peer...]
    unnamed x9 -> x12, local copies, waits for them, and re-layouts: 0.11 us -> 4.74 us
  transfers between devices with their start and end apart: 7 -> 23, of which waited for: 7 -> 10; matrix products, arithmetic and copies ran while one was open for 0% -> 4% of each run, Pallas kernels for 0% -> 15%
where the time goes in v2:
time: 78.5 us; the launch traced here: 78.7 us
  waiting for transfers between devices  36.5 us (46%)
  starting transfers between devices  17.1 us (22%)
  Pallas kernels  16.5 us (21%)
  local copies, waits for them, and re-layouts  4.74 us (6%)
  other arithmetic  2.92 us (4%)
  between operations  0.88 us (1%)
    ppermute x23, waiting for transfers between devices, sent(): lax.ppermute(array, 'section', [(i, target(i, peers)) for i in range(peer...  36.5 us
    ppermute x23, starting transfers between devices, sent(): lax.ppermute(array, 'section', [(i, target(i, peers)) for i in range(peer...  17.1 us
    pallas_call x6, Pallas kernels, run_phase(): pl.pallas_call(functools.partial(phase_kernel, phase, len(pieces), first,...  16.5 us
    unnamed x12, local copies, waits for them, and re-layouts  4.74 us
  transfers between devices with their start and end apart: 23, of which 10 were waited for; matrix products, arithmetic and copies ran while one was open for 4% of the time, Pallas kernels for 15%

profile of v2, /device:TPU:0, one launch (start us, length us, event | category | flops | bytes accessed | tf_op | source)
XLA Modules:
  0.0 78.7 jit_solution(6641308967321223093)
XLA Ops:
  0.0 0.5 collective-permute-start
  0.5 2.5 %collective-permute-start.1 = (bf16[64,4096]{1,0:T(8,128)(2,1)}, bf16[64,4096]{1,0:T(8,128)(2,1)S(1)}, u32[]{:S(2)}, u32[]{:S(2)}) collective-permute-start(bf16[64,4096]{1,0:T(8,128)(2,1)} %bitcast.10), channel_id=1, source_target_pairs={{0,2},{1,5},{2,0},{3,7},{4,6},{5,1},{6,4},{7,3},{8,10},{9,13},{10,... | collective-permute-start | bytes 1572872 | tf_op jit(solution)/shard_map/ppermute | solution.py:21
  2.9 1.6 %collective-permute-start.2 = (bf16[64,4096]{1,0:T(8,128)(2,1)}, bf16[64,4096]{1,0:T(8,128)(2,1)S(1)}, u32[]{:S(2)}, u32[]{:S(2)}) collective-permute-start(bf16[64,4096]{1,0:T(8,128)(2,1)} %bitcast.11), channel_id=1, source_target_pairs={{0,4},{1,3},{2,6},{3,1},{4,0},{5,7},{6,2},{7,5},{8,12},{9,11},{10,... | collective-permute-start | bytes 1572872 | tf_op jit(solution)/shard_map/ppermute | solution.py:21
  5.2 0.7 add_add_fusion
  5.9 0.1 convert_reduce_fusion.2
  6.0 0.2 convert_reduce_fusion
  6.3 0.7 fusion.13
  7.0 0.1 convert_reduce_fusion.3
  7.1 0.2 convert_reduce_fusion.1
  7.4 0.1 select_reduce_fusion.5.starts_ref
  7.5 0.1 select_reduce_fusion.4.starts_ref
  7.6 0.1 select_reduce_fusion.2
  7.7 0.1 select_reduce_fusion.3
  7.8 0.2 select_reduce_fusion
  8.0 0.0 collective-permute-done.refs_1_
  8.0 0.0 copy-start
  8.0 3.7 %copy-done = bf16[288,128,128]{2,1,0:T(8,128)(2,1)S(1)} copy-done((bf16[288,128,128]{2,1,0:T(8,128)(2,1)S(1)}, bf16[288,128,128]{2,1,0:T(8,128)(2,1)}, u32[]{:S(2)}) %copy-start) | copy-done | bytes 9437208
  11.7 1.0 %copy-done.1 = bf16[1,64,4096]{2,1,0:T(8,128)(2,1)S(1)} copy-done((bf16[1,64,4096]{2,1,0:T(8,128)(2,1)S(1)}, bf16[1,64,4096]{2,1,0:T(8,128)(2,1)}, u32[]{:S(2)}) %copy-start.1) | copy-done | bytes 524312
  12.7 2.1 %phase_0.2.refs_0_ = f32[33,64,128]{2,1,0:T(8,128)S(1)} custom-call(s32[4]{0:T(128)S(1)} %select_reduce_fusion.4.starts_ref, s32[336]{0:T(512)S(1)} %broadcast_add_fusion.list_ref, bf16[288,128,128]{2,1,0:T(8,128)(2,1)S(1)} %copy-done, bf16[64,4096]{1,0:T(8,128)(2,1)S(1)} %bitcast.12, bf16[64,4096]{1,0:T(8,128)(2,1)S(1)} %collective-permute-done.refs_1_), custom_call_target="tpu_custom_call" | custom-call | flops 2000000000 | bytes 6000000 | tf_op jit(solution)/shard_map/phase_0/pallas_call | solution.py:132
  14.9 0.0 copy-start.2
  14.9 0.0 collective-permute-done.1.refs_1_
  14.9 0.1 collective-permute-start.3
  15.0 0.9 %collective-permute-done.2.refs_2_ = bf16[64,4096]{1,0:T(8,128)(2,1)S(1)} collective-permute-done((bf16[64,4096]{1,0:T(8,128)(2,1)}, bf16[64,4096]{1,0:T(8,128)(2,1)S(1)}, u32[]{:S(2)}, u32[]{:S(2)}) %collective-permute-start.2) | collective-permute-done | bytes 524320 | tf_op jit(solution)/shard_map/ppermute | solution.py:21
  15.8 0.1 collective-permute-start.4
  15.9 2.1 %collective-permute-start.5 = (bf16[64,4096]{1,0:T(8,128)(2,1)S(1)}, bf16[64,4096]{1,0:T(8,128)(2,1)S(1)}, u32[]{:S(2)}, u32[]{:S(2)}) collective-permute-start(bf16[64,4096]{1,0:T(8,128)(2,1)S(1)} %collective-permute-done.1.refs_1_), channel_id=1, source_target_pairs={{0,4},{1,3},{2,6},{3,1},{4,0},{5,7},{6,2},{7,5},{8,12},{9,11},{10,... | collective-permute-start | bytes 1572872 | tf_op jit(solution)/shard_map/ppermute | solution.py:21
  18.1 0.0 collective-permute-done.3.refs_3_
  18.1 0.0 collective-permute-done.4.refs_4_
  18.1 0.0 slice-start.1
  18.1 3.4 %phase_1.2.refs_0_ = f32[33,64,128]{2,1,0:T(8,128)S(1)} custom-call(s32[4]{0:T(128)S(1)} %select_reduce_fusion.4.starts_ref, s32[336]{0:T(512)S(1)} %broadcast_add_fusion.list_ref, bf16[288,128,128]{2,1,0:T(8,128)(2,1)S(1)} %copy-done, f32[33,64,128]{2,1,0:T(8,128)S(1)} %phase_0.2.refs_0_, ...), custom_call_target="tpu_custom_call", output_to_operand_aliasing={{}: (3, {})} | custom-call | flops 2000000000 | bytes 6000000 | tf_op jit(solution)/shard_map/phase_1/pallas_call | solution.py:132
  21.5 3.7 %collective-permute-done.5.refs_2_ = bf16[64,4096]{1,0:T(8,128)(2,1)S(1)} collective-permute-done((bf16[64,4096]{1,0:T(8,128)(2,1)S(1)}, bf16[64,4096]{1,0:T(8,128)(2,1)S(1)}, u32[]{:S(2)}, u32[]{:S(2)}) %collective-permute-start.5) | collective-permute-done | bytes 524320 | tf_op jit(solution)/shard_map/ppermute | solution.py:21
  25.3 1.9 %collective-permute-done.6.refs_3_ = bf16[64,4096]{1,0:T(8,128)(2,1)S(1)} collective-permute-done((bf16[64,4096]{1,0:T(8,128)(2,1)S(1)}, bf16[64,4096]{1,0:T(8,128)(2,1)S(1)}, u32[]{:S(2)}, u32[]{:S(2)}) %collective-permute-start.6) | collective-permute-done | bytes 524320 | tf_op jit(solution)/shard_map/ppermute | solution.py:21
  27.2 2.2 %phase_2.2 = (bf16[64,2048]{1,0:T(8,128)(2,1)S(1)}, bf16[64,2048]{1,0:T(8,128)(2,1)S(1)}) custom-call(s32[4]{0:T(128)S(1)} %select_reduce_fusion.4.starts_ref, s32[336]{0:T(512)S(1)} %broadcast_add_fusion.list_ref, bf16[288,128,128]{2,1,0:T(8,128)(2,1)S(1)} %copy-done, f32[33,64,128]{2,1,0:T(8,128)S(1)} %phase_1.2.refs_0_, f32[1,4096]{1,0:T(1,128)S(1)} %bitcast.13, ...), custom_call_target="tpu_custom_call" | custom-call | flops 2000000000 | bytes 6000000 | tf_op jit(solution)/shard_map/phase_2/pallas_call | solution.py:132
  29.4 1.7 %collective-permute-start.7 = (bf16[64,2048]{1,0:T(8,128)(2,1)S(1)}, bf16[64,2048]{1,0:T(8,128)(2,1)S(1)}, u32[]{:S(2)}, u32[]{:S(2)}) collective-permute-start(bf16[64,2048]{1,0:T(8,128)(2,1)S(1)} %get-tuple-element.12), channel_id=1, source_target_pairs={{0,8},{1,9},{2,10},{3,11},{4,12},{5,13},{6,14},{7,15},{8,0},{9,1},... | collective-permute-start | bytes 786440 | tf_op jit(solution)/shard_map/ppermute | solution.py:21
  31.1 1.2 %collective-permute-start.15 = (bf16[64,2048]{1,0:T(8,128)(2,1)S(1)}, bf16[64,2048]{1,0:T(8,128)(2,1)S(1)}, u32[]{:S(2)}, u32[]{:S(2)}) collective-permute-start(bf16[64,2048]{1,0:T(8,128)(2,1)S(1)} %get-tuple-element.13), channel_id=1, source_target_pairs={{0,8},{1,9},{2,10},{3,11},{4,12},{5,13},{6,14},{7,15},{8,0},{9,1},... | collective-permute-start | bytes 786440 | tf_op jit(solution)/shard_map/ppermute | solution.py:21
  32.4 18.5 %collective-permute-done.7.refs_0_ = bf16[64,2048]{1,0:T(8,128)(2,1)S(1)} collective-permute-done((bf16[64,2048]{1,0:T(8,128)(2,1)S(1)}, bf16[64,2048]{1,0:T(8,128)(2,1)S(1)}, u32[]{:S(2)}, u32[]{:S(2)}) %collective-permute-start.7) | collective-permute-done | bytes 262176 | tf_op jit(solution)/shard_map/ppermute | solution.py:21
  50.8 1.0 %collective-permute-start.9 = (bf16[64,2048]{1,0:T(8,128)(2,1)S(1)}, bf16[64,2048]{1,0:T(8,128)(2,1)S(1)}, u32[]{:S(2)}, u32[]{:S(2)}) collective-permute-start(bf16[64,2048]{1,0:T(8,128)(2,1)S(1)} %collective-permute-done.7.refs_0_), channel_id=1, source_target_pairs={{0,2},{1,5},{2,0},{3,7},{4,6},{5,1},{6,4},{7,3},{8,10},{9,13},{10,... | collective-permute-start | bytes 786440 | tf_op jit(solution)/shard_map/ppermute | solution.py:21
  51.8 3.1 %collective-permute-done.15.refs_1_ = bf16[64,2048]{1,0:T(8,128)(2,1)S(1)} collective-permute-done((bf16[64,2048]{1,0:T(8,128)(2,1)S(1)}, bf16[64,2048]{1,0:T(8,128)(2,1)S(1)}, u32[]{:S(2)}, u32[]{:S(2)}) %collective-permute-start.15) | collective-permute-done | bytes 262176 | tf_op jit(solution)/shard_map/ppermute | solution.py:21
  55.0 1.8 %collective-permute-start.17 = (bf16[64,2048]{1,0:T(8,128)(2,1)S(1)}, bf16[64,2048]{1,0:T(8,128)(2,1)S(1)}, u32[]{:S(2)}, u32[]{:S(2)}) collective-permute-start(bf16[64,2048]{1,0:T(8,128)(2,1)S(1)} %collective-permute-done.15.refs_1_), channel_id=1, source_target_pairs={{0,2},{1,5},{2,0},{3,7},{4,6},{5,1},{6,4},{7,3},{8,10},{9,13},{10,... | collective-permute-start | bytes 786440 | tf_op jit(solution)/shard_map/ppermute | solution.py:21
  56.8 0.0 collective-permute-start.10
  56.8 0.4 collective-permute-done.9.refs_2_
  57.2 1.6 %collective-permute-start.13 = (bf16[64,2048]{1,0:T(8,128)(2,1)S(1)}, bf16[64,2048]{1,0:T(8,128)(2,1)S(1)}, u32[]{:S(2)}, u32[]{:S(2)}) collective-permute-start(bf16[64,2048]{1,0:T(8,128)(2,1)S(1)} %collective-permute-done.9.refs_2_), channel_id=1, source_target_pairs={{0,4},{1,3},{2,6},{3,1},{4,0},{5,7},{6,2},{7,5},{8,12},{9,11},{10,... | collective-permute-start | bytes 786440 | tf_op jit(solution)/shard_map/ppermute | solution.py:21
  58.8 0.2 collective-permute-start.8
  59.1 0.2 collective-permute-start.18
  59.2 4.9 %collective-permute-done.17.refs_3_ = bf16[64,2048]{1,0:T(8,128)(2,1)S(1)} collective-permute-done((bf16[64,2048]{1,0:T(8,128)(2,1)S(1)}, bf16[64,2048]{1,0:T(8,128)(2,1)S(1)}, u32[]{:S(2)}, u32[]{:S(2)}) %collective-permute-start.17) | collective-permute-done | bytes 262176 | tf_op jit(solution)/shard_map/ppermute | solution.py:21
  64.1 0.5 collective-permute-start.12
  64.6 1.5 %collective-permute-done.13.refs_6_ = bf16[64,2048]{1,0:T(8,128)(2,1)S(1)} collective-permute-done((bf16[64,2048]{1,0:T(8,128)(2,1)S(1)}, bf16[64,2048]{1,0:T(8,128)(2,1)S(1)}, u32[]{:S(2)}, u32[]{:S(2)}) %collective-permute-start.13) | collective-permute-done | bytes 262176 | tf_op jit(solution)/shard_map/ppermute | solution.py:21
  66.1 0.4 collective-permute-start.14
  66.6 0.2 select_reduce_fusion.1
  66.7 0.0 collective-permute-done.8.refs_1_
  66.7 0.7 collective-permute-start.21
  67.5 1.4 %collective-permute-done.18.refs_4_ = bf16[64,2048]{1,0:T(8,128)(2,1)S(1)} collective-permute-done((bf16[64,2048]{1,0:T(8,128)(2,1)S(1)}, bf16[64,2048]{1,0:T(8,128)(2,1)S(1)}, u32[]{:S(2)}, u32[]{:S(2)}) %collective-permute-start.18) | collective-permute-done | bytes 262176 | tf_op jit(solution)/shard_map/ppermute | solution.py:21
  68.9 0.2 collective-permute-start.16
  69.1 0.0 collective-permute-done.11.refs_4_
  69.1 0.4 collective-permute-start.19
  69.4 0.2 collective-permute-start.20
  69.6 0.0 collective-permute-done.14.refs_7_
  69.6 3.3 %phase_0.3.refs_0_ = f32[33,64,128]{2,1,0:T(8,128)S(1)} custom-call(s32[4]{0:T(128)S(1)} %select_reduce_fusion.5.starts_ref, s32[336]{0:T(512)S(1)} %broadcast_add_fusion.1.list_ref, bf16[288,128,128]{2,1,0:T(8,128)(2,1)S(1)} %bitcast.8, bf16[64,2048]{1,0:T(8,128)(2,1)S(1)} %collective-permute-done.7.refs_0_, ...), custom_call_target="tpu_custom_call" | custom-call | flops 2000000000 | bytes 6000000 | tf_op jit(solution)/shard_map/phase_0/pallas_call | solution.py:132
  72.9 0.2 collective-permute-done.21.refs_2_
  73.2 0.0 collective-permute-start.22
  73.2 0.0 collective-permute-done.16.refs_2_
  73.2 0.0 collective-permute-done.19.refs_5_
  73.2 3.1 %phase_1.3.refs_0_ = f32[33,64,128]{2,1,0:T(8,128)S(1)} custom-call(s32[4]{0:T(128)S(1)} %select_reduce_fusion.5.starts_ref, s32[336]{0:T(512)S(1)} %broadcast_add_fusion.1.list_ref, bf16[288,128,128]{2,1,0:T(8,128)(2,1)S(1)} %bitcast.8, f32[33,64,128]{2,1,0:T(8,128)S(1)} %phase_0.3.refs_0_, ...), custom_call_target="tpu_custom_call", output_to_operand_aliasing={{}: (3, {})} | custom-call | flops 2000000000 | bytes 6000000 | tf_op jit(solution)/shard_map/phase_1/pallas_call | solution.py:132
  76.3 0.0 collective-permute-done.22.refs_3_
  76.3 2.4 %phase_2.3 = bf16[64,4096]{1,0:T(8,128)(2,1)} custom-call(s32[4]{0:T(128)S(1)} %select_reduce_fusion.5.starts_ref, s32[336]{0:T(512)S(1)} %broadcast_add_fusion.1.list_ref, bf16[288,128,128]{2,1,0:T(8,128)(2,1)S(1)} %bitcast.8, f32[33,64,128]{2,1,0:T(8,128)S(1)} %phase_1.3.refs_0_, f32[1,4096]{1,0:T(1,128)S(1)} %bitcast.14, ...), custom_call_target="tpu_custom_call" | custom-call | flops 2000000000 | bytes 6000000 | tf_op jit(solution)/shard_map/phase_2/pallas_call | solution.py:132
  (22 shorter events, 0.1 us)
Async XLA Ops:
  0.0 8.0 %collective-permute-start = (bf16[64,4096]{1,0:T(8,128)(2,1)}, bf16[64,4096]{1,0:T(8,128)(2,1)S(1)}, u32[]{:S(2)}, u32[]{:S(2)}) collective-permute-start(bf16[64,4096]{1,0:T(8,128)(2,1)} %bitcast.9), channel_id=1, source_target_pairs={{0,1},{1,0},{2,3},{3,2},{4,5},{5,4},{6,7},{7,6},{8,9},{9,8},{10,11... | collective-permute-start | bytes 1572872 | tf_op jit(solution)/shard_map/ppermute | solution.py:21
  0.5 14.4 %collective-permute-start.1 = (bf16[64,4096]{1,0:T(8,128)(2,1)}, bf16[64,4096]{1,0:T(8,128)(2,1)S(1)}, u32[]{:S(2)}, u32[]{:S(2)}) collective-permute-start(bf16[64,4096]{1,0:T(8,128)(2,1)} %bitcast.10), channel_id=1, source_target_pairs={{0,2},{1,5},{2,0},{3,7},{4,6},{5,1},{6,4},{7,3},{8,10},{9,13},{10,... | collective-permute-start | bytes 1572872 | tf_op jit(solution)/shard_map/ppermute | solution.py:21
  2.9 12.9 %collective-permute-start.2 = (bf16[64,4096]{1,0:T(8,128)(2,1)}, bf16[64,4096]{1,0:T(8,128)(2,1)S(1)}, u32[]{:S(2)}, u32[]{:S(2)}) collective-permute-start(bf16[64,4096]{1,0:T(8,128)(2,1)} %bitcast.11), channel_id=1, source_target_pairs={{0,4},{1,3},{2,6},{3,1},{4,0},{5,7},{6,2},{7,5},{8,12},{9,11},{10,... | collective-permute-start | bytes 1572872 | tf_op jit(solution)/shard_map/ppermute | solution.py:21
  8.0 3.7 %copy-start = (bf16[288,128,128]{2,1,0:T(8,128)(2,1)S(1)}, bf16[288,128,128]{2,1,0:T(8,128)(2,1)}, u32[]{:S(2)}) copy-start(bf16[288,128,128]{2,1,0:T(8,128)(2,1)} %w_ref.11) | copy-start | bytes 28311556
  11.7 1.0 %copy-start.1 = (bf16[1,64,4096]{2,1,0:T(8,128)(2,1)S(1)}, bf16[1,64,4096]{2,1,0:T(8,128)(2,1)}, u32[]{:S(2)}) copy-start(bf16[1,64,4096]{2,1,0:T(8,128)(2,1)} %param.6) | copy-start | bytes 1572868
  14.9 12.3 %copy-start.2 = (f32[4096]{0:T(1024)S(1)}, f32[4096]{0:T(1024)}, u32[]{:S(2)}) copy-start(f32[4096]{0:T(1024)} %param.11) | copy-start | bytes 49156
  14.9 3.2 %collective-permute-start.3 = (bf16[64,4096]{1,0:T(8,128)(2,1)S(1)}, bf16[64,4096]{1,0:T(8,128)(2,1)S(1)}, u32[]{:S(2)}, u32[]{:S(2)}) collective-permute-start(bf16[64,4096]{1,0:T(8,128)(2,1)S(1)} %collective-permute-done.1.refs_1_), channel_id=1, source_target_pairs={{0,1},{1,0},{2,3},{3,2},{4,5},{5,4},{6,7},{7,6},{8,9},{9,8},{10,11... | collective-permute-start | bytes 1572872 | tf_op jit(solution)/shard_map/ppermute | solution.py:21
  15.8 2.3 %collective-permute-start.4 = (bf16[64,4096]{1,0:T(8,128)(2,1)S(1)}, bf16[64,4096]{1,0:T(8,128)(2,1)S(1)}, u32[]{:S(2)}, u32[]{:S(2)}) collective-permute-start(bf16[64,4096]{1,0:T(8,128)(2,1)S(1)} %collective-permute-done.2.refs_2_), channel_id=1, source_target_pairs={{0,1},{1,0},{2,3},{3,2},{4,5},{5,4},{6,7},{7,6},{8,9},{9,8},{10,11... | collective-permute-start | bytes 1572872 | tf_op jit(solution)/shard_map/ppermute | solution.py:21
  15.9 9.3 %collective-permute-start.5 = (bf16[64,4096]{1,0:T(8,128)(2,1)S(1)}, bf16[64,4096]{1,0:T(8,128)(2,1)S(1)}, u32[]{:S(2)}, u32[]{:S(2)}) collective-permute-start(bf16[64,4096]{1,0:T(8,128)(2,1)S(1)} %collective-permute-done.1.refs_1_), channel_id=1, source_target_pairs={{0,4},{1,3},{2,6},{3,1},{4,0},{5,7},{6,2},{7,5},{8,12},{9,11},{10,... | collective-permute-start | bytes 1572872 | tf_op jit(solution)/shard_map/ppermute | solution.py:21
  18.1 51.5 %slice-start = ((s8[9437184]{0:T(1024)(128)(4,1)}), s8[4194304]{0:T(1024)(128)(4,1)S(1)}, s32[]{:S(2)}) async-start(s8[9437184]{0:T(1024)(128)(4,1)} %bitcast.7), calls=%async_computation | async-start | bytes 8388608
  18.1 51.5 %slice-start.1 = ((s8[9437184]{0:T(1024)(128)(4,1)}), s8[4194304]{0:T(1024)(128)(4,1)S(1)}, s32[]{:S(2)}) async-start(s8[9437184]{0:T(1024)(128)(4,1)} %bitcast.7), calls=%async_computation.1 | async-start | bytes 8388608
  25.3 1.9 %collective-permute-start.6 = (bf16[64,4096]{1,0:T(8,128)(2,1)S(1)}, bf16[64,4096]{1,0:T(8,128)(2,1)S(1)}, u32[]{:S(2)}, u32[]{:S(2)}) collective-permute-start(bf16[64,4096]{1,0:T(8,128)(2,1)S(1)} %collective-permute-done.5.refs_2_), channel_id=1, source_target_pairs={{0,1},{1,0},{2,3},{3,2},{4,5},{5,4},{6,7},{7,6},{8,9},{9,8},{10,11... | collective-permute-start | bytes 1572872 | tf_op jit(solution)/shard_map/ppermute | solution.py:21
  27.2 42.4 %slice-start.2 = ((s8[9437184]{0:T(1024)(128)(4,1)}), s8[1048576]{0:T(1024)(128)(4,1)S(1)}, s32[]{:S(2)}) async-start(s8[9437184]{0:T(1024)(128)(4,1)} %bitcast.7), calls=%async_computation.2 | async-start | bytes 2097152
  29.4 21.4 %collective-permute-start.7 = (bf16[64,2048]{1,0:T(8,128)(2,1)S(1)}, bf16[64,2048]{1,0:T(8,128)(2,1)S(1)}, u32[]{:S(2)}, u32[]{:S(2)}) collective-permute-start(bf16[64,2048]{1,0:T(8,128)(2,1)S(1)} %get-tuple-element.12), channel_id=1, source_target_pairs={{0,8},{1,9},{2,10},{3,11},{4,12},{5,13},{6,14},{7,15},{8,0},{9,1},... | collective-permute-start | bytes 786440 | tf_op jit(solution)/shard_map/ppermute | solution.py:21
  31.1 23.8 %collective-permute-start.15 = (bf16[64,2048]{1,0:T(8,128)(2,1)S(1)}, bf16[64,2048]{1,0:T(8,128)(2,1)S(1)}, u32[]{:S(2)}, u32[]{:S(2)}) collective-permute-start(bf16[64,2048]{1,0:T(8,128)(2,1)S(1)} %get-tuple-element.13), channel_id=1, source_target_pairs={{0,8},{1,9},{2,10},{3,11},{4,12},{5,13},{6,14},{7,15},{8,0},{9,1},... | collective-permute-start | bytes 786440 | tf_op jit(solution)/shard_map/ppermute | solution.py:21
  50.8 6.4 %collective-permute-start.9 = (bf16[64,2048]{1,0:T(8,128)(2,1)S(1)}, bf16[64,2048]{1,0:T(8,128)(2,1)S(1)}, u32[]{:S(2)}, u32[]{:S(2)}) collective-permute-start(bf16[64,2048]{1,0:T(8,128)(2,1)S(1)} %collective-permute-done.7.refs_0_), channel_id=1, source_target_pairs={{0,2},{1,5},{2,0},{3,7},{4,6},{5,1},{6,4},{7,3},{8,10},{9,13},{10,... | collective-permute-start | bytes 786440 | tf_op jit(solution)/shard_map/ppermute | solution.py:21
  55.0 9.1 %collective-permute-start.17 = (bf16[64,2048]{1,0:T(8,128)(2,1)S(1)}, bf16[64,2048]{1,0:T(8,128)(2,1)S(1)}, u32[]{:S(2)}, u32[]{:S(2)}) collective-permute-start(bf16[64,2048]{1,0:T(8,128)(2,1)S(1)} %collective-permute-done.15.refs_1_), channel_id=1, source_target_pairs={{0,2},{1,5},{2,0},{3,7},{4,6},{5,1},{6,4},{7,3},{8,10},{9,13},{10,... | collective-permute-start | bytes 786440 | tf_op jit(solution)/shard_map/ppermute | solution.py:21
  56.8 7.3 %collective-permute-start.10 = (bf16[64,2048]{1,0:T(8,128)(2,1)S(1)}, bf16[64,2048]{1,0:T(8,128)(2,1)S(1)}, u32[]{:S(2)}, u32[]{:S(2)}) collective-permute-start(bf16[64,2048]{1,0:T(8,128)(2,1)S(1)} %collective-permute-done.7.refs_0_), channel_id=1, source_target_pairs={{0,4},{1,3},{2,6},{3,1},{4,0},{5,7},{6,2},{7,5},{8,12},{9,11},{10,... | collective-permute-start | bytes 786440 | tf_op jit(solution)/shard_map/ppermute | solution.py:21
  57.2 8.9 %collective-permute-start.13 = (bf16[64,2048]{1,0:T(8,128)(2,1)S(1)}, bf16[64,2048]{1,0:T(8,128)(2,1)S(1)}, u32[]{:S(2)}, u32[]{:S(2)}) collective-permute-start(bf16[64,2048]{1,0:T(8,128)(2,1)S(1)} %collective-permute-done.9.refs_2_), channel_id=1, source_target_pairs={{0,4},{1,3},{2,6},{3,1},{4,0},{5,7},{6,2},{7,5},{8,12},{9,11},{10,... | collective-permute-start | bytes 786440 | tf_op jit(solution)/shard_map/ppermute | solution.py:21
  58.8 7.9 %collective-permute-start.8 = (bf16[64,2048]{1,0:T(8,128)(2,1)S(1)}, bf16[64,2048]{1,0:T(8,128)(2,1)S(1)}, u32[]{:S(2)}, u32[]{:S(2)}) collective-permute-start(bf16[64,2048]{1,0:T(8,128)(2,1)S(1)} %collective-permute-done.7.refs_0_), channel_id=1, source_target_pairs={{0,1},{1,0},{2,3},{3,2},{4,5},{5,4},{6,7},{7,6},{8,9},{9,8},{10,11... | collective-permute-start | bytes 786440 | tf_op jit(solution)/shard_map/ppermute | solution.py:21
  59.1 9.9 %collective-permute-start.18 = (bf16[64,2048]{1,0:T(8,128)(2,1)S(1)}, bf16[64,2048]{1,0:T(8,128)(2,1)S(1)}, u32[]{:S(2)}, u32[]{:S(2)}) collective-permute-start(bf16[64,2048]{1,0:T(8,128)(2,1)S(1)} %collective-permute-done.15.refs_1_), channel_id=1, source_target_pairs={{0,4},{1,3},{2,6},{3,1},{4,0},{5,7},{6,2},{7,5},{8,12},{9,11},{10,... | collective-permute-start | bytes 786440 | tf_op jit(solution)/shard_map/ppermute | solution.py:21
  64.1 5.0 %collective-permute-start.11 = (bf16[64,2048]{1,0:T(8,128)(2,1)S(1)}, bf16[64,2048]{1,0:T(8,128)(2,1)S(1)}, u32[]{:S(2)}, u32[]{:S(2)}) collective-permute-start(bf16[64,2048]{1,0:T(8,128)(2,1)S(1)} %collective-permute-done.9.refs_2_), channel_id=1, source_target_pairs={{0,1},{1,0},{2,3},{3,2},{4,5},{5,4},{6,7},{7,6},{8,9},{9,8},{10,11... | collective-permute-start | bytes 786440 | tf_op jit(solution)/shard_map/ppermute | solution.py:21
  64.1 5.3 %collective-permute-start.12 = (bf16[64,2048]{1,0:T(8,128)(2,1)S(1)}, bf16[64,2048]{1,0:T(8,128)(2,1)S(1)}, u32[]{:S(2)}, u32[]{:S(2)}) collective-permute-start(bf16[64,2048]{1,0:T(8,128)(2,1)S(1)} %collective-permute-done.10.refs_3_), channel_id=1, source_target_pairs={{0,1},{1,0},{2,3},{3,2},{4,5},{5,4},{6,7},{7,6},{8,9},{9,8},{10,11... | collective-permute-start | bytes 786440 | tf_op jit(solution)/shard_map/ppermute | solution.py:21
  66.1 3.5 %collective-permute-start.14 = (bf16[64,2048]{1,0:T(8,128)(2,1)S(1)}, bf16[64,2048]{1,0:T(8,128)(2,1)S(1)}, u32[]{:S(2)}, u32[]{:S(2)}) collective-permute-start(bf16[64,2048]{1,0:T(8,128)(2,1)S(1)} %collective-permute-done.13.refs_6_), channel_id=1, source_target_pairs={{0,1},{1,0},{2,3},{3,2},{4,5},{5,4},{6,7},{7,6},{8,9},{9,8},{10,11... | collective-permute-start | bytes 786440 | tf_op jit(solution)/shard_map/ppermute | solution.py:21
  66.7 6.4 %collective-permute-start.21 = (bf16[64,2048]{1,0:T(8,128)(2,1)S(1)}, bf16[64,2048]{1,0:T(8,128)(2,1)S(1)}, u32[]{:S(2)}, u32[]{:S(2)}) collective-permute-start(bf16[64,2048]{1,0:T(8,128)(2,1)S(1)} %collective-permute-done.17.refs_3_), channel_id=1, source_target_pairs={{0,4},{1,3},{2,6},{3,1},{4,0},{5,7},{6,2},{7,5},{8,12},{9,11},{10,... | collective-permute-start | bytes 786440 | tf_op jit(solution)/shard_map/ppermute | solution.py:21
  68.9 4.3 %collective-permute-start.16 = (bf16[64,2048]{1,0:T(8,128)(2,1)S(1)}, bf16[64,2048]{1,0:T(8,128)(2,1)S(1)}, u32[]{:S(2)}, u32[]{:S(2)}) collective-permute-start(bf16[64,2048]{1,0:T(8,128)(2,1)S(1)} %collective-permute-done.15.refs_1_), channel_id=1, source_target_pairs={{0,1},{1,0},{2,3},{3,2},{4,5},{5,4},{6,7},{7,6},{8,9},{9,8},{10,11... | collective-permute-start | bytes 786440 | tf_op jit(solution)/shard_map/ppermute | solution.py:21
  69.1 4.1 %collective-permute-start.19 = (bf16[64,2048]{1,0:T(8,128)(2,1)S(1)}, bf16[64,2048]{1,0:T(8,128)(2,1)S(1)}, u32[]{:S(2)}, u32[]{:S(2)}) collective-permute-start(bf16[64,2048]{1,0:T(8,128)(2,1)S(1)} %collective-permute-done.17.refs_3_), channel_id=1, source_target_pairs={{0,1},{1,0},{2,3},{3,2},{4,5},{5,4},{6,7},{7,6},{8,9},{9,8},{10,11... | collective-permute-start | bytes 786440 | tf_op jit(solution)/shard_map/ppermute | solution.py:21
  69.4 3.7 %collective-permute-start.20 = (bf16[64,2048]{1,0:T(8,128)(2,1)S(1)}, bf16[64,2048]{1,0:T(8,128)(2,1)S(1)}, u32[]{:S(2)}, u32[]{:S(2)}) collective-permute-start(bf16[64,2048]{1,0:T(8,128)(2,1)S(1)} %collective-permute-done.18.refs_4_), channel_id=1, source_target_pairs={{0,1},{1,0},{2,3},{3,2},{4,5},{5,4},{6,7},{7,6},{8,9},{9,8},{10,11... | collective-permute-start | bytes 786440 | tf_op jit(solution)/shard_map/ppermute | solution.py:21
  73.2 3.1 %collective-permute-start.22 = (bf16[64,2048]{1,0:T(8,128)(2,1)S(1)}, bf16[64,2048]{1,0:T(8,128)(2,1)S(1)}, u32[]{:S(2)}, u32[]{:S(2)}) collective-permute-start(bf16[64,2048]{1,0:T(8,128)(2,1)S(1)} %collective-permute-done.21.refs_2_), channel_id=1, source_target_pairs={{0,1},{1,0},{2,3},{3,2},{4,5},{5,4},{6,7},{7,6},{8,9},{9,8},{10,11... | collective-permute-start | bytes 786440 | tf_op jit(solution)/shard_map/ppermute | solution.py:21

commit v3 on v2

v3 whole, which is shorter than its diff:
```python
import functools

import jax
import jax.numpy as jnp
from jax import lax
from jax.experimental import pallas as pl
from jax.experimental.pallas import tpu as pltpu
from jax.sharding import PartitionSpec as P

TILE = 128
SPLIT = 8
TICKS = 2
UNROLL = 16
CHUNKS = 2

CORE, X, Z = 1, 2, 4


def sent(array, name, target):
    peers = lax.axis_size("section")
    with jax.named_scope(name):
        return lax.ppermute(array, "section", [(i, target(i, peers)) for i in range(peers)])


def across_core(array, name):
    return sent(array, name, lambda i, n: i ^ CORE)


def across_first(array, name):
    return sent(array, name, lambda i, n: i ^ (Z if i & CORE else X))


def across_second(array, name):
    return sent(array, name, lambda i, n: i ^ (X if i & CORE else Z))


def from_behind(array, name):
    return sent(array, name, lambda i, n: (i + SPLIT) % n)


def after(array, *others):
    return lax.optimization_barrier((array, *others))[0]


PLACE = ((0, 1, 2, 5, 3, 4, 6, 7), (0, 1, 3, 4, 2, 5, 6, 7))


def slab_place(source, position):
    difference = source ^ position
    odd = (position & CORE) == 1
    even_place = sum(jnp.where(difference == j, PLACE[0][j], 0) for j in range(SPLIT))
    odd_place = sum(jnp.where(difference == j, PLACE[1][j], 0) for j in range(SPLIT))
    return jnp.where(odd, odd_place, even_place)


def slot_lists(phases, place, chunk, tile, cols, live, spare):
    slots = cols.shape[0]
    index = jnp.arange(slots, dtype=jnp.int32)
    count = len(phases)
    phase = jnp.full((slots,), count, jnp.int32)
    block = jnp.zeros((slots,), jnp.int32)
    for k, blocks in enumerate(phases):
        for p, c, at in blocks:
            hit = live & (place == p) & (chunk == c)
            phase = jnp.where(hit, k, phase)
            block = jnp.where(hit, at, block)
    member = phase[:, None] == jnp.arange(count, dtype=jnp.int32)[None, :]
    steps = (jnp.sum(member, axis=0, dtype=jnp.int32) + UNROLL - 1) // UNROLL
    lower = jnp.arange(count + 1)[:, None] > jnp.arange(count)[None, :]
    starts = jnp.sum(jnp.where(lower, steps[None, :], 0), axis=1, dtype=jnp.int32)
    before = (phase[None, :] == phase[:, None]) & (index[None, :] < index[:, None])
    rank = jnp.sum(before, axis=1, dtype=jnp.int32)
    base = jnp.sum(jnp.where(member, starts[None, :count] * UNROLL, 0), axis=1, dtype=jnp.int32)
    spot = jnp.where(live, base + rank, -1)
    hit = spot[None, :] == jnp.arange(slots + count * UNROLL, dtype=jnp.int32)[:, None]
    word = ((index * 32 + block) * 64 + tile) * 64 + cols
    packed = jnp.sum(jnp.where(hit, (word - spare)[None, :], 0), axis=1, dtype=jnp.int32) + spare
    return starts, packed


def phase_kernel(phase, pieces, first, columns, starts_ref, list_ref, w_ref, *refs):
    refs = list(refs)
    if not first:
        refs.pop(0)
    bias_ref = refs.pop(0) if columns else None
    piece_refs = [refs.pop(0) for _ in range(pieces)]
    acc = refs.pop(0)
    out = refs.pop(0) if columns else None
    held = refs.pop(0)
    rows = held.shape[1]
    at = 0
    for piece in piece_refs:
        for row in range(0, piece.shape[0], rows):
            held[at] = piece[row:row + rows]
            at += 1
    if first:
        acc[...] = jnp.zeros_like(acc)

    def step(it, carry):
        products = []
        places = []
        for u in range(UNROLL):
            word = list_ref[it * UNROLL + u]
            at = pl.ds(pl.multiple_of(((word >> 6) & 63) * TILE, TILE), TILE)
            x = held[(word >> 12) & 31, :, at]
            products.append(jnp.dot(x, w_ref[word >> 17], preferred_element_type=jnp.float32))
            places.append(word & 63)
        for place, product in zip(places, products):
            acc[place] = acc[place] + product
        return carry

    lax.fori_loop(starts_ref[phase], starts_ref[phase + 1], step, 0)
    for k, c in enumerate(columns):
        at = slice(c * TILE, (c + 1) * TILE)
        out[:, k * TILE:(k + 1) * TILE] = jnp.maximum(acc[c] + bias_ref[:, at], 0.0).astype(out.dtype)


def run_phase(phase, lists, weights, acc, pieces, wide, bias=None, columns=()):
    first, last = acc is None, bias is not None
    tall, piece_wide = pieces[0].shape
    slabs = sum(piece.shape[0] for piece in pieces) // tall
    smem = pl.BlockSpec(memory_space=pltpu.SMEM)
    vmem = pl.BlockSpec(memory_space=pltpu.VMEM)
    operands = [*lists, weights] + ([] if first else [acc]) + ([bias] if last else []) + list(pieces)
    shape = (wide // TILE + 1, tall, TILE)
    scratch = [pltpu.VMEM((slabs, tall, piece_wide), jnp.bfloat16)]
    out = [jax.ShapeDtypeStruct(shape, jnp.float32)]
    if last:
        out.append(jax.ShapeDtypeStruct((tall, len(columns) * TILE), jnp.bfloat16))
    aliases = {} if first else {3: 0}
    results = pl.pallas_call(
        functools.partial(phase_kernel, phase, len(pieces), first, tuple(columns)),
        out_shape=out,
        in_specs=[smem, smem] + [vmem] * (len(operands) - 2),
        out_specs=[vmem] * len(out),
        scratch_shapes=scratch,
        input_output_aliases=aliases,
        compiler_params=pltpu.CompilerParams(vmem_limit_bytes=12 << 20),
        cost_estimate=pl.CostEstimate(flops=2_000_000_000, bytes_accessed=6_000_000, transcendentals=0),
        name=f"phase_{phase}",
    )(*operands)
    return results if last else results[0]


def blocks(*slabs, columns=None):
    if columns is None:
        return tuple((place, chunk, at) for at, (place, chunk) in enumerate(slabs))
    return tuple((place, chunk, at) for at, place in enumerate(slabs) for chunk in columns)


ALL = tuple(range(CHUNKS))
FIRST_PHASES = (
    blocks(0, 1, columns=ALL),
    blocks(2, 3, 4, 5, columns=ALL),
) + tuple(blocks(6, 7, columns=(k,)) for k in ALL)
LATER_PHASES = (
    blocks(*((p, 0) for p in range(6))),
    blocks((6, 0), (7, 0), *((p, 1) for p in range(6))),
    blocks((6, 1), (7, 1)),
)


def first_layer(own, lists, weights, bias):
    wide = own.shape[1]
    a = across_first(own, "a")
    core = across_core(own, "core")
    b = across_second(own, "b")
    acc = run_phase(0, lists, weights, None, [own, core], wide)
    a = after(a, acc)
    e = across_second(a, "e")
    pieces = [a, b, across_core(a, "ac"), across_core(b, "bc")]
    acc = run_phase(1, lists, weights, acc, pieces, wide)
    e = after(e, acc)
    pieces = [e, across_core(e, "ec")]
    outs = []
    part = wide // TILE // CHUNKS
    for k in ALL:
        acc, out = run_phase(2 + k, lists, weights, acc, pieces, wide, bias, range(k * part, (k + 1) * part))
        outs.append(out)
    return outs


def later_layer(parts, lists, weights, bias, wide):
    done = parts[-1]
    parts = [from_behind(part, f"cross{k}") for k, part in enumerate(parts)]
    parts[0] = after(parts[0], done)
    acc, late = None, []
    for k, own in enumerate(parts):
        a = across_first(own, f"A{k}")
        b = across_second(own, f"B{k}")
        core = across_core(own, f"CORE{k}")
        e = across_second(a, f"E{k}")
        pieces = [*late, own, core, a, b, across_core(a, f"AC{k}"), across_core(b, f"BC{k}")]
        if k:
            e = after(e, acc)
        late = [e, across_core(e, f"EC{k}")]
        acc = run_phase(k, lists, weights, acc, pieces, wide)
    return run_phase(len(parts), lists, weights, acc, late, wide, bias, range(wide // TILE))[1]


def on_device(held, tile_values, tile_rows, tile_cols, tile_count, bias):
    position = lax.axis_index("section") % SPLIT
    own = held[0]
    wide = own.shape[1]
    tiles = wide // TILE
    live = jnp.arange(tile_rows.shape[0], dtype=jnp.int32) < tile_count[0]
    place = slab_place(tile_rows // tiles, position)
    tile = tile_rows % tiles
    part = tiles // CHUNKS
    first_lists = slot_lists(FIRST_PHASES, place, tile_cols // part, tile, tile_cols, live, tiles)
    later_lists = slot_lists(LATER_PHASES, place, tile // part, tile % part, tile_cols, live, tiles)
    bias_row = bias[None, :]
    parts = first_layer(own, first_lists, tile_values, bias_row)
    for tick in range(1, TICKS):
        slab = later_layer(parts, later_lists, tile_values, bias_row, wide)
        parts = jnp.split(slab, CHUNKS, axis=1)
    return slab[None]


def solution(mesh):
    return jax.shard_map(
        on_device,
        mesh=mesh,
        in_specs=(
            P("section", "groups", None),
            P("section", None, None),
            P("section"),
            P("section"),
            P("section"),
            P("section"),
        ),
        out_specs=P("section", "groups", None),
        check_vma=False,
    )
```

time: 78.5 us -> 76.1 us (0.969)
  Pallas kernels: 16.5 us -> 11.7 us
  starting transfers between devices: 17.1 us -> 19.4 us
    pallas_call x6 -> x7, Pallas kernels: 16.5 us -> 11.7 us  [run_phase(): pl.pallas_call(functools.partial(phase_kernel, phase, len(pieces), first,...]
    ppermute x23, starting transfers between devices: 17.1 us -> 19.4 us  [sent(): lax.ppermute(array, 'section', [(i, target(i, peers)) for i in range(peer...]
  transfers between devices with their start and end apart: 23 -> 23, of which waited for: 10 -> 12; matrix products, arithmetic and copies ran while one was open for 4% -> 4% of each run, Pallas kernels for 15% -> 12%
where the time goes in v3:
time: 76.1 us; the launch traced here: 75.9 us
  waiting for transfers between devices  36.3 us (48%)
  starting transfers between devices  19.4 us (25%)
  Pallas kernels  11.7 us (15%)
  local copies, waits for them, and re-layouts  4.73 us (6%)
  other arithmetic  2.92 us (4%)
  between operations  0.85 us (1%)
    ppermute x23, waiting for transfers between devices, sent(): lax.ppermute(array, 'section', [(i, target(i, peers)) for i in range(peer...  36.3 us
    ppermute x23, starting transfers between devices, sent(): lax.ppermute(array, 'section', [(i, target(i, peers)) for i in range(peer...  19.4 us
    pallas_call x7, Pallas kernels, run_phase(): pl.pallas_call(functools.partial(phase_kernel, phase, len(pieces), first,...  11.7 us
    unnamed x12, local copies, waits for them, and re-layouts  4.73 us
  transfers between devices with their start and end apart: 23, of which 12 were waited for; matrix products, arithmetic and copies ran while one was open for 4% of the time, Pallas kernels for 12%

profile of v3, /device:TPU:0, one launch (start us, length us, event | category | flops | bytes accessed | tf_op | source)
XLA Modules:
  0.0 75.9 jit_solution(15588206018571622340)
XLA Ops:
  0.0 0.5 collective-permute-start
  0.5 2.5 %collective-permute-start.1 = (bf16[64,4096]{1,0:T(8,128)(2,1)}, bf16[64,4096]{1,0:T(8,128)(2,1)S(1)}, u32[]{:S(2)}, u32[]{:S(2)}) collective-permute-start(bf16[64,4096]{1,0:T(8,128)(2,1)} %bitcast.10), channel_id=1, source_target_pairs={{0,2},{1,5},{2,0},{3,7},{4,6},{5,1},{6,4},{7,3},{8,10},{9,13},{10,... | collective-permute-start | bytes 1572872 | tf_op jit(solution)/shard_map/a/ppermute | solution.py:22
  2.9 1.6 %collective-permute-start.2 = (bf16[64,4096]{1,0:T(8,128)(2,1)}, bf16[64,4096]{1,0:T(8,128)(2,1)S(1)}, u32[]{:S(2)}, u32[]{:S(2)}) collective-permute-start(bf16[64,4096]{1,0:T(8,128)(2,1)} %bitcast.11), channel_id=1, source_target_pairs={{0,4},{1,3},{2,6},{3,1},{4,0},{5,7},{6,2},{7,5},{8,12},{9,11},{10,... | collective-permute-start | bytes 1572872 | tf_op jit(solution)/shard_map/b/ppermute | solution.py:22
  5.2 0.7 add_add_fusion
  5.9 0.7 fusion.13
  6.7 0.1 convert_reduce_fusion.3
  6.8 0.2 convert_reduce_fusion.1
  7.0 0.1 convert_reduce_fusion.2
  7.2 0.2 convert_reduce_fusion
  7.4 0.1 select_reduce_fusion.5.starts_ref
  7.5 0.1 select_reduce_fusion.3
  7.6 0.1 select_reduce_fusion.4.starts_ref
  7.7 0.1 select_reduce_fusion.2
  7.8 0.2 select_reduce_fusion
  8.0 0.0 collective-permute-done.refs_1_
  8.0 0.0 copy-start
  8.0 3.7 %copy-done = bf16[288,128,128]{2,1,0:T(8,128)(2,1)S(1)} copy-done((bf16[288,128,128]{2,1,0:T(8,128)(2,1)S(1)}, bf16[288,128,128]{2,1,0:T(8,128)(2,1)}, u32[]{:S(2)}) %copy-start) | copy-done | bytes 9437208
  11.7 1.0 %copy-done.1 = bf16[1,64,4096]{2,1,0:T(8,128)(2,1)S(1)} copy-done((bf16[1,64,4096]{2,1,0:T(8,128)(2,1)S(1)}, bf16[1,64,4096]{2,1,0:T(8,128)(2,1)}, u32[]{:S(2)}) %copy-start.1) | copy-done | bytes 524312
  12.7 1.5 %phase_0.2.refs_0_ = f32[33,64,128]{2,1,0:T(8,128)S(1)} custom-call(s32[5]{0:T(128)S(1)} %select_reduce_fusion.4.starts_ref, s32[352]{0:T(512)S(1)} %broadcast_add_fusion.list_ref, bf16[288,128,128]{2,1,0:T(8,128)(2,1)S(1)} %copy-done, bf16[64,4096]{1,0:T(8,128)(2,1)S(1)} %bitcast.12, bf16[64,4096]{1,0:T(8,128)(2,1)S(1)} %collective-permute-done.refs_1_), custom_call_target="tpu_custom_call" | custom-call | flops 2000000000 | bytes 6000000 | tf_op jit(solution)/shard_map/phase_0/pallas_call | solution.py:131
  14.3 0.0 copy-start.2
  14.3 0.5 collective-permute-done.1.refs_1_
  14.8 0.0 collective-permute-start.3
  14.8 1.1 %collective-permute-done.2.refs_2_ = bf16[64,4096]{1,0:T(8,128)(2,1)S(1)} collective-permute-done((bf16[64,4096]{1,0:T(8,128)(2,1)}, bf16[64,4096]{1,0:T(8,128)(2,1)S(1)}, u32[]{:S(2)}, u32[]{:S(2)}) %collective-permute-start.2) | collective-permute-done | bytes 524320 | tf_op jit(solution)/shard_map/b/ppermute | solution.py:22
  15.8 0.1 collective-permute-start.4
  15.9 2.1 %collective-permute-start.5 = (bf16[64,4096]{1,0:T(8,128)(2,1)S(1)}, bf16[64,4096]{1,0:T(8,128)(2,1)S(1)}, u32[]{:S(2)}, u32[]{:S(2)}) collective-permute-start(bf16[64,4096]{1,0:T(8,128)(2,1)S(1)} %collective-permute-done.1.refs_1_), channel_id=1, source_target_pairs={{0,4},{1,3},{2,6},{3,1},{4,0},{5,7},{6,2},{7,5},{8,12},{9,11},{10,... | collective-permute-start | bytes 1572872 | tf_op jit(solution)/shard_map/e/ppermute | solution.py:22
  18.1 0.0 collective-permute-done.3.refs_3_
  18.1 0.0 collective-permute-done.4.refs_4_
  18.1 2.1 %phase_1.2.refs_0_ = f32[33,64,128]{2,1,0:T(8,128)S(1)} custom-call(s32[5]{0:T(128)S(1)} %select_reduce_fusion.4.starts_ref, s32[352]{0:T(512)S(1)} %broadcast_add_fusion.list_ref, bf16[288,128,128]{2,1,0:T(8,128)(2,1)S(1)} %copy-done, f32[33,64,128]{2,1,0:T(8,128)S(1)} %phase_0.2.refs_0_, ...), custom_call_target="tpu_custom_call", output_to_operand_aliasing={{}: (3, {})} | custom-call | flops 2000000000 | bytes 6000000 | tf_op jit(solution)/shard_map/phase_1/pallas_call | solution.py:131
  20.2 5.0 %collective-permute-done.5.refs_2_ = bf16[64,4096]{1,0:T(8,128)(2,1)S(1)} collective-permute-done((bf16[64,4096]{1,0:T(8,128)(2,1)S(1)}, bf16[64,4096]{1,0:T(8,128)(2,1)S(1)}, u32[]{:S(2)}, u32[]{:S(2)}) %collective-permute-start.5) | collective-permute-done | bytes 524320 | tf_op jit(solution)/shard_map/e/ppermute | solution.py:22
  25.3 1.9 %collective-permute-done.6.refs_3_ = bf16[64,4096]{1,0:T(8,128)(2,1)S(1)} collective-permute-done((bf16[64,4096]{1,0:T(8,128)(2,1)S(1)}, bf16[64,4096]{1,0:T(8,128)(2,1)S(1)}, u32[]{:S(2)}, u32[]{:S(2)}) %collective-permute-start.6) | collective-permute-done | bytes 524320 | tf_op jit(solution)/shard_map/ec/ppermute | solution.py:22
  27.2 1.0 %phase_2.2 = (f32[33,64,128]{2,1,0:T(8,128)S(1)}, bf16[64,2048]{1,0:T(8,128)(2,1)S(1)}) custom-call(s32[5]{0:T(128)S(1)} %select_reduce_fusion.4.starts_ref, s32[352]{0:T(512)S(1)} %broadcast_add_fusion.list_ref, bf16[288,128,128]{2,1,0:T(8,128)(2,1)S(1)} %copy-done, f32[33,64,128]{2,1,0:T(8,128)S(1)} %phase_1.2.refs_0_, ...), custom_call_target="tpu_custom_call", output_to_operand_aliasing={{0}: (3, {})} | custom-call | flops 2000000000 | bytes 6000000 | tf_op jit(solution)/shard_map/phase_2/pallas_call | solution.py:131
  28.1 3.2 %collective-permute-start.7 = (bf16[64,2048]{1,0:T(8,128)(2,1)S(1)}, bf16[64,2048]{1,0:T(8,128)(2,1)S(1)}, u32[]{:S(2)}, u32[]{:S(2)}) collective-permute-start(bf16[64,2048]{1,0:T(8,128)(2,1)S(1)} %get-tuple-element.15), channel_id=1, source_target_pairs={{0,8},{1,9},{2,10},{3,11},{4,12},{5,13},{6,14},{7,15},{8,0},{9,1},... | collective-permute-start | bytes 786440 | tf_op jit(solution)/shard_map/cross0/ppermute | solution.py:22
  31.3 1.0 %phase_3.1 = (f32[33,64,128]{2,1,0:T(8,128)S(1)}, bf16[64,2048]{1,0:T(8,128)(2,1)S(1)}) custom-call(s32[5]{0:T(128)S(1)} %select_reduce_fusion.4.starts_ref, s32[352]{0:T(512)S(1)} %broadcast_add_fusion.list_ref, bf16[288,128,128]{2,1,0:T(8,128)(2,1)S(1)} %copy-done, f32[33,64,128]{2,1,0:T(8,128)S(1)} %get-tuple-element.16.refs_0_, ...), custom_call_target="tpu_custom_call", output_to_operand_aliasing={{0}: (3, {})} | custom-call | flops 2000000000 | bytes 6000000 | tf_op jit(solution)/shard_map/phase_3/pallas_call | solution.py:131
  32.3 0.4 collective-permute-start.15
  32.6 17.0 %collective-permute-done.7.refs_0_ = bf16[64,2048]{1,0:T(8,128)(2,1)S(1)} collective-permute-done((bf16[64,2048]{1,0:T(8,128)(2,1)S(1)}, bf16[64,2048]{1,0:T(8,128)(2,1)S(1)}, u32[]{:S(2)}, u32[]{:S(2)}) %collective-permute-start.7) | collective-permute-done | bytes 262176 | tf_op jit(solution)/shard_map/cross0/ppermute | solution.py:22
  49.6 1.9 %collective-permute-start.9 = (bf16[64,2048]{1,0:T(8,128)(2,1)S(1)}, bf16[64,2048]{1,0:T(8,128)(2,1)S(1)}, u32[]{:S(2)}, u32[]{:S(2)}) collective-permute-start(bf16[64,2048]{1,0:T(8,128)(2,1)S(1)} %collective-permute-done.7.refs_0_), channel_id=1, source_target_pairs={{0,2},{1,5},{2,0},{3,7},{4,6},{5,1},{6,4},{7,3},{8,10},{9,13},{10,... | collective-permute-start | bytes 786440 | tf_op jit(solution)/shard_map/A0/ppermute | solution.py:22
  51.5 0.0 collective-permute-start.8
  51.5 3.3 %collective-permute-done.15.refs_3_ = bf16[64,2048]{1,0:T(8,128)(2,1)S(1)} collective-permute-done((bf16[64,2048]{1,0:T(8,128)(2,1)S(1)}, bf16[64,2048]{1,0:T(8,128)(2,1)S(1)}, u32[]{:S(2)}, u32[]{:S(2)}) %collective-permute-start.15) | collective-permute-done | bytes 262176 | tf_op jit(solution)/shard_map/cross1/ppermute | solution.py:22
  54.9 1.3 %collective-permute-start.17 = (bf16[64,2048]{1,0:T(8,128)(2,1)S(1)}, bf16[64,2048]{1,0:T(8,128)(2,1)S(1)}, u32[]{:S(2)}, u32[]{:S(2)}) collective-permute-start(bf16[64,2048]{1,0:T(8,128)(2,1)S(1)} %collective-permute-done.15.refs_3_), channel_id=1, source_target_pairs={{0,2},{1,5},{2,0},{3,7},{4,6},{5,1},{6,4},{7,3},{8,10},{9,13},{10,... | collective-permute-start | bytes 786440 | tf_op jit(solution)/shard_map/A1/ppermute | solution.py:22
  56.2 0.6 collective-permute-start.18
  56.7 1.1 %collective-permute-done.9.refs_2_ = bf16[64,2048]{1,0:T(8,128)(2,1)S(1)} collective-permute-done((bf16[64,2048]{1,0:T(8,128)(2,1)S(1)}, bf16[64,2048]{1,0:T(8,128)(2,1)S(1)}, u32[]{:S(2)}, u32[]{:S(2)}) %collective-permute-start.9) | collective-permute-done | bytes 262176 | tf_op jit(solution)/shard_map/A0/ppermute | solution.py:22
  57.8 2.3 %collective-permute-start.11 = (bf16[64,2048]{1,0:T(8,128)(2,1)S(1)}, bf16[64,2048]{1,0:T(8,128)(2,1)S(1)}, u32[]{:S(2)}, u32[]{:S(2)}) collective-permute-start(bf16[64,2048]{1,0:T(8,128)(2,1)S(1)} %collective-permute-done.9.refs_2_), channel_id=1, source_target_pairs={{0,1},{1,0},{2,3},{3,2},{4,5},{5,4},{6,7},{7,6},{8,9},{9,8},{10,11... | collective-permute-start | bytes 786440 | tf_op jit(solution)/shard_map/AC0/ppermute | solution.py:22
  60.2 0.5 collective-permute-done.10.refs_3_
  60.7 0.0 collective-permute-done.8.refs_1_
  60.7 0.7 collective-permute-start.12
  61.4 0.2 select_reduce_fusion.1
  61.5 2.4 %collective-permute-done.17.refs_5_ = bf16[64,2048]{1,0:T(8,128)(2,1)S(1)} collective-permute-done((bf16[64,2048]{1,0:T(8,128)(2,1)S(1)}, bf16[64,2048]{1,0:T(8,128)(2,1)S(1)}, u32[]{:S(2)}, u32[]{:S(2)}) %collective-permute-start.17) | collective-permute-done | bytes 262176 | tf_op jit(solution)/shard_map/A1/ppermute | solution.py:22
  64.0 0.7 collective-permute-start.21
  64.7 1.3 %collective-permute-done.18.refs_6_ = bf16[64,2048]{1,0:T(8,128)(2,1)S(1)} collective-permute-done((bf16[64,2048]{1,0:T(8,128)(2,1)S(1)}, bf16[64,2048]{1,0:T(8,128)(2,1)S(1)}, u32[]{:S(2)}, u32[]{:S(2)}) %collective-permute-start.18) | collective-permute-done | bytes 262176 | tf_op jit(solution)/shard_map/B1/ppermute | solution.py:22
  66.0 1.0 %collective-permute-start.16 = (bf16[64,2048]{1,0:T(8,128)(2,1)S(1)}, bf16[64,2048]{1,0:T(8,128)(2,1)S(1)}, u32[]{:S(2)}, u32[]{:S(2)}) collective-permute-start(bf16[64,2048]{1,0:T(8,128)(2,1)S(1)} %collective-permute-done.15.refs_3_), channel_id=1, source_target_pairs={{0,1},{1,0},{2,3},{3,2},{4,5},{5,4},{6,7},{7,6},{8,9},{9,8},{10,11... | collective-permute-start | bytes 786440 | tf_op jit(solution)/shard_map/CORE1/ppermute | solution.py:22
  67.0 0.0 collective-permute-done.11.refs_4_
  67.0 0.1 collective-permute-start.19
  67.1 0.4 collective-permute-start.20
  67.5 1.3 %collective-permute-done.13.refs_1_ = bf16[64,2048]{1,0:T(8,128)(2,1)S(1)} collective-permute-done((bf16[64,2048]{1,0:T(8,128)(2,1)S(1)}, bf16[64,2048]{1,0:T(8,128)(2,1)S(1)}, u32[]{:S(2)}, u32[]{:S(2)}) %collective-permute-start.13) | collective-permute-done | bytes 262176 | tf_op jit(solution)/shard_map/E0/ppermute | solution.py:22
  68.8 0.0 collective-permute-start.14
  68.8 1.9 %phase_0.3.refs_0_ = f32[33,64,128]{2,1,0:T(8,128)S(1)} custom-call(s32[4]{0:T(128)S(1)} %select_reduce_fusion.5.starts_ref, s32[336]{0:T(512)S(1)} %broadcast_add_fusion.1.list_ref, bf16[288,128,128]{2,1,0:T(8,128)(2,1)S(1)} %bitcast.8, bf16[64,2048]{1,0:T(8,128)(2,1)S(1)} %collective-permute-done.7.refs_0_, ...), custom_call_target="tpu_custom_call" | custom-call | flops 2000000000 | bytes 6000000 | tf_op jit(solution)/shard_map/phase_0/pallas_call | solution.py:131
  70.7 0.9 %collective-permute-done.21.refs_2_ = bf16[64,2048]{1,0:T(8,128)(2,1)S(1)} collective-permute-done((bf16[64,2048]{1,0:T(8,128)(2,1)S(1)}, bf16[64,2048]{1,0:T(8,128)(2,1)S(1)}, u32[]{:S(2)}, u32[]{:S(2)}) %collective-permute-start.21) | collective-permute-done | bytes 262176 | tf_op jit(solution)/shard_map/E1/ppermute | solution.py:22
  71.6 0.0 collective-permute-done.16.refs_4_
  71.6 0.0 collective-permute-done.19.refs_7_
  71.6 0.0 collective-permute-done.20.refs_8_
  71.6 0.0 collective-permute-done.14.refs_2_
  71.6 2.4 %phase_1.3.refs_0_ = f32[33,64,128]{2,1,0:T(8,128)S(1)} custom-call(s32[4]{0:T(128)S(1)} %select_reduce_fusion.5.starts_ref, s32[336]{0:T(512)S(1)} %broadcast_add_fusion.1.list_ref, bf16[288,128,128]{2,1,0:T(8,128)(2,1)S(1)} %bitcast.8, f32[33,64,128]{2,1,0:T(8,128)S(1)} %phase_0.3.refs_0_, ...), custom_call_target="tpu_custom_call", output_to_operand_aliasing={{}: (3, {})} | custom-call | flops 2000000000 | bytes 6000000 | tf_op jit(solution)/shard_map/phase_1/pallas_call | solution.py:131
  74.1 0.0 collective-permute-done.22.refs_3_
  74.1 1.8 %phase_2.3 = (f32[33,64,128]{2,1,0:T(8,128)S(1)}, bf16[64,4096]{1,0:T(8,128)(2,1)}) custom-call(s32[4]{0:T(128)S(1)} %select_reduce_fusion.5.starts_ref, s32[336]{0:T(512)S(1)} %broadcast_add_fusion.1.list_ref, bf16[288,128,128]{2,1,0:T(8,128)(2,1)S(1)} %bitcast.8, f32[33,64,128]{2,1,0:T(8,128)S(1)} %phase_1.3.refs_0_, ...), custom_call_target="tpu_custom_call", output_to_operand_aliasing={{0}: (3, {})} | custom-call | flops 2000000000 | bytes 6000000 | tf_op jit(solution)/shard_map/phase_2/pallas_call | solution.py:131
  (23 shorter events, 0.1 us)
Async XLA Ops:
  0.0 8.0 %collective-permute-start = (bf16[64,4096]{1,0:T(8,128)(2,1)}, bf16[64,4096]{1,0:T(8,128)(2,1)S(1)}, u32[]{:S(2)}, u32[]{:S(2)}) collective-permute-start(bf16[64,4096]{1,0:T(8,128)(2,1)} %bitcast.9), channel_id=1, source_target_pairs={{0,1},{1,0},{2,3},{3,2},{4,5},{5,4},{6,7},{7,6},{8,9},{9,8},{10,11... | collective-permute-start | bytes 1572872 | tf_op jit(solution)/shard_map/core/ppermute | solution.py:22
  0.5 14.3 %collective-permute-start.1 = (bf16[64,4096]{1,0:T(8,128)(2,1)}, bf16[64,4096]{1,0:T(8,128)(2,1)S(1)}, u32[]{:S(2)}, u32[]{:S(2)}) collective-permute-start(bf16[64,4096]{1,0:T(8,128)(2,1)} %bitcast.10), channel_id=1, source_target_pairs={{0,2},{1,5},{2,0},{3,7},{4,6},{5,1},{6,4},{7,3},{8,10},{9,13},{10,... | collective-permute-start | bytes 1572872 | tf_op jit(solution)/shard_map/a/ppermute | solution.py:22
  2.9 12.9 %collective-permute-start.2 = (bf16[64,4096]{1,0:T(8,128)(2,1)}, bf16[64,4096]{1,0:T(8,128)(2,1)S(1)}, u32[]{:S(2)}, u32[]{:S(2)}) collective-permute-start(bf16[64,4096]{1,0:T(8,128)(2,1)} %bitcast.11), channel_id=1, source_target_pairs={{0,4},{1,3},{2,6},{3,1},{4,0},{5,7},{6,2},{7,5},{8,12},{9,11},{10,... | collective-permute-start | bytes 1572872 | tf_op jit(solution)/shard_map/b/ppermute | solution.py:22
  8.0 3.7 %copy-start = (bf16[288,128,128]{2,1,0:T(8,128)(2,1)S(1)}, bf16[288,128,128]{2,1,0:T(8,128)(2,1)}, u32[]{:S(2)}) copy-start(bf16[288,128,128]{2,1,0:T(8,128)(2,1)} %w_ref.13) | copy-start | bytes 28311556
  11.7 1.0 %copy-start.1 = (bf16[1,64,4096]{2,1,0:T(8,128)(2,1)S(1)}, bf16[1,64,4096]{2,1,0:T(8,128)(2,1)}, u32[]{:S(2)}) copy-start(bf16[1,64,4096]{2,1,0:T(8,128)(2,1)} %param.6) | copy-start | bytes 1572868
  14.3 12.9 %copy-start.2 = (f32[4096]{0:T(1024)S(1)}, f32[4096]{0:T(1024)}, u32[]{:S(2)}) copy-start(f32[4096]{0:T(1024)} %param.11) | copy-start | bytes 49156
  14.8 3.3 %collective-permute-start.3 = (bf16[64,4096]{1,0:T(8,128)(2,1)S(1)}, bf16[64,4096]{1,0:T(8,128)(2,1)S(1)}, u32[]{:S(2)}, u32[]{:S(2)}) collective-permute-start(bf16[64,4096]{1,0:T(8,128)(2,1)S(1)} %collective-permute-done.1.refs_1_), channel_id=1, source_target_pairs={{0,1},{1,0},{2,3},{3,2},{4,5},{5,4},{6,7},{7,6},{8,9},{9,8},{10,11... | collective-permute-start | bytes 1572872 | tf_op jit(solution)/shard_map/ac/ppermute | solution.py:22
  15.8 2.3 %collective-permute-start.4 = (bf16[64,4096]{1,0:T(8,128)(2,1)S(1)}, bf16[64,4096]{1,0:T(8,128)(2,1)S(1)}, u32[]{:S(2)}, u32[]{:S(2)}) collective-permute-start(bf16[64,4096]{1,0:T(8,128)(2,1)S(1)} %collective-permute-done.2.refs_2_), channel_id=1, source_target_pairs={{0,1},{1,0},{2,3},{3,2},{4,5},{5,4},{6,7},{7,6},{8,9},{9,8},{10,11... | collective-permute-start | bytes 1572872 | tf_op jit(solution)/shard_map/bc/ppermute | solution.py:22
  15.9 9.3 %collective-permute-start.5 = (bf16[64,4096]{1,0:T(8,128)(2,1)S(1)}, bf16[64,4096]{1,0:T(8,128)(2,1)S(1)}, u32[]{:S(2)}, u32[]{:S(2)}) collective-permute-start(bf16[64,4096]{1,0:T(8,128)(2,1)S(1)} %collective-permute-done.1.refs_1_), channel_id=1, source_target_pairs={{0,4},{1,3},{2,6},{3,1},{4,0},{5,7},{6,2},{7,5},{8,12},{9,11},{10,... | collective-permute-start | bytes 1572872 | tf_op jit(solution)/shard_map/e/ppermute | solution.py:22
  25.3 1.9 %collective-permute-start.6 = (bf16[64,4096]{1,0:T(8,128)(2,1)S(1)}, bf16[64,4096]{1,0:T(8,128)(2,1)S(1)}, u32[]{:S(2)}, u32[]{:S(2)}) collective-permute-start(bf16[64,4096]{1,0:T(8,128)(2,1)S(1)} %collective-permute-done.5.refs_2_), channel_id=1, source_target_pairs={{0,1},{1,0},{2,3},{3,2},{4,5},{5,4},{6,7},{7,6},{8,9},{9,8},{10,11... | collective-permute-start | bytes 1572872 | tf_op jit(solution)/shard_map/ec/ppermute | solution.py:22
  27.2 41.6 %slice-start = ((s8[9437184]{0:T(1024)(128)(4,1)}), s8[4194304]{0:T(1024)(128)(4,1)S(1)}, s32[]{:S(2)}) async-start(s8[9437184]{0:T(1024)(128)(4,1)} %bitcast.7), calls=%async_computation | async-start | bytes 8388608
  27.2 41.6 %slice-start.1 = ((s8[9437184]{0:T(1024)(128)(4,1)}), s8[4194304]{0:T(1024)(128)(4,1)S(1)}, s32[]{:S(2)}) async-start(s8[9437184]{0:T(1024)(128)(4,1)} %bitcast.7), calls=%async_computation.1 | async-start | bytes 8388608
  28.1 21.5 %collective-permute-start.7 = (bf16[64,2048]{1,0:T(8,128)(2,1)S(1)}, bf16[64,2048]{1,0:T(8,128)(2,1)S(1)}, u32[]{:S(2)}, u32[]{:S(2)}) collective-permute-start(bf16[64,2048]{1,0:T(8,128)(2,1)S(1)} %get-tuple-element.15), channel_id=1, source_target_pairs={{0,8},{1,9},{2,10},{3,11},{4,12},{5,13},{6,14},{7,15},{8,0},{9,1},... | collective-permute-start | bytes 786440 | tf_op jit(solution)/shard_map/cross0/ppermute | solution.py:22
  31.3 37.5 %slice-start.2 = ((s8[9437184]{0:T(1024)(128)(4,1)}), s8[1048576]{0:T(1024)(128)(4,1)S(1)}, s32[]{:S(2)}) async-start(s8[9437184]{0:T(1024)(128)(4,1)} %bitcast.7), calls=%async_computation.2 | async-start | bytes 2097152
  32.3 22.6 %collective-permute-start.15 = (bf16[64,2048]{1,0:T(8,128)(2,1)S(1)}, bf16[64,2048]{1,0:T(8,128)(2,1)S(1)}, u32[]{:S(2)}, u32[]{:S(2)}) collective-permute-start(bf16[64,2048]{1,0:T(8,128)(2,1)S(1)} %get-tuple-element.17), channel_id=1, source_target_pairs={{0,8},{1,9},{2,10},{3,11},{4,12},{5,13},{6,14},{7,15},{8,0},{9,1},... | collective-permute-start | bytes 786440 | tf_op jit(solution)/shard_map/cross1/ppermute | solution.py:22
  49.6 8.2 %collective-permute-start.9 = (bf16[64,2048]{1,0:T(8,128)(2,1)S(1)}, bf16[64,2048]{1,0:T(8,128)(2,1)S(1)}, u32[]{:S(2)}, u32[]{:S(2)}) collective-permute-start(bf16[64,2048]{1,0:T(8,128)(2,1)S(1)} %collective-permute-done.7.refs_0_), channel_id=1, source_target_pairs={{0,2},{1,5},{2,0},{3,7},{4,6},{5,1},{6,4},{7,3},{8,10},{9,13},{10,... | collective-permute-start | bytes 786440 | tf_op jit(solution)/shard_map/A0/ppermute | solution.py:22
  51.5 9.2 %collective-permute-start.10 = (bf16[64,2048]{1,0:T(8,128)(2,1)S(1)}, bf16[64,2048]{1,0:T(8,128)(2,1)S(1)}, u32[]{:S(2)}, u32[]{:S(2)}) collective-permute-start(bf16[64,2048]{1,0:T(8,128)(2,1)S(1)} %collective-permute-done.7.refs_0_), channel_id=1, source_target_pairs={{0,4},{1,3},{2,6},{3,1},{4,0},{5,7},{6,2},{7,5},{8,12},{9,11},{10,... | collective-permute-start | bytes 786440 | tf_op jit(solution)/shard_map/B0/ppermute | solution.py:22
  51.5 9.2 %collective-permute-start.8 = (bf16[64,2048]{1,0:T(8,128)(2,1)S(1)}, bf16[64,2048]{1,0:T(8,128)(2,1)S(1)}, u32[]{:S(2)}, u32[]{:S(2)}) collective-permute-start(bf16[64,2048]{1,0:T(8,128)(2,1)S(1)} %collective-permute-done.7.refs_0_), channel_id=1, source_target_pairs={{0,1},{1,0},{2,3},{3,2},{4,5},{5,4},{6,7},{7,6},{8,9},{9,8},{10,11... | collective-permute-start | bytes 786440 | tf_op jit(solution)/shard_map/CORE0/ppermute | solution.py:22
  54.9 9.1 %collective-permute-start.17 = (bf16[64,2048]{1,0:T(8,128)(2,1)S(1)}, bf16[64,2048]{1,0:T(8,128)(2,1)S(1)}, u32[]{:S(2)}, u32[]{:S(2)}) collective-permute-start(bf16[64,2048]{1,0:T(8,128)(2,1)S(1)} %collective-permute-done.15.refs_3_), channel_id=1, source_target_pairs={{0,2},{1,5},{2,0},{3,7},{4,6},{5,1},{6,4},{7,3},{8,10},{9,13},{10,... | collective-permute-start | bytes 786440 | tf_op jit(solution)/shard_map/A1/ppermute | solution.py:22
  56.2 9.8 %collective-permute-start.18 = (bf16[64,2048]{1,0:T(8,128)(2,1)S(1)}, bf16[64,2048]{1,0:T(8,128)(2,1)S(1)}, u32[]{:S(2)}, u32[]{:S(2)}) collective-permute-start(bf16[64,2048]{1,0:T(8,128)(2,1)S(1)} %collective-permute-done.15.refs_3_), channel_id=1, source_target_pairs={{0,4},{1,3},{2,6},{3,1},{4,0},{5,7},{6,2},{7,5},{8,12},{9,11},{10,... | collective-permute-start | bytes 786440 | tf_op jit(solution)/shard_map/B1/ppermute | solution.py:22
  57.8 9.2 %collective-permute-start.11 = (bf16[64,2048]{1,0:T(8,128)(2,1)S(1)}, bf16[64,2048]{1,0:T(8,128)(2,1)S(1)}, u32[]{:S(2)}, u32[]{:S(2)}) collective-permute-start(bf16[64,2048]{1,0:T(8,128)(2,1)S(1)} %collective-permute-done.9.refs_2_), channel_id=1, source_target_pairs={{0,1},{1,0},{2,3},{3,2},{4,5},{5,4},{6,7},{7,6},{8,9},{9,8},{10,11... | collective-permute-start | bytes 786440 | tf_op jit(solution)/shard_map/AC0/ppermute | solution.py:22
  60.7 8.1 %collective-permute-start.13 = (bf16[64,2048]{1,0:T(8,128)(2,1)S(1)}, bf16[64,2048]{1,0:T(8,128)(2,1)S(1)}, u32[]{:S(2)}, u32[]{:S(2)}) collective-permute-start(bf16[64,2048]{1,0:T(8,128)(2,1)S(1)} %collective-permute-done.9.refs_2_), channel_id=1, source_target_pairs={{0,4},{1,3},{2,6},{3,1},{4,0},{5,7},{6,2},{7,5},{8,12},{9,11},{10,... | collective-permute-start | bytes 786440 | tf_op jit(solution)/shard_map/E0/ppermute | solution.py:22
  60.7 6.4 %collective-permute-start.12 = (bf16[64,2048]{1,0:T(8,128)(2,1)S(1)}, bf16[64,2048]{1,0:T(8,128)(2,1)S(1)}, u32[]{:S(2)}, u32[]{:S(2)}) collective-permute-start(bf16[64,2048]{1,0:T(8,128)(2,1)S(1)} %collective-permute-done.10.refs_3_), channel_id=1, source_target_pairs={{0,1},{1,0},{2,3},{3,2},{4,5},{5,4},{6,7},{7,6},{8,9},{9,8},{10,11... | collective-permute-start | bytes 786440 | tf_op jit(solution)/shard_map/BC0/ppermute | solution.py:22
  64.0 7.6 %collective-permute-start.21 = (bf16[64,2048]{1,0:T(8,128)(2,1)S(1)}, bf16[64,2048]{1,0:T(8,128)(2,1)S(1)}, u32[]{:S(2)}, u32[]{:S(2)}) collective-permute-start(bf16[64,2048]{1,0:T(8,128)(2,1)S(1)} %collective-permute-done.17.refs_5_), channel_id=1, source_target_pairs={{0,4},{1,3},{2,6},{3,1},{4,0},{5,7},{6,2},{7,5},{8,12},{9,11},{10,... | collective-permute-start | bytes 786440 | tf_op jit(solution)/shard_map/E1/ppermute | solution.py:22
  66.0 5.6 %collective-permute-start.16 = (bf16[64,2048]{1,0:T(8,128)(2,1)S(1)}, bf16[64,2048]{1,0:T(8,128)(2,1)S(1)}, u32[]{:S(2)}, u32[]{:S(2)}) collective-permute-start(bf16[64,2048]{1,0:T(8,128)(2,1)S(1)} %collective-permute-done.15.refs_3_), channel_id=1, source_target_pairs={{0,1},{1,0},{2,3},{3,2},{4,5},{5,4},{6,7},{7,6},{8,9},{9,8},{10,11... | collective-permute-start | bytes 786440 | tf_op jit(solution)/shard_map/CORE1/ppermute | solution.py:22
  67.0 4.6 %collective-permute-start.19 = (bf16[64,2048]{1,0:T(8,128)(2,1)S(1)}, bf16[64,2048]{1,0:T(8,128)(2,1)S(1)}, u32[]{:S(2)}, u32[]{:S(2)}) collective-permute-start(bf16[64,2048]{1,0:T(8,128)(2,1)S(1)} %collective-permute-done.17.refs_5_), channel_id=1, source_target_pairs={{0,1},{1,0},{2,3},{3,2},{4,5},{5,4},{6,7},{7,6},{8,9},{9,8},{10,11... | collective-permute-start | bytes 786440 | tf_op jit(solution)/shard_map/AC1/ppermute | solution.py:22
  67.1 4.5 %collective-permute-start.20 = (bf16[64,2048]{1,0:T(8,128)(2,1)S(1)}, bf16[64,2048]{1,0:T(8,128)(2,1)S(1)}, u32[]{:S(2)}, u32[]{:S(2)}) collective-permute-start(bf16[64,2048]{1,0:T(8,128)(2,1)S(1)} %collective-permute-done.18.refs_6_), channel_id=1, source_target_pairs={{0,1},{1,0},{2,3},{3,2},{4,5},{5,4},{6,7},{7,6},{8,9},{9,8},{10,11... | collective-permute-start | bytes 786440 | tf_op jit(solution)/shard_map/BC1/ppermute | solution.py:22
  68.8 2.8 %collective-permute-start.14 = (bf16[64,2048]{1,0:T(8,128)(2,1)S(1)}, bf16[64,2048]{1,0:T(8,128)(2,1)S(1)}, u32[]{:S(2)}, u32[]{:S(2)}) collective-permute-start(bf16[64,2048]{1,0:T(8,128)(2,1)S(1)} %collective-permute-done.13.refs_1_), channel_id=1, source_target_pairs={{0,1},{1,0},{2,3},{3,2},{4,5},{5,4},{6,7},{7,6},{8,9},{9,8},{10,11... | collective-permute-start | bytes 786440 | tf_op jit(solution)/shard_map/EC0/ppermute | solution.py:22
  71.6 2.5 %collective-permute-start.22 = (bf16[64,2048]{1,0:T(8,128)(2,1)S(1)}, bf16[64,2048]{1,0:T(8,128)(2,1)S(1)}, u32[]{:S(2)}, u32[]{:S(2)}) collective-permute-start(bf16[64,2048]{1,0:T(8,128)(2,1)S(1)} %collective-permute-done.21.refs_2_), channel_id=1, source_target_pairs={{0,1},{1,0},{2,3},{3,2},{4,5},{5,4},{6,7},{7,6},{8,9},{9,8},{10,11... | collective-permute-start | bytes 786440 | tf_op jit(solution)/shard_map/EC1/ppermute | solution.py:22

commit v4 on v3

--- a/solution.py
+++ b/solution.py
@@ -154,7 +154,8 @@
     blocks(2, 3, 4, 5, columns=ALL),
 ) + tuple(blocks(6, 7, columns=(k,)) for k in ALL)
 LATER_PHASES = (
-    blocks(*((p, 0) for p in range(6))),
+    blocks((0, 0), (1, 0)),
+    blocks(*((p, 0) for p in range(2, 6))),
     blocks((6, 0), (7, 0), *((p, 1) for p in range(6))),
     blocks((6, 1), (7, 1)),
 )
@@ -184,18 +185,22 @@
     done = parts[-1]
     parts = [from_behind(part, f"cross{k}") for k, part in enumerate(parts)]
     parts[0] = after(parts[0], done)
-    acc, late = None, []
+    core = [across_core(part, f"CORE{k}") for k, part in enumerate(parts[:1])]
+    acc = run_phase(0, lists, weights, None, [parts[0], core[0]], wide)
+    core.append(across_core(parts[1], "CORE1"))
+    late = []
     for k, own in enumerate(parts):
         a = across_first(own, f"A{k}")
         b = across_second(own, f"B{k}")
-        core = across_core(own, f"CORE{k}")
+        if k == 0:
+            a = after(a, acc)
         e = across_second(a, f"E{k}")
-        pieces = [*late, own, core, a, b, across_core(a, f"AC{k}"), across_core(b, f"BC{k}")]
+        pieces = [*late, *([own, core[k]] if k else []), a, b, across_core(a, f"AC{k}"), across_core(b, f"BC{k}")]
         if k:
             e = after(e, acc)
         late = [e, across_core(e, f"EC{k}")]
-        acc = run_phase(k, lists, weights, acc, pieces, wide)
-    return run_phase(len(parts), lists, weights, acc, late, wide, bias, range(wide // TILE))[1]
+        acc = run_phase(k + 1, lists, weights, acc, pieces, wide)
+    return run_phase(3, lists, weights, acc, late, wide, bias, range(wide // TILE))[1]
 
 
 def on_device(held, tile_values, tile_rows, tile_cols, tile_count, bias):

time: 76.1 us -> 76.4 us (level)
  starting transfers between devices: 19.4 us -> 15.8 us
  Pallas kernels: 11.7 us -> 13.6 us
  waiting for transfers between devices: 36.3 us -> 37.7 us
    ppermute x23, starting transfers between devices: 19.4 us -> 15.8 us  [sent(): lax.ppermute(array, 'section', [(i, target(i, peers)) for i in range(peer...]
    pallas_call x7 -> x8, Pallas kernels: 11.7 us -> 13.6 us  [run_phase(): pl.pallas_call(functools.partial(phase_kernel, phase, len(pieces), first,...]
    ppermute x23, waiting for transfers between devices: 36.3 us -> 37.7 us  [sent(): lax.ppermute(array, 'section', [(i, target(i, peers)) for i in range(peer...]
  transfers between devices with their start and end apart: 23 -> 23, of which waited for: 12 -> 12; matrix products, arithmetic and copies ran while one was open for 4% -> 4% of each run, Pallas kernels for 12% -> 14%
where the time goes in v4:
time: 76.4 us; the launch traced here: 75.6 us
  waiting for transfers between devices  37.7 us (49%)
  starting transfers between devices  15.8 us (21%)
  Pallas kernels  13.6 us (18%)
  local copies, waits for them, and re-layouts  4.73 us (6%)
  other arithmetic  2.89 us (4%)
  between operations  0.85 us (1%)
    ppermute x23, waiting for transfers between devices, sent(): lax.ppermute(array, 'section', [(i, target(i, peers)) for i in range(peer...  37.7 us
    ppermute x23, starting transfers between devices, sent(): lax.ppermute(array, 'section', [(i, target(i, peers)) for i in range(peer...  15.8 us
    pallas_call x8, Pallas kernels, run_phase(): pl.pallas_call(functools.partial(phase_kernel, phase, len(pieces), first,...  13.6 us
    unnamed x12, local copies, waits for them, and re-layouts  4.73 us
  transfers between devices with their start and end apart: 23, of which 12 were waited for; matrix products, arithmetic and copies ran while one was open for 4% of the time, Pallas kernels for 14%

profile of v4, /device:TPU:0, one launch (start us, length us, event | category | flops | bytes accessed | tf_op | source)
XLA Modules:
  0.0 75.6 jit_solution(1175997343212630061)
XLA Ops:
  0.0 0.5 collective-permute-start
  0.5 2.5 %collective-permute-start.1 = (bf16[64,4096]{1,0:T(8,128)(2,1)}, bf16[64,4096]{1,0:T(8,128)(2,1)S(1)}, u32[]{:S(2)}, u32[]{:S(2)}) collective-permute-start(bf16[64,4096]{1,0:T(8,128)(2,1)} %bitcast.10), channel_id=1, source_target_pairs={{0,2},{1,5},{2,0},{3,7},{4,6},{5,1},{6,4},{7,3},{8,10},{9,13},{10,... | collective-permute-start | bytes 1572872 | tf_op jit(solution)/shard_map/a/ppermute | solution.py:22
  2.9 1.6 %collective-permute-start.2 = (bf16[64,4096]{1,0:T(8,128)(2,1)}, bf16[64,4096]{1,0:T(8,128)(2,1)S(1)}, u32[]{:S(2)}, u32[]{:S(2)}) collective-permute-start(bf16[64,4096]{1,0:T(8,128)(2,1)} %bitcast.11), channel_id=1, source_target_pairs={{0,4},{1,3},{2,6},{3,1},{4,0},{5,7},{6,2},{7,5},{8,12},{9,11},{10,... | collective-permute-start | bytes 1572872 | tf_op jit(solution)/shard_map/b/ppermute | solution.py:22
  5.2 0.7 add_add_fusion
  5.9 0.7 fusion.13
  6.7 0.1 convert_reduce_fusion.3
  6.8 0.2 convert_reduce_fusion.1
  7.0 0.1 convert_reduce_fusion.2
  7.2 0.2 convert_reduce_fusion
  7.4 0.1 select_reduce_fusion.5.starts_ref
  7.5 0.1 select_reduce_fusion.3
  7.6 0.1 select_reduce_fusion.4.starts_ref
  7.7 0.1 select_reduce_fusion.2
  7.8 0.2 select_reduce_fusion
  8.0 0.0 collective-permute-done.refs_1_
  8.0 0.0 copy-start
  8.0 3.7 %copy-done = bf16[288,128,128]{2,1,0:T(8,128)(2,1)S(1)} copy-done((bf16[288,128,128]{2,1,0:T(8,128)(2,1)S(1)}, bf16[288,128,128]{2,1,0:T(8,128)(2,1)}, u32[]{:S(2)}) %copy-start) | copy-done | bytes 9437208
  11.7 1.0 %copy-done.1 = bf16[1,64,4096]{2,1,0:T(8,128)(2,1)S(1)} copy-done((bf16[1,64,4096]{2,1,0:T(8,128)(2,1)S(1)}, bf16[1,64,4096]{2,1,0:T(8,128)(2,1)}, u32[]{:S(2)}) %copy-start.1) | copy-done | bytes 524312
  12.7 1.5 %phase_0.2.refs_0_ = f32[33,64,128]{2,1,0:T(8,128)S(1)} custom-call(s32[5]{0:T(128)S(1)} %select_reduce_fusion.4.starts_ref, s32[352]{0:T(512)S(1)} %broadcast_add_fusion.list_ref, bf16[288,128,128]{2,1,0:T(8,128)(2,1)S(1)} %copy-done, bf16[64,4096]{1,0:T(8,128)(2,1)S(1)} %bitcast.12, bf16[64,4096]{1,0:T(8,128)(2,1)S(1)} %collective-permute-done.refs_1_), custom_call_target="tpu_custom_call" | custom-call | flops 2000000000 | bytes 6000000 | tf_op jit(solution)/shard_map/phase_0/pallas_call | solution.py:131
  14.2 0.0 copy-start.2
  14.3 0.5 collective-permute-done.1.refs_1_
  14.8 0.0 collective-permute-start.3
  14.8 1.1 %collective-permute-done.2.refs_2_ = bf16[64,4096]{1,0:T(8,128)(2,1)S(1)} collective-permute-done((bf16[64,4096]{1,0:T(8,128)(2,1)}, bf16[64,4096]{1,0:T(8,128)(2,1)S(1)}, u32[]{:S(2)}, u32[]{:S(2)}) %collective-permute-start.2) | collective-permute-done | bytes 524320 | tf_op jit(solution)/shard_map/b/ppermute | solution.py:22
  15.8 0.1 collective-permute-start.4
  15.9 2.1 %collective-permute-start.5 = (bf16[64,4096]{1,0:T(8,128)(2,1)S(1)}, bf16[64,4096]{1,0:T(8,128)(2,1)S(1)}, u32[]{:S(2)}, u32[]{:S(2)}) collective-permute-start(bf16[64,4096]{1,0:T(8,128)(2,1)S(1)} %collective-permute-done.1.refs_1_), channel_id=1, source_target_pairs={{0,4},{1,3},{2,6},{3,1},{4,0},{5,7},{6,2},{7,5},{8,12},{9,11},{10,... | collective-permute-start | bytes 1572872 | tf_op jit(solution)/shard_map/e/ppermute | solution.py:22
  18.1 0.0 collective-permute-done.3.refs_3_
  18.1 0.0 collective-permute-done.4.refs_4_
  18.1 2.7 %phase_1.2.refs_0_ = f32[33,64,128]{2,1,0:T(8,128)S(1)} custom-call(s32[5]{0:T(128)S(1)} %select_reduce_fusion.4.starts_ref, s32[352]{0:T(512)S(1)} %broadcast_add_fusion.list_ref, bf16[288,128,128]{2,1,0:T(8,128)(2,1)S(1)} %copy-done, f32[33,64,128]{2,1,0:T(8,128)S(1)} %phase_0.2.refs_0_, ...), custom_call_target="tpu_custom_call", output_to_operand_aliasing={{}: (3, {})} | custom-call | flops 2000000000 | bytes 6000000 | tf_op jit(solution)/shard_map/phase_1/pallas_call | solution.py:131
  20.8 4.5 %collective-permute-done.5.refs_2_ = bf16[64,4096]{1,0:T(8,128)(2,1)S(1)} collective-permute-done((bf16[64,4096]{1,0:T(8,128)(2,1)S(1)}, bf16[64,4096]{1,0:T(8,128)(2,1)S(1)}, u32[]{:S(2)}, u32[]{:S(2)}) %collective-permute-start.5) | collective-permute-done | bytes 524320 | tf_op jit(solution)/shard_map/e/ppermute | solution.py:22
  25.3 0.0 collective-permute-start.6
  25.3 1.9 %collective-permute-done.6.refs_3_ = bf16[64,4096]{1,0:T(8,128)(2,1)S(1)} collective-permute-done((bf16[64,4096]{1,0:T(8,128)(2,1)S(1)}, bf16[64,4096]{1,0:T(8,128)(2,1)S(1)}, u32[]{:S(2)}, u32[]{:S(2)}) %collective-permute-start.6) | collective-permute-done | bytes 524320 | tf_op jit(solution)/shard_map/ec/ppermute | solution.py:22
  27.2 1.3 %phase_2.2 = (f32[33,64,128]{2,1,0:T(8,128)S(1)}, bf16[64,2048]{1,0:T(8,128)(2,1)S(1)}) custom-call(s32[5]{0:T(128)S(1)} %select_reduce_fusion.4.starts_ref, s32[352]{0:T(512)S(1)} %broadcast_add_fusion.list_ref, bf16[288,128,128]{2,1,0:T(8,128)(2,1)S(1)} %copy-done, f32[33,64,128]{2,1,0:T(8,128)S(1)} %phase_1.2.refs_0_, ...), custom_call_target="tpu_custom_call", output_to_operand_aliasing={{0}: (3, {})} | custom-call | flops 2000000000 | bytes 6000000 | tf_op jit(solution)/shard_map/phase_2/pallas_call | solution.py:131
  28.4 2.9 %collective-permute-start.7 = (bf16[64,2048]{1,0:T(8,128)(2,1)S(1)}, bf16[64,2048]{1,0:T(8,128)(2,1)S(1)}, u32[]{:S(2)}, u32[]{:S(2)}) collective-permute-start(bf16[64,2048]{1,0:T(8,128)(2,1)S(1)} %get-tuple-element.16), channel_id=1, source_target_pairs={{0,8},{1,9},{2,10},{3,11},{4,12},{5,13},{6,14},{7,15},{8,0},{9,1},... | collective-permute-start | bytes 786440 | tf_op jit(solution)/shard_map/cross0/ppermute | solution.py:22
  31.3 1.3 %phase_3.2 = (f32[33,64,128]{2,1,0:T(8,128)S(1)}, bf16[64,2048]{1,0:T(8,128)(2,1)S(1)}) custom-call(s32[5]{0:T(128)S(1)} %select_reduce_fusion.4.starts_ref, s32[352]{0:T(512)S(1)} %broadcast_add_fusion.list_ref, bf16[288,128,128]{2,1,0:T(8,128)(2,1)S(1)} %copy-done, f32[33,64,128]{2,1,0:T(8,128)S(1)} %get-tuple-element.17.refs_0_, ...), custom_call_target="tpu_custom_call", output_to_operand_aliasing={{0}: (3, {})} | custom-call | flops 2000000000 | bytes 6000000 | tf_op jit(solution)/shard_map/phase_3/pallas_call | solution.py:131
  32.6 0.2 collective-permute-start.15
  32.8 17.0 %collective-permute-done.7.refs_0_ = bf16[64,2048]{1,0:T(8,128)(2,1)S(1)} collective-permute-done((bf16[64,2048]{1,0:T(8,128)(2,1)S(1)}, bf16[64,2048]{1,0:T(8,128)(2,1)S(1)}, u32[]{:S(2)}, u32[]{:S(2)}) %collective-permute-start.7) | collective-permute-done | bytes 262176 | tf_op jit(solution)/shard_map/cross0/ppermute | solution.py:22
  49.8 0.0 collective-permute-start.8
  49.8 0.2 select_reduce_fusion.1
  50.0 1.5 %collective-permute-start.9 = (bf16[64,2048]{1,0:T(8,128)(2,1)S(1)}, bf16[64,2048]{1,0:T(8,128)(2,1)S(1)}, u32[]{:S(2)}, u32[]{:S(2)}) collective-permute-start(bf16[64,2048]{1,0:T(8,128)(2,1)S(1)} %collective-permute-done.7.refs_0_), channel_id=1, source_target_pairs={{0,2},{1,5},{2,0},{3,7},{4,6},{5,1},{6,4},{7,3},{8,10},{9,13},{10,... | collective-permute-start | bytes 786440 | tf_op jit(solution)/shard_map/A0/ppermute | solution.py:22
  51.4 0.0 collective-permute-start.10
  51.4 3.2 %collective-permute-done.15.refs_3_ = bf16[64,2048]{1,0:T(8,128)(2,1)S(1)} collective-permute-done((bf16[64,2048]{1,0:T(8,128)(2,1)S(1)}, bf16[64,2048]{1,0:T(8,128)(2,1)S(1)}, u32[]{:S(2)}, u32[]{:S(2)}) %collective-permute-start.15) | collective-permute-done | bytes 262176 | tf_op jit(solution)/shard_map/cross1/ppermute | solution.py:22
  54.6 1.5 %collective-permute-start.17 = (bf16[64,2048]{1,0:T(8,128)(2,1)S(1)}, bf16[64,2048]{1,0:T(8,128)(2,1)S(1)}, u32[]{:S(2)}, u32[]{:S(2)}) collective-permute-start(bf16[64,2048]{1,0:T(8,128)(2,1)S(1)} %collective-permute-done.15.refs_3_), channel_id=1, source_target_pairs={{0,2},{1,5},{2,0},{3,7},{4,6},{5,1},{6,4},{7,3},{8,10},{9,13},{10,... | collective-permute-start | bytes 786440 | tf_op jit(solution)/shard_map/A1/ppermute | solution.py:22
  56.1 0.6 collective-permute-start.18
  56.7 0.0 collective-permute-done.8.refs_1_
  56.8 1.0 %phase_0.3.refs_0_ = f32[33,64,128]{2,1,0:T(8,128)S(1)} custom-call(s32[5]{0:T(128)S(1)} %select_reduce_fusion.5.starts_ref, s32[352]{0:T(512)S(1)} %broadcast_add_fusion.1.list_ref, bf16[288,128,128]{2,1,0:T(8,128)(2,1)S(1)} %bitcast.8, bf16[64,2048]{1,0:T(8,128)(2,1)S(1)} %collective-permute-done.7.refs_0_, bf16[64,2048]{1,0:T(8,128)(2,1)S(1)} %collective-permute-done.8.refs_1_), custom_call_target="tpu_custom_call" | custom-call | flops 2000000000 | bytes 6000000 | tf_op jit(solution)/shard_map/phase_0/pallas_call | solution.py:131
  57.7 1.4 %collective-permute-done.9.refs_1_ = bf16[64,2048]{1,0:T(8,128)(2,1)S(1)} collective-permute-done((bf16[64,2048]{1,0:T(8,128)(2,1)S(1)}, bf16[64,2048]{1,0:T(8,128)(2,1)S(1)}, u32[]{:S(2)}, u32[]{:S(2)}) %collective-permute-start.9) | collective-permute-done | bytes 262176 | tf_op jit(solution)/shard_map/A0/ppermute | solution.py:22
  59.1 0.5 collective-permute-start.11
  59.6 1.0 %collective-permute-done.10.refs_2_ = bf16[64,2048]{1,0:T(8,128)(2,1)S(1)} collective-permute-done((bf16[64,2048]{1,0:T(8,128)(2,1)S(1)}, bf16[64,2048]{1,0:T(8,128)(2,1)S(1)}, u32[]{:S(2)}, u32[]{:S(2)}) %collective-permute-start.10) | collective-permute-done | bytes 262176 | tf_op jit(solution)/shard_map/B0/ppermute | solution.py:22
  60.7 0.0 collective-permute-start.12
  60.7 4.1 %collective-permute-done.17.refs_5_ = bf16[64,2048]{1,0:T(8,128)(2,1)S(1)} collective-permute-done((bf16[64,2048]{1,0:T(8,128)(2,1)S(1)}, bf16[64,2048]{1,0:T(8,128)(2,1)S(1)}, u32[]{:S(2)}, u32[]{:S(2)}) %collective-permute-start.17) | collective-permute-done | bytes 262176 | tf_op jit(solution)/shard_map/A1/ppermute | solution.py:22
  64.7 0.0 collective-permute-start.21
  64.7 1.0 %collective-permute-done.18.refs_6_ = bf16[64,2048]{1,0:T(8,128)(2,1)S(1)} collective-permute-done((bf16[64,2048]{1,0:T(8,128)(2,1)S(1)}, bf16[64,2048]{1,0:T(8,128)(2,1)S(1)}, u32[]{:S(2)}, u32[]{:S(2)}) %collective-permute-start.18) | collective-permute-done | bytes 262176 | tf_op jit(solution)/shard_map/B1/ppermute | solution.py:22
  65.7 1.3 %collective-permute-start.16 = (bf16[64,2048]{1,0:T(8,128)(2,1)S(1)}, bf16[64,2048]{1,0:T(8,128)(2,1)S(1)}, u32[]{:S(2)}, u32[]{:S(2)}) collective-permute-start(bf16[64,2048]{1,0:T(8,128)(2,1)S(1)} %collective-permute-done.15.refs_3_), channel_id=1, source_target_pairs={{0,1},{1,0},{2,3},{3,2},{4,5},{5,4},{6,7},{7,6},{8,9},{9,8},{10,11... | collective-permute-start | bytes 786440 | tf_op jit(solution)/shard_map/CORE1/ppermute | solution.py:22
  67.0 0.1 collective-permute-start.19
  67.1 0.0 collective-permute-done.12.refs_4_
  67.1 0.4 collective-permute-start.20
  67.5 1.0 %collective-permute-done.13.refs_1_ = bf16[64,2048]{1,0:T(8,128)(2,1)S(1)} collective-permute-done((bf16[64,2048]{1,0:T(8,128)(2,1)S(1)}, bf16[64,2048]{1,0:T(8,128)(2,1)S(1)}, u32[]{:S(2)}, u32[]{:S(2)}) %collective-permute-start.13) | collective-permute-done | bytes 262176 | tf_op jit(solution)/shard_map/E0/ppermute | solution.py:22
  68.5 0.0 collective-permute-start.14
  68.5 1.8 %phase_1.3.refs_0_ = f32[33,64,128]{2,1,0:T(8,128)S(1)} custom-call(s32[5]{0:T(128)S(1)} %select_reduce_fusion.5.starts_ref, s32[352]{0:T(512)S(1)} %broadcast_add_fusion.1.list_ref, bf16[288,128,128]{2,1,0:T(8,128)(2,1)S(1)} %bitcast.8, f32[33,64,128]{2,1,0:T(8,128)S(1)} %phase_0.3.refs_0_, ...), custom_call_target="tpu_custom_call", output_to_operand_aliasing={{}: (3, {})} | custom-call | flops 2000000000 | bytes 6000000 | tf_op jit(solution)/shard_map/phase_1/pallas_call | solution.py:131
  70.3 1.0 %collective-permute-done.21.refs_2_ = bf16[64,2048]{1,0:T(8,128)(2,1)S(1)} collective-permute-done((bf16[64,2048]{1,0:T(8,128)(2,1)S(1)}, bf16[64,2048]{1,0:T(8,128)(2,1)S(1)}, u32[]{:S(2)}, u32[]{:S(2)}) %collective-permute-start.21) | collective-permute-done | bytes 262176 | tf_op jit(solution)/shard_map/E1/ppermute | solution.py:22
  71.3 0.0 collective-permute-done.20.refs_8_
  71.4 2.4 %phase_2.3.refs_0_ = f32[33,64,128]{2,1,0:T(8,128)S(1)} custom-call(s32[5]{0:T(128)S(1)} %select_reduce_fusion.5.starts_ref, s32[352]{0:T(512)S(1)} %broadcast_add_fusion.1.list_ref, bf16[288,128,128]{2,1,0:T(8,128)(2,1)S(1)} %bitcast.8, f32[33,64,128]{2,1,0:T(8,128)S(1)} %phase_1.3.refs_0_, ...), custom_call_target="tpu_custom_call", output_to_operand_aliasing={{}: (3, {})} | custom-call | flops 2000000000 | bytes 6000000 | tf_op jit(solution)/shard_map/phase_2/pallas_call | solution.py:131
  73.8 0.0 collective-permute-done.22.refs_3_
  73.8 1.8 %phase_3.3 = (f32[33,64,128]{2,1,0:T(8,128)S(1)}, bf16[64,4096]{1,0:T(8,128)(2,1)}) custom-call(s32[5]{0:T(128)S(1)} %select_reduce_fusion.5.starts_ref, s32[352]{0:T(512)S(1)} %broadcast_add_fusion.1.list_ref, bf16[288,128,128]{2,1,0:T(8,128)(2,1)S(1)} %bitcast.8, f32[33,64,128]{2,1,0:T(8,128)S(1)} %phase_2.3.refs_0_, ...), custom_call_target="tpu_custom_call", output_to_operand_aliasing={{0}: (3, {})} | custom-call | flops 2000000000 | bytes 6000000 | tf_op jit(solution)/shard_map/phase_3/pallas_call | solution.py:131
  (24 shorter events, 0.1 us)
Async XLA Ops:
  0.0 8.0 %collective-permute-start = (bf16[64,4096]{1,0:T(8,128)(2,1)}, bf16[64,4096]{1,0:T(8,128)(2,1)S(1)}, u32[]{:S(2)}, u32[]{:S(2)}) collective-permute-start(bf16[64,4096]{1,0:T(8,128)(2,1)} %bitcast.9), channel_id=1, source_target_pairs={{0,1},{1,0},{2,3},{3,2},{4,5},{5,4},{6,7},{7,6},{8,9},{9,8},{10,11... | collective-permute-start | bytes 1572872 | tf_op jit(solution)/shard_map/core/ppermute | solution.py:22
  0.5 14.3 %collective-permute-start.1 = (bf16[64,4096]{1,0:T(8,128)(2,1)}, bf16[64,4096]{1,0:T(8,128)(2,1)S(1)}, u32[]{:S(2)}, u32[]{:S(2)}) collective-permute-start(bf16[64,4096]{1,0:T(8,128)(2,1)} %bitcast.10), channel_id=1, source_target_pairs={{0,2},{1,5},{2,0},{3,7},{4,6},{5,1},{6,4},{7,3},{8,10},{9,13},{10,... | collective-permute-start | bytes 1572872 | tf_op jit(solution)/shard_map/a/ppermute | solution.py:22
  2.9 12.9 %collective-permute-start.2 = (bf16[64,4096]{1,0:T(8,128)(2,1)}, bf16[64,4096]{1,0:T(8,128)(2,1)S(1)}, u32[]{:S(2)}, u32[]{:S(2)}) collective-permute-start(bf16[64,4096]{1,0:T(8,128)(2,1)} %bitcast.11), channel_id=1, source_target_pairs={{0,4},{1,3},{2,6},{3,1},{4,0},{5,7},{6,2},{7,5},{8,12},{9,11},{10,... | collective-permute-start | bytes 1572872 | tf_op jit(solution)/shard_map/b/ppermute | solution.py:22
  8.0 3.7 %copy-start = (bf16[288,128,128]{2,1,0:T(8,128)(2,1)S(1)}, bf16[288,128,128]{2,1,0:T(8,128)(2,1)}, u32[]{:S(2)}) copy-start(bf16[288,128,128]{2,1,0:T(8,128)(2,1)} %w_ref.15) | copy-start | bytes 28311556
  11.7 1.0 %copy-start.1 = (bf16[1,64,4096]{2,1,0:T(8,128)(2,1)S(1)}, bf16[1,64,4096]{2,1,0:T(8,128)(2,1)}, u32[]{:S(2)}) copy-start(bf16[1,64,4096]{2,1,0:T(8,128)(2,1)} %param.6) | copy-start | bytes 1572868
  14.2 12.9 %copy-start.2 = (f32[4096]{0:T(1024)S(1)}, f32[4096]{0:T(1024)}, u32[]{:S(2)}) copy-start(f32[4096]{0:T(1024)} %param.11) | copy-start | bytes 49156
  14.8 3.3 %collective-permute-start.3 = (bf16[64,4096]{1,0:T(8,128)(2,1)S(1)}, bf16[64,4096]{1,0:T(8,128)(2,1)S(1)}, u32[]{:S(2)}, u32[]{:S(2)}) collective-permute-start(bf16[64,4096]{1,0:T(8,128)(2,1)S(1)} %collective-permute-done.1.refs_1_), channel_id=1, source_target_pairs={{0,1},{1,0},{2,3},{3,2},{4,5},{5,4},{6,7},{7,6},{8,9},{9,8},{10,11... | collective-permute-start | bytes 1572872 | tf_op jit(solution)/shard_map/ac/ppermute | solution.py:22
  15.8 2.3 %collective-permute-start.4 = (bf16[64,4096]{1,0:T(8,128)(2,1)S(1)}, bf16[64,4096]{1,0:T(8,128)(2,1)S(1)}, u32[]{:S(2)}, u32[]{:S(2)}) collective-permute-start(bf16[64,4096]{1,0:T(8,128)(2,1)S(1)} %collective-permute-done.2.refs_2_), channel_id=1, source_target_pairs={{0,1},{1,0},{2,3},{3,2},{4,5},{5,4},{6,7},{7,6},{8,9},{9,8},{10,11... | collective-permute-start | bytes 1572872 | tf_op jit(solution)/shard_map/bc/ppermute | solution.py:22
  15.9 9.3 %collective-permute-start.5 = (bf16[64,4096]{1,0:T(8,128)(2,1)S(1)}, bf16[64,4096]{1,0:T(8,128)(2,1)S(1)}, u32[]{:S(2)}, u32[]{:S(2)}) collective-permute-start(bf16[64,4096]{1,0:T(8,128)(2,1)S(1)} %collective-permute-done.1.refs_1_), channel_id=1, source_target_pairs={{0,4},{1,3},{2,6},{3,1},{4,0},{5,7},{6,2},{7,5},{8,12},{9,11},{10,... | collective-permute-start | bytes 1572872 | tf_op jit(solution)/shard_map/e/ppermute | solution.py:22
  25.3 1.9 %collective-permute-start.6 = (bf16[64,4096]{1,0:T(8,128)(2,1)S(1)}, bf16[64,4096]{1,0:T(8,128)(2,1)S(1)}, u32[]{:S(2)}, u32[]{:S(2)}) collective-permute-start(bf16[64,4096]{1,0:T(8,128)(2,1)S(1)} %collective-permute-done.5.refs_2_), channel_id=1, source_target_pairs={{0,1},{1,0},{2,3},{3,2},{4,5},{5,4},{6,7},{7,6},{8,9},{9,8},{10,11... | collective-permute-start | bytes 1572872 | tf_op jit(solution)/shard_map/ec/ppermute | solution.py:22
  27.2 29.6 %slice-start = ((s8[9437184]{0:T(1024)(128)(4,1)}), s8[4194304]{0:T(1024)(128)(4,1)S(1)}, s32[]{:S(2)}) async-start(s8[9437184]{0:T(1024)(128)(4,1)} %bitcast.7), calls=%async_computation | async-start | bytes 8388608
  27.2 29.6 %slice-start.1 = ((s8[9437184]{0:T(1024)(128)(4,1)}), s8[4194304]{0:T(1024)(128)(4,1)S(1)}, s32[]{:S(2)}) async-start(s8[9437184]{0:T(1024)(128)(4,1)} %bitcast.7), calls=%async_computation.1 | async-start | bytes 8388608
  28.4 21.4 %collective-permute-start.7 = (bf16[64,2048]{1,0:T(8,128)(2,1)S(1)}, bf16[64,2048]{1,0:T(8,128)(2,1)S(1)}, u32[]{:S(2)}, u32[]{:S(2)}) collective-permute-start(bf16[64,2048]{1,0:T(8,128)(2,1)S(1)} %get-tuple-element.16), channel_id=1, source_target_pairs={{0,8},{1,9},{2,10},{3,11},{4,12},{5,13},{6,14},{7,15},{8,0},{9,1},... | collective-permute-start | bytes 786440 | tf_op jit(solution)/shard_map/cross0/ppermute | solution.py:22
  31.3 25.5 %slice-start.2 = ((s8[9437184]{0:T(1024)(128)(4,1)}), s8[1048576]{0:T(1024)(128)(4,1)S(1)}, s32[]{:S(2)}) async-start(s8[9437184]{0:T(1024)(128)(4,1)} %bitcast.7), calls=%async_computation.2 | async-start | bytes 2097152
  32.6 22.0 %collective-permute-start.15 = (bf16[64,2048]{1,0:T(8,128)(2,1)S(1)}, bf16[64,2048]{1,0:T(8,128)(2,1)S(1)}, u32[]{:S(2)}, u32[]{:S(2)}) collective-permute-start(bf16[64,2048]{1,0:T(8,128)(2,1)S(1)} %get-tuple-element.18), channel_id=1, source_target_pairs={{0,8},{1,9},{2,10},{3,11},{4,12},{5,13},{6,14},{7,15},{8,0},{9,1},... | collective-permute-start | bytes 786440 | tf_op jit(solution)/shard_map/cross1/ppermute | solution.py:22
  49.8 7.0 %collective-permute-start.8 = (bf16[64,2048]{1,0:T(8,128)(2,1)S(1)}, bf16[64,2048]{1,0:T(8,128)(2,1)S(1)}, u32[]{:S(2)}, u32[]{:S(2)}) collective-permute-start(bf16[64,2048]{1,0:T(8,128)(2,1)S(1)} %collective-permute-done.7.refs_0_), channel_id=1, source_target_pairs={{0,1},{1,0},{2,3},{3,2},{4,5},{5,4},{6,7},{7,6},{8,9},{9,8},{10,11... | collective-permute-start | bytes 786440 | tf_op jit(solution)/shard_map/CORE0/ppermute | solution.py:22
  50.0 9.2 %collective-permute-start.9 = (bf16[64,2048]{1,0:T(8,128)(2,1)S(1)}, bf16[64,2048]{1,0:T(8,128)(2,1)S(1)}, u32[]{:S(2)}, u32[]{:S(2)}) collective-permute-start(bf16[64,2048]{1,0:T(8,128)(2,1)S(1)} %collective-permute-done.7.refs_0_), channel_id=1, source_target_pairs={{0,2},{1,5},{2,0},{3,7},{4,6},{5,1},{6,4},{7,3},{8,10},{9,13},{10,... | collective-permute-start | bytes 786440 | tf_op jit(solution)/shard_map/A0/ppermute | solution.py:22
  51.4 9.2 %collective-permute-start.10 = (bf16[64,2048]{1,0:T(8,128)(2,1)S(1)}, bf16[64,2048]{1,0:T(8,128)(2,1)S(1)}, u32[]{:S(2)}, u32[]{:S(2)}) collective-permute-start(bf16[64,2048]{1,0:T(8,128)(2,1)S(1)} %collective-permute-done.7.refs_0_), channel_id=1, source_target_pairs={{0,4},{1,3},{2,6},{3,1},{4,0},{5,7},{6,2},{7,5},{8,12},{9,11},{10,... | collective-permute-start | bytes 786440 | tf_op jit(solution)/shard_map/B0/ppermute | solution.py:22
  54.6 10.2 %collective-permute-start.17 = (bf16[64,2048]{1,0:T(8,128)(2,1)S(1)}, bf16[64,2048]{1,0:T(8,128)(2,1)S(1)}, u32[]{:S(2)}, u32[]{:S(2)}) collective-permute-start(bf16[64,2048]{1,0:T(8,128)(2,1)S(1)} %collective-permute-done.15.refs_3_), channel_id=1, source_target_pairs={{0,2},{1,5},{2,0},{3,7},{4,6},{5,1},{6,4},{7,3},{8,10},{9,13},{10,... | collective-permute-start | bytes 786440 | tf_op jit(solution)/shard_map/A1/ppermute | solution.py:22
  56.1 9.6 %collective-permute-start.18 = (bf16[64,2048]{1,0:T(8,128)(2,1)S(1)}, bf16[64,2048]{1,0:T(8,128)(2,1)S(1)}, u32[]{:S(2)}, u32[]{:S(2)}) collective-permute-start(bf16[64,2048]{1,0:T(8,128)(2,1)S(1)} %collective-permute-done.15.refs_3_), channel_id=1, source_target_pairs={{0,4},{1,3},{2,6},{3,1},{4,0},{5,7},{6,2},{7,5},{8,12},{9,11},{10,... | collective-permute-start | bytes 786440 | tf_op jit(solution)/shard_map/B1/ppermute | solution.py:22
  59.1 7.9 %collective-permute-start.11 = (bf16[64,2048]{1,0:T(8,128)(2,1)S(1)}, bf16[64,2048]{1,0:T(8,128)(2,1)S(1)}, u32[]{:S(2)}, u32[]{:S(2)}) collective-permute-start(bf16[64,2048]{1,0:T(8,128)(2,1)S(1)} %collective-permute-done.9.refs_1_), channel_id=1, source_target_pairs={{0,1},{1,0},{2,3},{3,2},{4,5},{5,4},{6,7},{7,6},{8,9},{9,8},{10,11... | collective-permute-start | bytes 786440 | tf_op jit(solution)/shard_map/AC0/ppermute | solution.py:22
  60.7 6.4 %collective-permute-start.12 = (bf16[64,2048]{1,0:T(8,128)(2,1)S(1)}, bf16[64,2048]{1,0:T(8,128)(2,1)S(1)}, u32[]{:S(2)}, u32[]{:S(2)}) collective-permute-start(bf16[64,2048]{1,0:T(8,128)(2,1)S(1)} %collective-permute-done.10.refs_2_), channel_id=1, source_target_pairs={{0,1},{1,0},{2,3},{3,2},{4,5},{5,4},{6,7},{7,6},{8,9},{9,8},{10,11... | collective-permute-start | bytes 786440 | tf_op jit(solution)/shard_map/BC0/ppermute | solution.py:22
  60.7 7.9 %collective-permute-start.13 = (bf16[64,2048]{1,0:T(8,128)(2,1)S(1)}, bf16[64,2048]{1,0:T(8,128)(2,1)S(1)}, u32[]{:S(2)}, u32[]{:S(2)}) collective-permute-start(bf16[64,2048]{1,0:T(8,128)(2,1)S(1)} %collective-permute-done.9.refs_1_), channel_id=1, source_target_pairs={{0,4},{1,3},{2,6},{3,1},{4,0},{5,7},{6,2},{7,5},{8,12},{9,11},{10,... | collective-permute-start | bytes 786440 | tf_op jit(solution)/shard_map/E0/ppermute | solution.py:22
  64.7 6.6 %collective-permute-start.21 = (bf16[64,2048]{1,0:T(8,128)(2,1)S(1)}, bf16[64,2048]{1,0:T(8,128)(2,1)S(1)}, u32[]{:S(2)}, u32[]{:S(2)}) collective-permute-start(bf16[64,2048]{1,0:T(8,128)(2,1)S(1)} %collective-permute-done.17.refs_5_), channel_id=1, source_target_pairs={{0,4},{1,3},{2,6},{3,1},{4,0},{5,7},{6,2},{7,5},{8,12},{9,11},{10,... | collective-permute-start | bytes 786440 | tf_op jit(solution)/shard_map/E1/ppermute | solution.py:22
  65.7 5.6 %collective-permute-start.16 = (bf16[64,2048]{1,0:T(8,128)(2,1)S(1)}, bf16[64,2048]{1,0:T(8,128)(2,1)S(1)}, u32[]{:S(2)}, u32[]{:S(2)}) collective-permute-start(bf16[64,2048]{1,0:T(8,128)(2,1)S(1)} %collective-permute-done.15.refs_3_), channel_id=1, source_target_pairs={{0,1},{1,0},{2,3},{3,2},{4,5},{5,4},{6,7},{7,6},{8,9},{9,8},{10,11... | collective-permute-start | bytes 786440 | tf_op jit(solution)/shard_map/CORE1/ppermute | solution.py:22
  67.0 4.3 %collective-permute-start.19 = (bf16[64,2048]{1,0:T(8,128)(2,1)S(1)}, bf16[64,2048]{1,0:T(8,128)(2,1)S(1)}, u32[]{:S(2)}, u32[]{:S(2)}) collective-permute-start(bf16[64,2048]{1,0:T(8,128)(2,1)S(1)} %collective-permute-done.17.refs_5_), channel_id=1, source_target_pairs={{0,1},{1,0},{2,3},{3,2},{4,5},{5,4},{6,7},{7,6},{8,9},{9,8},{10,11... | collective-permute-start | bytes 786440 | tf_op jit(solution)/shard_map/AC1/ppermute | solution.py:22
  67.1 4.3 %collective-permute-start.20 = (bf16[64,2048]{1,0:T(8,128)(2,1)S(1)}, bf16[64,2048]{1,0:T(8,128)(2,1)S(1)}, u32[]{:S(2)}, u32[]{:S(2)}) collective-permute-start(bf16[64,2048]{1,0:T(8,128)(2,1)S(1)} %collective-permute-done.18.refs_6_), channel_id=1, source_target_pairs={{0,1},{1,0},{2,3},{3,2},{4,5},{5,4},{6,7},{7,6},{8,9},{9,8},{10,11... | collective-permute-start | bytes 786440 | tf_op jit(solution)/shard_map/BC1/ppermute | solution.py:22
  68.5 2.8 %collective-permute-start.14 = (bf16[64,2048]{1,0:T(8,128)(2,1)S(1)}, bf16[64,2048]{1,0:T(8,128)(2,1)S(1)}, u32[]{:S(2)}, u32[]{:S(2)}) collective-permute-start(bf16[64,2048]{1,0:T(8,128)(2,1)S(1)} %collective-permute-done.13.refs_1_), channel_id=1, source_target_pairs={{0,1},{1,0},{2,3},{3,2},{4,5},{5,4},{6,7},{7,6},{8,9},{9,8},{10,11... | collective-permute-start | bytes 786440 | tf_op jit(solution)/shard_map/EC0/ppermute | solution.py:22
  71.3 2.4 %collective-permute-start.22 = (bf16[64,2048]{1,0:T(8,128)(2,1)S(1)}, bf16[64,2048]{1,0:T(8,128)(2,1)S(1)}, u32[]{:S(2)}, u32[]{:S(2)}) collective-permute-start(bf16[64,2048]{1,0:T(8,128)(2,1)S(1)} %collective-permute-done.21.refs_2_), channel_id=1, source_target_pairs={{0,1},{1,0},{2,3},{3,2},{4,5},{5,4},{6,7},{7,6},{8,9},{9,8},{10,11... | collective-permute-start | bytes 786440 | tf_op jit(solution)/shard_map/EC1/ppermute | solution.py:22

commit v5 on v4

--- a/solution.py
+++ b/solution.py
@@ -10,7 +10,7 @@
 TILE = 128
 SPLIT = 8
 TICKS = 2
-UNROLL = 16
+UNROLL = 32
 CHUNKS = 2
 
 CORE, X, Z = 1, 2, 4

time: 76.4 us -> 75.5 us (0.988)
  Pallas kernels: 13.6 us -> 10.7 us
  waiting for transfers between devices: 37.7 us -> 39.5 us
    pallas_call x8, Pallas kernels: 13.6 us -> 10.7 us  [run_phase(): pl.pallas_call(functools.partial(phase_kernel, phase, len(pieces), first,...]
    ppermute x23, waiting for transfers between devices: 37.7 us -> 39.5 us  [sent(): lax.ppermute(array, 'section', [(i, target(i, peers)) for i in range(peer...]
  transfers between devices with their start and end apart: 23 -> 23, of which waited for: 12 -> 12; matrix products, arithmetic and copies ran while one was open for 4% -> 4% of each run, Pallas kernels for 14% -> 10%
where the time goes in v5:
time: 75.5 us; the launch traced here: 75.1 us
  waiting for transfers between devices  39.5 us (52%)
  starting transfers between devices  16.5 us (22%)
  Pallas kernels  10.7 us (14%)
  local copies, waits for them, and re-layouts  4.73 us (6%)
  other arithmetic  2.89 us (4%)
  between operations  0.83 us (1%)
    ppermute x23, waiting for transfers between devices, sent(): lax.ppermute(array, 'section', [(i, target(i, peers)) for i in range(peer...  39.5 us
    ppermute x23, starting transfers between devices, sent(): lax.ppermute(array, 'section', [(i, target(i, peers)) for i in range(peer...  16.5 us
    pallas_call x8, Pallas kernels, run_phase(): pl.pallas_call(functools.partial(phase_kernel, phase, len(pieces), first,...  10.7 us
    unnamed x12, local copies, waits for them, and re-layouts  4.73 us
  transfers between devices with their start and end apart: 23, of which 12 were waited for; matrix products, arithmetic and copies ran while one was open for 4% of the time, Pallas kernels for 10%

profile of v5, /device:TPU:0, one launch (start us, length us, event | category | flops | bytes accessed | tf_op | source)
XLA Modules:
  0.0 75.1 jit_solution(4337802003617434883)
XLA Ops:
  0.0 0.5 collective-permute-start
  0.5 2.5 %collective-permute-start.1 = (bf16[64,4096]{1,0:T(8,128)(2,1)}, bf16[64,4096]{1,0:T(8,128)(2,1)S(1)}, u32[]{:S(2)}, u32[]{:S(2)}) collective-permute-start(bf16[64,4096]{1,0:T(8,128)(2,1)} %bitcast.10), channel_id=1, source_target_pairs={{0,2},{1,5},{2,0},{3,7},{4,6},{5,1},{6,4},{7,3},{8,10},{9,13},{10,... | collective-permute-start | bytes 1572872 | tf_op jit(solution)/shard_map/a/ppermute | solution.py:22
  2.9 1.6 %collective-permute-start.2 = (bf16[64,4096]{1,0:T(8,128)(2,1)}, bf16[64,4096]{1,0:T(8,128)(2,1)S(1)}, u32[]{:S(2)}, u32[]{:S(2)}) collective-permute-start(bf16[64,4096]{1,0:T(8,128)(2,1)} %bitcast.11), channel_id=1, source_target_pairs={{0,4},{1,3},{2,6},{3,1},{4,0},{5,7},{6,2},{7,5},{8,12},{9,11},{10,... | collective-permute-start | bytes 1572872 | tf_op jit(solution)/shard_map/b/ppermute | solution.py:22
  5.2 0.7 add_add_fusion
  5.9 0.7 fusion.13
  6.7 0.1 convert_reduce_fusion.3
  6.8 0.2 convert_reduce_fusion.1
  7.0 0.1 convert_reduce_fusion.2
  7.2 0.2 convert_reduce_fusion
  7.4 0.1 select_reduce_fusion.5.starts_ref
  7.5 0.1 select_reduce_fusion.3
  7.6 0.1 select_reduce_fusion.4.starts_ref
  7.7 0.1 select_reduce_fusion.2
  7.8 0.2 select_reduce_fusion
  8.0 0.0 collective-permute-done.refs_1_
  8.0 0.0 copy-start
  8.0 3.7 %copy-done = bf16[288,128,128]{2,1,0:T(8,128)(2,1)S(1)} copy-done((bf16[288,128,128]{2,1,0:T(8,128)(2,1)S(1)}, bf16[288,128,128]{2,1,0:T(8,128)(2,1)}, u32[]{:S(2)}) %copy-start) | copy-done | bytes 9437208
  11.7 1.0 %copy-done.1 = bf16[1,64,4096]{2,1,0:T(8,128)(2,1)S(1)} copy-done((bf16[1,64,4096]{2,1,0:T(8,128)(2,1)S(1)}, bf16[1,64,4096]{2,1,0:T(8,128)(2,1)}, u32[]{:S(2)}) %copy-start.1) | copy-done | bytes 524312
  12.7 1.1 %phase_0.2.refs_0_ = f32[33,64,128]{2,1,0:T(8,128)S(1)} custom-call(s32[5]{0:T(128)S(1)} %select_reduce_fusion.4.starts_ref, s32[416]{0:T(512)S(1)} %broadcast_add_fusion.list_ref, bf16[288,128,128]{2,1,0:T(8,128)(2,1)S(1)} %copy-done, bf16[64,4096]{1,0:T(8,128)(2,1)S(1)} %bitcast.12, bf16[64,4096]{1,0:T(8,128)(2,1)S(1)} %collective-permute-done.refs_1_), custom_call_target="tpu_custom_call" | custom-call | flops 2000000000 | bytes 6000000 | tf_op jit(solution)/shard_map/phase_0/pallas_call | solution.py:131
  13.8 0.0 copy-start.2
  13.8 0.9 %collective-permute-done.1.refs_1_ = bf16[64,4096]{1,0:T(8,128)(2,1)S(1)} collective-permute-done((bf16[64,4096]{1,0:T(8,128)(2,1)}, bf16[64,4096]{1,0:T(8,128)(2,1)S(1)}, u32[]{:S(2)}, u32[]{:S(2)}) %collective-permute-start.1) | collective-permute-done | bytes 524320 | tf_op jit(solution)/shard_map/a/ppermute | solution.py:22
  14.8 0.0 collective-permute-start.3
  14.8 1.1 %collective-permute-done.2.refs_2_ = bf16[64,4096]{1,0:T(8,128)(2,1)S(1)} collective-permute-done((bf16[64,4096]{1,0:T(8,128)(2,1)}, bf16[64,4096]{1,0:T(8,128)(2,1)S(1)}, u32[]{:S(2)}, u32[]{:S(2)}) %collective-permute-start.2) | collective-permute-done | bytes 524320 | tf_op jit(solution)/shard_map/b/ppermute | solution.py:22
  15.8 0.1 collective-permute-start.4
  15.9 2.1 %collective-permute-start.5 = (bf16[64,4096]{1,0:T(8,128)(2,1)S(1)}, bf16[64,4096]{1,0:T(8,128)(2,1)S(1)}, u32[]{:S(2)}, u32[]{:S(2)}) collective-permute-start(bf16[64,4096]{1,0:T(8,128)(2,1)S(1)} %collective-permute-done.1.refs_1_), channel_id=1, source_target_pairs={{0,4},{1,3},{2,6},{3,1},{4,0},{5,7},{6,2},{7,5},{8,12},{9,11},{10,... | collective-permute-start | bytes 1572872 | tf_op jit(solution)/shard_map/e/ppermute | solution.py:22
  18.1 0.0 collective-permute-done.3.refs_3_
  18.1 0.0 collective-permute-done.4.refs_4_
  18.1 1.6 %phase_1.2.refs_0_ = f32[33,64,128]{2,1,0:T(8,128)S(1)} custom-call(s32[5]{0:T(128)S(1)} %select_reduce_fusion.4.starts_ref, s32[416]{0:T(512)S(1)} %broadcast_add_fusion.list_ref, bf16[288,128,128]{2,1,0:T(8,128)(2,1)S(1)} %copy-done, f32[33,64,128]{2,1,0:T(8,128)S(1)} %phase_0.2.refs_0_, ...), custom_call_target="tpu_custom_call", output_to_operand_aliasing={{}: (3, {})} | custom-call | flops 2000000000 | bytes 6000000 | tf_op jit(solution)/shard_map/phase_1/pallas_call | solution.py:131
  19.7 5.6 %collective-permute-done.5.refs_2_ = bf16[64,4096]{1,0:T(8,128)(2,1)S(1)} collective-permute-done((bf16[64,4096]{1,0:T(8,128)(2,1)S(1)}, bf16[64,4096]{1,0:T(8,128)(2,1)S(1)}, u32[]{:S(2)}, u32[]{:S(2)}) %collective-permute-start.5) | collective-permute-done | bytes 524320 | tf_op jit(solution)/shard_map/e/ppermute | solution.py:22
  25.3 0.0 collective-permute-start.6
  25.3 1.9 %collective-permute-done.6.refs_3_ = bf16[64,4096]{1,0:T(8,128)(2,1)S(1)} collective-permute-done((bf16[64,4096]{1,0:T(8,128)(2,1)S(1)}, bf16[64,4096]{1,0:T(8,128)(2,1)S(1)}, u32[]{:S(2)}, u32[]{:S(2)}) %collective-permute-start.6) | collective-permute-done | bytes 524320 | tf_op jit(solution)/shard_map/ec/ppermute | solution.py:22
  27.2 1.1 %phase_2.2 = (f32[33,64,128]{2,1,0:T(8,128)S(1)}, bf16[64,2048]{1,0:T(8,128)(2,1)S(1)}) custom-call(s32[5]{0:T(128)S(1)} %select_reduce_fusion.4.starts_ref, s32[416]{0:T(512)S(1)} %broadcast_add_fusion.list_ref, bf16[288,128,128]{2,1,0:T(8,128)(2,1)S(1)} %copy-done, f32[33,64,128]{2,1,0:T(8,128)S(1)} %phase_1.2.refs_0_, ...), custom_call_target="tpu_custom_call", output_to_operand_aliasing={{0}: (3, {})} | custom-call | flops 2000000000 | bytes 6000000 | tf_op jit(solution)/shard_map/phase_2/pallas_call | solution.py:131
  28.3 3.3 %collective-permute-start.7 = (bf16[64,2048]{1,0:T(8,128)(2,1)S(1)}, bf16[64,2048]{1,0:T(8,128)(2,1)S(1)}, u32[]{:S(2)}, u32[]{:S(2)}) collective-permute-start(bf16[64,2048]{1,0:T(8,128)(2,1)S(1)} %get-tuple-element.16), channel_id=1, source_target_pairs={{0,8},{1,9},{2,10},{3,11},{4,12},{5,13},{6,14},{7,15},{8,0},{9,1},... | collective-permute-start | bytes 786440 | tf_op jit(solution)/shard_map/cross0/ppermute | solution.py:22
  31.6 1.1 %phase_3.2 = (f32[33,64,128]{2,1,0:T(8,128)S(1)}, bf16[64,2048]{1,0:T(8,128)(2,1)S(1)}) custom-call(s32[5]{0:T(128)S(1)} %select_reduce_fusion.4.starts_ref, s32[416]{0:T(512)S(1)} %broadcast_add_fusion.list_ref, bf16[288,128,128]{2,1,0:T(8,128)(2,1)S(1)} %copy-done, f32[33,64,128]{2,1,0:T(8,128)S(1)} %get-tuple-element.17.refs_0_, ...), custom_call_target="tpu_custom_call", output_to_operand_aliasing={{0}: (3, {})} | custom-call | flops 2000000000 | bytes 6000000 | tf_op jit(solution)/shard_map/phase_3/pallas_call | solution.py:131
  32.7 0.5 collective-permute-start.15
  33.3 16.7 %collective-permute-done.7.refs_0_ = bf16[64,2048]{1,0:T(8,128)(2,1)S(1)} collective-permute-done((bf16[64,2048]{1,0:T(8,128)(2,1)S(1)}, bf16[64,2048]{1,0:T(8,128)(2,1)S(1)}, u32[]{:S(2)}, u32[]{:S(2)}) %collective-permute-start.7) | collective-permute-done | bytes 262176 | tf_op jit(solution)/shard_map/cross0/ppermute | solution.py:22
  50.0 0.2 select_reduce_fusion.1
  50.2 1.4 %collective-permute-start.9 = (bf16[64,2048]{1,0:T(8,128)(2,1)S(1)}, bf16[64,2048]{1,0:T(8,128)(2,1)S(1)}, u32[]{:S(2)}, u32[]{:S(2)}) collective-permute-start(bf16[64,2048]{1,0:T(8,128)(2,1)S(1)} %collective-permute-done.7.refs_0_), channel_id=1, source_target_pairs={{0,2},{1,5},{2,0},{3,7},{4,6},{5,1},{6,4},{7,3},{8,10},{9,13},{10,... | collective-permute-start | bytes 786440 | tf_op jit(solution)/shard_map/A0/ppermute | solution.py:22
  51.6 0.0 collective-permute-start.10
  51.6 3.1 %collective-permute-done.15.refs_3_ = bf16[64,2048]{1,0:T(8,128)(2,1)S(1)} collective-permute-done((bf16[64,2048]{1,0:T(8,128)(2,1)S(1)}, bf16[64,2048]{1,0:T(8,128)(2,1)S(1)}, u32[]{:S(2)}, u32[]{:S(2)}) %collective-permute-start.15) | collective-permute-done | bytes 262176 | tf_op jit(solution)/shard_map/cross1/ppermute | solution.py:22
  54.7 1.5 %collective-permute-start.17 = (bf16[64,2048]{1,0:T(8,128)(2,1)S(1)}, bf16[64,2048]{1,0:T(8,128)(2,1)S(1)}, u32[]{:S(2)}, u32[]{:S(2)}) collective-permute-start(bf16[64,2048]{1,0:T(8,128)(2,1)S(1)} %collective-permute-done.15.refs_3_), channel_id=1, source_target_pairs={{0,2},{1,5},{2,0},{3,7},{4,6},{5,1},{6,4},{7,3},{8,10},{9,13},{10,... | collective-permute-start | bytes 786440 | tf_op jit(solution)/shard_map/A1/ppermute | solution.py:22
  56.3 0.6 collective-permute-start.18
  56.9 0.0 collective-permute-done.8.refs_1_
  56.9 1.1 %phase_0.3.refs_0_ = f32[33,64,128]{2,1,0:T(8,128)S(1)} custom-call(s32[5]{0:T(128)S(1)} %select_reduce_fusion.5.starts_ref, s32[416]{0:T(512)S(1)} %broadcast_add_fusion.1.list_ref, bf16[288,128,128]{2,1,0:T(8,128)(2,1)S(1)} %bitcast.8, bf16[64,2048]{1,0:T(8,128)(2,1)S(1)} %collective-permute-done.7.refs_0_, bf16[64,2048]{1,0:T(8,128)(2,1)S(1)} %collective-permute-done.8.refs_1_), custom_call_target="tpu_custom_call" | custom-call | flops 2000000000 | bytes 6000000 | tf_op jit(solution)/shard_map/phase_0/pallas_call | solution.py:131
  58.0 1.3 %collective-permute-done.9.refs_1_ = bf16[64,2048]{1,0:T(8,128)(2,1)S(1)} collective-permute-done((bf16[64,2048]{1,0:T(8,128)(2,1)S(1)}, bf16[64,2048]{1,0:T(8,128)(2,1)S(1)}, u32[]{:S(2)}, u32[]{:S(2)}) %collective-permute-start.9) | collective-permute-done | bytes 262176 | tf_op jit(solution)/shard_map/A0/ppermute | solution.py:22
  59.3 0.5 collective-permute-start.11
  59.8 1.1 %collective-permute-done.10.refs_2_ = bf16[64,2048]{1,0:T(8,128)(2,1)S(1)} collective-permute-done((bf16[64,2048]{1,0:T(8,128)(2,1)S(1)}, bf16[64,2048]{1,0:T(8,128)(2,1)S(1)}, u32[]{:S(2)}, u32[]{:S(2)}) %collective-permute-start.10) | collective-permute-done | bytes 262176 | tf_op jit(solution)/shard_map/B0/ppermute | solution.py:22
  60.8 0.0 collective-permute-start.13
  60.8 4.1 %collective-permute-done.17.refs_5_ = bf16[64,2048]{1,0:T(8,128)(2,1)S(1)} collective-permute-done((bf16[64,2048]{1,0:T(8,128)(2,1)S(1)}, bf16[64,2048]{1,0:T(8,128)(2,1)S(1)}, u32[]{:S(2)}, u32[]{:S(2)}) %collective-permute-start.17) | collective-permute-done | bytes 262176 | tf_op jit(solution)/shard_map/A1/ppermute | solution.py:22
  64.9 0.0 collective-permute-start.21
  64.9 0.9 %collective-permute-done.18.refs_6_ = bf16[64,2048]{1,0:T(8,128)(2,1)S(1)} collective-permute-done((bf16[64,2048]{1,0:T(8,128)(2,1)S(1)}, bf16[64,2048]{1,0:T(8,128)(2,1)S(1)}, u32[]{:S(2)}, u32[]{:S(2)}) %collective-permute-start.18) | collective-permute-done | bytes 262176 | tf_op jit(solution)/shard_map/B1/ppermute | solution.py:22
  65.9 1.3 %collective-permute-start.16 = (bf16[64,2048]{1,0:T(8,128)(2,1)S(1)}, bf16[64,2048]{1,0:T(8,128)(2,1)S(1)}, u32[]{:S(2)}, u32[]{:S(2)}) collective-permute-start(bf16[64,2048]{1,0:T(8,128)(2,1)S(1)} %collective-permute-done.15.refs_3_), channel_id=1, source_target_pairs={{0,1},{1,0},{2,3},{3,2},{4,5},{5,4},{6,7},{7,6},{8,9},{9,8},{10,11... | collective-permute-start | bytes 786440 | tf_op jit(solution)/shard_map/CORE1/ppermute | solution.py:22
  67.1 0.0 collective-permute-done.11.refs_3_
  67.1 0.1 collective-permute-start.19
  67.2 0.4 collective-permute-start.20
  67.7 1.0 %collective-permute-done.13.refs_1_ = bf16[64,2048]{1,0:T(8,128)(2,1)S(1)} collective-permute-done((bf16[64,2048]{1,0:T(8,128)(2,1)S(1)}, bf16[64,2048]{1,0:T(8,128)(2,1)S(1)}, u32[]{:S(2)}, u32[]{:S(2)}) %collective-permute-start.13) | collective-permute-done | bytes 262176 | tf_op jit(solution)/shard_map/E0/ppermute | solution.py:22
  68.7 0.0 collective-permute-start.14
  68.7 1.1 %phase_1.3.refs_0_ = f32[33,64,128]{2,1,0:T(8,128)S(1)} custom-call(s32[5]{0:T(128)S(1)} %select_reduce_fusion.5.starts_ref, s32[416]{0:T(512)S(1)} %broadcast_add_fusion.1.list_ref, bf16[288,128,128]{2,1,0:T(8,128)(2,1)S(1)} %bitcast.8, f32[33,64,128]{2,1,0:T(8,128)S(1)} %phase_0.3.refs_0_, ...), custom_call_target="tpu_custom_call", output_to_operand_aliasing={{}: (3, {})} | custom-call | flops 2000000000 | bytes 6000000 | tf_op jit(solution)/shard_map/phase_1/pallas_call | solution.py:131
  69.7 1.7 %collective-permute-done.21.refs_2_ = bf16[64,2048]{1,0:T(8,128)(2,1)S(1)} collective-permute-done((bf16[64,2048]{1,0:T(8,128)(2,1)S(1)}, bf16[64,2048]{1,0:T(8,128)(2,1)S(1)}, u32[]{:S(2)}, u32[]{:S(2)}) %collective-permute-start.21) | collective-permute-done | bytes 262176 | tf_op jit(solution)/shard_map/E1/ppermute | solution.py:22
  71.5 0.0 collective-permute-done.19.refs_7_
  71.5 0.0 collective-permute-done.20.refs_8_
  71.5 1.6 %phase_2.3.refs_0_ = f32[33,64,128]{2,1,0:T(8,128)S(1)} custom-call(s32[5]{0:T(128)S(1)} %select_reduce_fusion.5.starts_ref, s32[416]{0:T(512)S(1)} %broadcast_add_fusion.1.list_ref, bf16[288,128,128]{2,1,0:T(8,128)(2,1)S(1)} %bitcast.8, f32[33,64,128]{2,1,0:T(8,128)S(1)} %phase_1.3.refs_0_, ...), custom_call_target="tpu_custom_call", output_to_operand_aliasing={{}: (3, {})} | custom-call | flops 2000000000 | bytes 6000000 | tf_op jit(solution)/shard_map/phase_2/pallas_call | solution.py:131
  73.1 0.0 collective-permute-done.22.refs_3_
  73.1 2.0 %phase_3.3 = (f32[33,64,128]{2,1,0:T(8,128)S(1)}, bf16[64,4096]{1,0:T(8,128)(2,1)}) custom-call(s32[5]{0:T(128)S(1)} %select_reduce_fusion.5.starts_ref, s32[416]{0:T(512)S(1)} %broadcast_add_fusion.1.list_ref, bf16[288,128,128]{2,1,0:T(8,128)(2,1)S(1)} %bitcast.8, f32[33,64,128]{2,1,0:T(8,128)S(1)} %phase_2.3.refs_0_, ...), custom_call_target="tpu_custom_call", output_to_operand_aliasing={{0}: (3, {})} | custom-call | flops 2000000000 | bytes 6000000 | tf_op jit(solution)/shard_map/phase_3/pallas_call | solution.py:131
  (24 shorter events, 0.1 us)
Async XLA Ops:
  0.0 8.0 %collective-permute-start = (bf16[64,4096]{1,0:T(8,128)(2,1)}, bf16[64,4096]{1,0:T(8,128)(2,1)S(1)}, u32[]{:S(2)}, u32[]{:S(2)}) collective-permute-start(bf16[64,4096]{1,0:T(8,128)(2,1)} %bitcast.9), channel_id=1, source_target_pairs={{0,1},{1,0},{2,3},{3,2},{4,5},{5,4},{6,7},{7,6},{8,9},{9,8},{10,11... | collective-permute-start | bytes 1572872 | tf_op jit(solution)/shard_map/core/ppermute | solution.py:22
  0.5 14.3 %collective-permute-start.1 = (bf16[64,4096]{1,0:T(8,128)(2,1)}, bf16[64,4096]{1,0:T(8,128)(2,1)S(1)}, u32[]{:S(2)}, u32[]{:S(2)}) collective-permute-start(bf16[64,4096]{1,0:T(8,128)(2,1)} %bitcast.10), channel_id=1, source_target_pairs={{0,2},{1,5},{2,0},{3,7},{4,6},{5,1},{6,4},{7,3},{8,10},{9,13},{10,... | collective-permute-start | bytes 1572872 | tf_op jit(solution)/shard_map/a/ppermute | solution.py:22
  2.9 12.9 %collective-permute-start.2 = (bf16[64,4096]{1,0:T(8,128)(2,1)}, bf16[64,4096]{1,0:T(8,128)(2,1)S(1)}, u32[]{:S(2)}, u32[]{:S(2)}) collective-permute-start(bf16[64,4096]{1,0:T(8,128)(2,1)} %bitcast.11), channel_id=1, source_target_pairs={{0,4},{1,3},{2,6},{3,1},{4,0},{5,7},{6,2},{7,5},{8,12},{9,11},{10,... | collective-permute-start | bytes 1572872 | tf_op jit(solution)/shard_map/b/ppermute | solution.py:22
  8.0 3.7 %copy-start = (bf16[288,128,128]{2,1,0:T(8,128)(2,1)S(1)}, bf16[288,128,128]{2,1,0:T(8,128)(2,1)}, u32[]{:S(2)}) copy-start(bf16[288,128,128]{2,1,0:T(8,128)(2,1)} %w_ref.15) | copy-start | bytes 28311556
  11.7 1.0 %copy-start.1 = (bf16[1,64,4096]{2,1,0:T(8,128)(2,1)S(1)}, bf16[1,64,4096]{2,1,0:T(8,128)(2,1)}, u32[]{:S(2)}) copy-start(bf16[1,64,4096]{2,1,0:T(8,128)(2,1)} %param.6) | copy-start | bytes 1572868
  13.8 13.3 %copy-start.2 = (f32[4096]{0:T(1024)S(1)}, f32[4096]{0:T(1024)}, u32[]{:S(2)}) copy-start(f32[4096]{0:T(1024)} %param.11) | copy-start | bytes 49156
  14.8 3.3 %collective-permute-start.3 = (bf16[64,4096]{1,0:T(8,128)(2,1)S(1)}, bf16[64,4096]{1,0:T(8,128)(2,1)S(1)}, u32[]{:S(2)}, u32[]{:S(2)}) collective-permute-start(bf16[64,4096]{1,0:T(8,128)(2,1)S(1)} %collective-permute-done.1.refs_1_), channel_id=1, source_target_pairs={{0,1},{1,0},{2,3},{3,2},{4,5},{5,4},{6,7},{7,6},{8,9},{9,8},{10,11... | collective-permute-start | bytes 1572872 | tf_op jit(solution)/shard_map/ac/ppermute | solution.py:22
  15.8 2.3 %collective-permute-start.4 = (bf16[64,4096]{1,0:T(8,128)(2,1)S(1)}, bf16[64,4096]{1,0:T(8,128)(2,1)S(1)}, u32[]{:S(2)}, u32[]{:S(2)}) collective-permute-start(bf16[64,4096]{1,0:T(8,128)(2,1)S(1)} %collective-permute-done.2.refs_2_), channel_id=1, source_target_pairs={{0,1},{1,0},{2,3},{3,2},{4,5},{5,4},{6,7},{7,6},{8,9},{9,8},{10,11... | collective-permute-start | bytes 1572872 | tf_op jit(solution)/shard_map/bc/ppermute | solution.py:22
  15.9 9.3 %collective-permute-start.5 = (bf16[64,4096]{1,0:T(8,128)(2,1)S(1)}, bf16[64,4096]{1,0:T(8,128)(2,1)S(1)}, u32[]{:S(2)}, u32[]{:S(2)}) collective-permute-start(bf16[64,4096]{1,0:T(8,128)(2,1)S(1)} %collective-permute-done.1.refs_1_), channel_id=1, source_target_pairs={{0,4},{1,3},{2,6},{3,1},{4,0},{5,7},{6,2},{7,5},{8,12},{9,11},{10,... | collective-permute-start | bytes 1572872 | tf_op jit(solution)/shard_map/e/ppermute | solution.py:22
  25.3 1.9 %collective-permute-start.6 = (bf16[64,4096]{1,0:T(8,128)(2,1)S(1)}, bf16[64,4096]{1,0:T(8,128)(2,1)S(1)}, u32[]{:S(2)}, u32[]{:S(2)}) collective-permute-start(bf16[64,4096]{1,0:T(8,128)(2,1)S(1)} %collective-permute-done.5.refs_2_), channel_id=1, source_target_pairs={{0,1},{1,0},{2,3},{3,2},{4,5},{5,4},{6,7},{7,6},{8,9},{9,8},{10,11... | collective-permute-start | bytes 1572872 | tf_op jit(solution)/shard_map/ec/ppermute | solution.py:22
  27.2 29.7 %slice-start = ((s8[9437184]{0:T(1024)(128)(4,1)}), s8[4194304]{0:T(1024)(128)(4,1)S(1)}, s32[]{:S(2)}) async-start(s8[9437184]{0:T(1024)(128)(4,1)} %bitcast.7), calls=%async_computation | async-start | bytes 8388608
  27.2 29.7 %slice-start.1 = ((s8[9437184]{0:T(1024)(128)(4,1)}), s8[4194304]{0:T(1024)(128)(4,1)S(1)}, s32[]{:S(2)}) async-start(s8[9437184]{0:T(1024)(128)(4,1)} %bitcast.7), calls=%async_computation.1 | async-start | bytes 8388608
  28.3 21.7 %collective-permute-start.7 = (bf16[64,2048]{1,0:T(8,128)(2,1)S(1)}, bf16[64,2048]{1,0:T(8,128)(2,1)S(1)}, u32[]{:S(2)}, u32[]{:S(2)}) collective-permute-start(bf16[64,2048]{1,0:T(8,128)(2,1)S(1)} %get-tuple-element.16), channel_id=1, source_target_pairs={{0,8},{1,9},{2,10},{3,11},{4,12},{5,13},{6,14},{7,15},{8,0},{9,1},... | collective-permute-start | bytes 786440 | tf_op jit(solution)/shard_map/cross0/ppermute | solution.py:22
  31.6 25.3 %slice-start.2 = ((s8[9437184]{0:T(1024)(128)(4,1)}), s8[1048576]{0:T(1024)(128)(4,1)S(1)}, s32[]{:S(2)}) async-start(s8[9437184]{0:T(1024)(128)(4,1)} %bitcast.7), calls=%async_computation.2 | async-start | bytes 2097152
  32.7 22.0 %collective-permute-start.15 = (bf16[64,2048]{1,0:T(8,128)(2,1)S(1)}, bf16[64,2048]{1,0:T(8,128)(2,1)S(1)}, u32[]{:S(2)}, u32[]{:S(2)}) collective-permute-start(bf16[64,2048]{1,0:T(8,128)(2,1)S(1)} %get-tuple-element.18), channel_id=1, source_target_pairs={{0,8},{1,9},{2,10},{3,11},{4,12},{5,13},{6,14},{7,15},{8,0},{9,1},... | collective-permute-start | bytes 786440 | tf_op jit(solution)/shard_map/cross1/ppermute | solution.py:22
  50.0 6.9 %collective-permute-start.8 = (bf16[64,2048]{1,0:T(8,128)(2,1)S(1)}, bf16[64,2048]{1,0:T(8,128)(2,1)S(1)}, u32[]{:S(2)}, u32[]{:S(2)}) collective-permute-start(bf16[64,2048]{1,0:T(8,128)(2,1)S(1)} %collective-permute-done.7.refs_0_), channel_id=1, source_target_pairs={{0,1},{1,0},{2,3},{3,2},{4,5},{5,4},{6,7},{7,6},{8,9},{9,8},{10,11... | collective-permute-start | bytes 786440 | tf_op jit(solution)/shard_map/CORE0/ppermute | solution.py:22
  50.2 9.2 %collective-permute-start.9 = (bf16[64,2048]{1,0:T(8,128)(2,1)S(1)}, bf16[64,2048]{1,0:T(8,128)(2,1)S(1)}, u32[]{:S(2)}, u32[]{:S(2)}) collective-permute-start(bf16[64,2048]{1,0:T(8,128)(2,1)S(1)} %collective-permute-done.7.refs_0_), channel_id=1, source_target_pairs={{0,2},{1,5},{2,0},{3,7},{4,6},{5,1},{6,4},{7,3},{8,10},{9,13},{10,... | collective-permute-start | bytes 786440 | tf_op jit(solution)/shard_map/A0/ppermute | solution.py:22
  51.6 9.2 %collective-permute-start.10 = (bf16[64,2048]{1,0:T(8,128)(2,1)S(1)}, bf16[64,2048]{1,0:T(8,128)(2,1)S(1)}, u32[]{:S(2)}, u32[]{:S(2)}) collective-permute-start(bf16[64,2048]{1,0:T(8,128)(2,1)S(1)} %collective-permute-done.7.refs_0_), channel_id=1, source_target_pairs={{0,4},{1,3},{2,6},{3,1},{4,0},{5,7},{6,2},{7,5},{8,12},{9,11},{10,... | collective-permute-start | bytes 786440 | tf_op jit(solution)/shard_map/B0/ppermute | solution.py:22
  54.7 10.2 %collective-permute-start.17 = (bf16[64,2048]{1,0:T(8,128)(2,1)S(1)}, bf16[64,2048]{1,0:T(8,128)(2,1)S(1)}, u32[]{:S(2)}, u32[]{:S(2)}) collective-permute-start(bf16[64,2048]{1,0:T(8,128)(2,1)S(1)} %collective-permute-done.15.refs_3_), channel_id=1, source_target_pairs={{0,2},{1,5},{2,0},{3,7},{4,6},{5,1},{6,4},{7,3},{8,10},{9,13},{10,... | collective-permute-start | bytes 786440 | tf_op jit(solution)/shard_map/A1/ppermute | solution.py:22
  56.3 9.6 %collective-permute-start.18 = (bf16[64,2048]{1,0:T(8,128)(2,1)S(1)}, bf16[64,2048]{1,0:T(8,128)(2,1)S(1)}, u32[]{:S(2)}, u32[]{:S(2)}) collective-permute-start(bf16[64,2048]{1,0:T(8,128)(2,1)S(1)} %collective-permute-done.15.refs_3_), channel_id=1, source_target_pairs={{0,4},{1,3},{2,6},{3,1},{4,0},{5,7},{6,2},{7,5},{8,12},{9,11},{10,... | collective-permute-start | bytes 786440 | tf_op jit(solution)/shard_map/B1/ppermute | solution.py:22
  59.3 7.8 %collective-permute-start.11 = (bf16[64,2048]{1,0:T(8,128)(2,1)S(1)}, bf16[64,2048]{1,0:T(8,128)(2,1)S(1)}, u32[]{:S(2)}, u32[]{:S(2)}) collective-permute-start(bf16[64,2048]{1,0:T(8,128)(2,1)S(1)} %collective-permute-done.9.refs_1_), channel_id=1, source_target_pairs={{0,1},{1,0},{2,3},{3,2},{4,5},{5,4},{6,7},{7,6},{8,9},{9,8},{10,11... | collective-permute-start | bytes 786440 | tf_op jit(solution)/shard_map/AC0/ppermute | solution.py:22
  60.8 6.4 %collective-permute-start.12 = (bf16[64,2048]{1,0:T(8,128)(2,1)S(1)}, bf16[64,2048]{1,0:T(8,128)(2,1)S(1)}, u32[]{:S(2)}, u32[]{:S(2)}) collective-permute-start(bf16[64,2048]{1,0:T(8,128)(2,1)S(1)} %collective-permute-done.10.refs_2_), channel_id=1, source_target_pairs={{0,1},{1,0},{2,3},{3,2},{4,5},{5,4},{6,7},{7,6},{8,9},{9,8},{10,11... | collective-permute-start | bytes 786440 | tf_op jit(solution)/shard_map/BC0/ppermute | solution.py:22
  60.8 7.8 %collective-permute-start.13 = (bf16[64,2048]{1,0:T(8,128)(2,1)S(1)}, bf16[64,2048]{1,0:T(8,128)(2,1)S(1)}, u32[]{:S(2)}, u32[]{:S(2)}) collective-permute-start(bf16[64,2048]{1,0:T(8,128)(2,1)S(1)} %collective-permute-done.9.refs_1_), channel_id=1, source_target_pairs={{0,4},{1,3},{2,6},{3,1},{4,0},{5,7},{6,2},{7,5},{8,12},{9,11},{10,... | collective-permute-start | bytes 786440 | tf_op jit(solution)/shard_map/E0/ppermute | solution.py:22
  64.9 6.5 %collective-permute-start.21 = (bf16[64,2048]{1,0:T(8,128)(2,1)S(1)}, bf16[64,2048]{1,0:T(8,128)(2,1)S(1)}, u32[]{:S(2)}, u32[]{:S(2)}) collective-permute-start(bf16[64,2048]{1,0:T(8,128)(2,1)S(1)} %collective-permute-done.17.refs_5_), channel_id=1, source_target_pairs={{0,4},{1,3},{2,6},{3,1},{4,0},{5,7},{6,2},{7,5},{8,12},{9,11},{10,... | collective-permute-start | bytes 786440 | tf_op jit(solution)/shard_map/E1/ppermute | solution.py:22
  65.9 5.6 %collective-permute-start.16 = (bf16[64,2048]{1,0:T(8,128)(2,1)S(1)}, bf16[64,2048]{1,0:T(8,128)(2,1)S(1)}, u32[]{:S(2)}, u32[]{:S(2)}) collective-permute-start(bf16[64,2048]{1,0:T(8,128)(2,1)S(1)} %collective-permute-done.15.refs_3_), channel_id=1, source_target_pairs={{0,1},{1,0},{2,3},{3,2},{4,5},{5,4},{6,7},{7,6},{8,9},{9,8},{10,11... | collective-permute-start | bytes 786440 | tf_op jit(solution)/shard_map/CORE1/ppermute | solution.py:22
  67.1 4.3 %collective-permute-start.19 = (bf16[64,2048]{1,0:T(8,128)(2,1)S(1)}, bf16[64,2048]{1,0:T(8,128)(2,1)S(1)}, u32[]{:S(2)}, u32[]{:S(2)}) collective-permute-start(bf16[64,2048]{1,0:T(8,128)(2,1)S(1)} %collective-permute-done.17.refs_5_), channel_id=1, source_target_pairs={{0,1},{1,0},{2,3},{3,2},{4,5},{5,4},{6,7},{7,6},{8,9},{9,8},{10,11... | collective-permute-start | bytes 786440 | tf_op jit(solution)/shard_map/AC1/ppermute | solution.py:22
  67.2 4.3 %collective-permute-start.20 = (bf16[64,2048]{1,0:T(8,128)(2,1)S(1)}, bf16[64,2048]{1,0:T(8,128)(2,1)S(1)}, u32[]{:S(2)}, u32[]{:S(2)}) collective-permute-start(bf16[64,2048]{1,0:T(8,128)(2,1)S(1)} %collective-permute-done.18.refs_6_), channel_id=1, source_target_pairs={{0,1},{1,0},{2,3},{3,2},{4,5},{5,4},{6,7},{7,6},{8,9},{9,8},{10,11... | collective-permute-start | bytes 786440 | tf_op jit(solution)/shard_map/BC1/ppermute | solution.py:22
  68.7 2.8 %collective-permute-start.14 = (bf16[64,2048]{1,0:T(8,128)(2,1)S(1)}, bf16[64,2048]{1,0:T(8,128)(2,1)S(1)}, u32[]{:S(2)}, u32[]{:S(2)}) collective-permute-start(bf16[64,2048]{1,0:T(8,128)(2,1)S(1)} %collective-permute-done.13.refs_1_), channel_id=1, source_target_pairs={{0,1},{1,0},{2,3},{3,2},{4,5},{5,4},{6,7},{7,6},{8,9},{9,8},{10,11... | collective-permute-start | bytes 786440 | tf_op jit(solution)/shard_map/EC0/ppermute | solution.py:22
  71.5 1.6 %collective-permute-start.22 = (bf16[64,2048]{1,0:T(8,128)(2,1)S(1)}, bf16[64,2048]{1,0:T(8,128)(2,1)S(1)}, u32[]{:S(2)}, u32[]{:S(2)}) collective-permute-start(bf16[64,2048]{1,0:T(8,128)(2,1)S(1)} %collective-permute-done.21.refs_2_), channel_id=1, source_target_pairs={{0,1},{1,0},{2,3},{3,2},{4,5},{5,4},{6,7},{7,6},{8,9},{9,8},{10,11... | collective-permute-start | bytes 786440 | tf_op jit(solution)/shard_map/EC1/ppermute | solution.py:22

commit v6 on v5

--- a/solution.py
+++ b/solution.py
@@ -152,7 +152,8 @@
 FIRST_PHASES = (
     blocks(0, 1, columns=ALL),
     blocks(2, 3, 4, 5, columns=ALL),
-) + tuple(blocks(6, 7, columns=(k,)) for k in ALL)
+    blocks(6, columns=ALL),
+) + tuple(blocks(7, columns=(k,)) for k in ALL)
 LATER_PHASES = (
     blocks((0, 0), (1, 0)),
     blocks(*((p, 0) for p in range(2, 6))),
@@ -172,11 +173,12 @@
     pieces = [a, b, across_core(a, "ac"), across_core(b, "bc")]
     acc = run_phase(1, lists, weights, acc, pieces, wide)
     e = after(e, acc)
-    pieces = [e, across_core(e, "ec")]
+    pieces = [across_core(e, "ec")]
+    acc = run_phase(2, lists, weights, acc, [e], wide)
     outs = []
     part = wide // TILE // CHUNKS
     for k in ALL:
-        acc, out = run_phase(2 + k, lists, weights, acc, pieces, wide, bias, range(k * part, (k + 1) * part))
+        acc, out = run_phase(3 + k, lists, weights, acc, pieces, wide, bias, range(k * part, (k + 1) * part))
         outs.append(out)
     return outs
 

time: 75.5 us -> 76 us (level)
  Pallas kernels: 10.7 us -> 13.4 us
  waiting for transfers between devices: 39.5 us -> 37.1 us
    pallas_call x8 -> x9, Pallas kernels: 10.7 us -> 13.4 us  [run_phase(): pl.pallas_call(functools.partial(phase_kernel, phase, len(pieces), first,...]
    ppermute x23, waiting for transfers between devices: 39.5 us -> 37.1 us  [sent(): lax.ppermute(array, 'section', [(i, target(i, peers)) for i in range(peer...]
  transfers between devices with their start and end apart: 23 -> 23, of which waited for: 12 -> 12; matrix products, arithmetic and copies ran while one was open for 4% -> 4% of each run, Pallas kernels for 10% -> 14%
where the time goes in v6:
time: 76 us; the launch traced here: 75.5 us
  waiting for transfers between devices  37.1 us (49%)
  starting transfers between devices  16.5 us (22%)
  Pallas kernels  13.4 us (18%)
  local copies, waits for them, and re-layouts  4.73 us (6%)
  other arithmetic  2.92 us (4%)
  between operations  0.84 us (1%)
    ppermute x23, waiting for transfers between devices, sent(): lax.ppermute(array, 'section', [(i, target(i, peers)) for i in range(peer...  37.1 us
    ppermute x23, starting transfers between devices, sent(): lax.ppermute(array, 'section', [(i, target(i, peers)) for i in range(peer...  16.5 us
    pallas_call x9, Pallas kernels, run_phase(): pl.pallas_call(functools.partial(phase_kernel, phase, len(pieces), first,...  13.4 us
    unnamed x12, local copies, waits for them, and re-layouts  4.73 us
  transfers between devices with their start and end apart: 23, of which 12 were waited for; matrix products, arithmetic and copies ran while one was open for 4% of the time, Pallas kernels for 14%

profile of v6, /device:TPU:0, one launch (start us, length us, event | category | flops | bytes accessed | tf_op | source)
XLA Modules:
  0.0 75.5 jit_solution(11218999126642739535)
XLA Ops:
  0.0 0.5 collective-permute-start
  0.5 2.5 %collective-permute-start.1 = (bf16[64,4096]{1,0:T(8,128)(2,1)}, bf16[64,4096]{1,0:T(8,128)(2,1)S(1)}, u32[]{:S(2)}, u32[]{:S(2)}) collective-permute-start(bf16[64,4096]{1,0:T(8,128)(2,1)} %bitcast.10), channel_id=1, source_target_pairs={{0,2},{1,5},{2,0},{3,7},{4,6},{5,1},{6,4},{7,3},{8,10},{9,13},{10,... | collective-permute-start | bytes 1572872 | tf_op jit(solution)/shard_map/a/ppermute | solution.py:22
  2.9 1.6 %collective-permute-start.2 = (bf16[64,4096]{1,0:T(8,128)(2,1)}, bf16[64,4096]{1,0:T(8,128)(2,1)S(1)}, u32[]{:S(2)}, u32[]{:S(2)}) collective-permute-start(bf16[64,4096]{1,0:T(8,128)(2,1)} %bitcast.11), channel_id=1, source_target_pairs={{0,4},{1,3},{2,6},{3,1},{4,0},{5,7},{6,2},{7,5},{8,12},{9,11},{10,... | collective-permute-start | bytes 1572872 | tf_op jit(solution)/shard_map/b/ppermute | solution.py:22
  5.2 0.7 add_add_fusion
  5.9 0.7 fusion.13
  6.7 0.1 convert_reduce_fusion.3
  6.8 0.2 convert_reduce_fusion.1
  7.0 0.1 convert_reduce_fusion.2
  7.2 0.2 convert_reduce_fusion
  7.4 0.1 select_reduce_fusion.5.starts_ref
  7.5 0.1 select_reduce_fusion.3
  7.6 0.1 select_reduce_fusion.4.starts_ref
  7.7 0.1 select_reduce_fusion.2
  7.8 0.2 select_reduce_fusion
  8.0 0.0 collective-permute-done.refs_1_
  8.0 0.0 copy-start
  8.0 3.7 %copy-done = bf16[288,128,128]{2,1,0:T(8,128)(2,1)S(1)} copy-done((bf16[288,128,128]{2,1,0:T(8,128)(2,1)S(1)}, bf16[288,128,128]{2,1,0:T(8,128)(2,1)}, u32[]{:S(2)}) %copy-start) | copy-done | bytes 9437208
  11.7 1.0 %copy-done.1 = bf16[1,64,4096]{2,1,0:T(8,128)(2,1)S(1)} copy-done((bf16[1,64,4096]{2,1,0:T(8,128)(2,1)S(1)}, bf16[1,64,4096]{2,1,0:T(8,128)(2,1)}, u32[]{:S(2)}) %copy-start.1) | copy-done | bytes 524312
  12.7 1.6 %phase_0.2.refs_0_ = f32[33,64,128]{2,1,0:T(8,128)S(1)} custom-call(s32[6]{0:T(128)S(1)} %select_reduce_fusion.4.starts_ref, s32[448]{0:T(512)S(1)} %broadcast_add_fusion.list_ref, bf16[288,128,128]{2,1,0:T(8,128)(2,1)S(1)} %copy-done, bf16[64,4096]{1,0:T(8,128)(2,1)S(1)} %bitcast.12, bf16[64,4096]{1,0:T(8,128)(2,1)S(1)} %collective-permute-done.refs_1_), custom_call_target="tpu_custom_call" | custom-call | flops 2000000000 | bytes 6000000 | tf_op jit(solution)/shard_map/phase_0/pallas_call | solution.py:131
  14.3 0.5 collective-permute-done.1.refs_1_
  14.8 0.0 collective-permute-start.3
  14.8 1.1 %collective-permute-done.2.refs_2_ = bf16[64,4096]{1,0:T(8,128)(2,1)S(1)} collective-permute-done((bf16[64,4096]{1,0:T(8,128)(2,1)}, bf16[64,4096]{1,0:T(8,128)(2,1)S(1)}, u32[]{:S(2)}, u32[]{:S(2)}) %collective-permute-start.2) | collective-permute-done | bytes 524320 | tf_op jit(solution)/shard_map/b/ppermute | solution.py:22
  15.8 0.1 collective-permute-start.4
  15.9 2.1 %collective-permute-start.5 = (bf16[64,4096]{1,0:T(8,128)(2,1)S(1)}, bf16[64,4096]{1,0:T(8,128)(2,1)S(1)}, u32[]{:S(2)}, u32[]{:S(2)}) collective-permute-start(bf16[64,4096]{1,0:T(8,128)(2,1)S(1)} %collective-permute-done.1.refs_1_), channel_id=1, source_target_pairs={{0,4},{1,3},{2,6},{3,1},{4,0},{5,7},{6,2},{7,5},{8,12},{9,11},{10,... | collective-permute-start | bytes 1572872 | tf_op jit(solution)/shard_map/e/ppermute | solution.py:22
  18.1 0.0 collective-permute-done.3.refs_3_
  18.1 0.0 collective-permute-done.4.refs_4_
  18.1 2.0 %phase_1.2.refs_0_ = f32[33,64,128]{2,1,0:T(8,128)S(1)} custom-call(s32[6]{0:T(128)S(1)} %select_reduce_fusion.4.starts_ref, s32[448]{0:T(512)S(1)} %broadcast_add_fusion.list_ref, bf16[288,128,128]{2,1,0:T(8,128)(2,1)S(1)} %copy-done, f32[33,64,128]{2,1,0:T(8,128)S(1)} %phase_0.2.refs_0_, ...), custom_call_target="tpu_custom_call", output_to_operand_aliasing={{}: (3, {})} | custom-call | flops 2000000000 | bytes 6000000 | tf_op jit(solution)/shard_map/phase_1/pallas_call | solution.py:131
  20.1 0.0 copy-start.2
  20.1 5.1 %collective-permute-done.5.refs_1_ = bf16[64,4096]{1,0:T(8,128)(2,1)S(1)} collective-permute-done((bf16[64,4096]{1,0:T(8,128)(2,1)S(1)}, bf16[64,4096]{1,0:T(8,128)(2,1)S(1)}, u32[]{:S(2)}, u32[]{:S(2)}) %collective-permute-start.5) | collective-permute-done | bytes 524320 | tf_op jit(solution)/shard_map/e/ppermute | solution.py:22
  25.3 0.0 collective-permute-start.6
  25.3 1.0 %phase_2.2.refs_0_ = f32[33,64,128]{2,1,0:T(8,128)S(1)} custom-call(s32[6]{0:T(128)S(1)} %select_reduce_fusion.4.starts_ref, s32[448]{0:T(512)S(1)} %broadcast_add_fusion.list_ref, bf16[288,128,128]{2,1,0:T(8,128)(2,1)S(1)} %copy-done, f32[33,64,128]{2,1,0:T(8,128)S(1)} %phase_1.2.refs_0_, ...), custom_call_target="tpu_custom_call", output_to_operand_aliasing={{}: (3, {})} | custom-call | flops 2000000000 | bytes 6000000 | tf_op jit(solution)/shard_map/phase_2/pallas_call | solution.py:131
  26.3 0.9 %collective-permute-done.6.refs_2_ = bf16[64,4096]{1,0:T(8,128)(2,1)S(1)} collective-permute-done((bf16[64,4096]{1,0:T(8,128)(2,1)S(1)}, bf16[64,4096]{1,0:T(8,128)(2,1)S(1)}, u32[]{:S(2)}, u32[]{:S(2)}) %collective-permute-start.6) | collective-permute-done | bytes 524320 | tf_op jit(solution)/shard_map/ec/ppermute | solution.py:22
  27.2 1.1 %phase_3.2 = (f32[33,64,128]{2,1,0:T(8,128)S(1)}, bf16[64,2048]{1,0:T(8,128)(2,1)S(1)}) custom-call(s32[6]{0:T(128)S(1)} %select_reduce_fusion.4.starts_ref, s32[448]{0:T(512)S(1)} %broadcast_add_fusion.list_ref, bf16[288,128,128]{2,1,0:T(8,128)(2,1)S(1)} %copy-done, f32[33,64,128]{2,1,0:T(8,128)S(1)} %phase_2.2.refs_0_, ...), custom_call_target="tpu_custom_call", output_to_operand_aliasing={{0}: (3, {})} | custom-call | flops 2000000000 | bytes 6000000 | tf_op jit(solution)/shard_map/phase_3/pallas_call | solution.py:131
  28.3 2.9 %collective-permute-start.7 = (bf16[64,2048]{1,0:T(8,128)(2,1)S(1)}, bf16[64,2048]{1,0:T(8,128)(2,1)S(1)}, u32[]{:S(2)}, u32[]{:S(2)}) collective-permute-start(bf16[64,2048]{1,0:T(8,128)(2,1)S(1)} %get-tuple-element.16), channel_id=1, source_target_pairs={{0,8},{1,9},{2,10},{3,11},{4,12},{5,13},{6,14},{7,15},{8,0},{9,1},... | collective-permute-start | bytes 786440 | tf_op jit(solution)/shard_map/cross0/ppermute | solution.py:22
  31.1 1.1 %phase_4.1 = (f32[33,64,128]{2,1,0:T(8,128)S(1)}, bf16[64,2048]{1,0:T(8,128)(2,1)S(1)}) custom-call(s32[6]{0:T(128)S(1)} %select_reduce_fusion.4.starts_ref, s32[448]{0:T(512)S(1)} %broadcast_add_fusion.list_ref, bf16[288,128,128]{2,1,0:T(8,128)(2,1)S(1)} %copy-done, f32[33,64,128]{2,1,0:T(8,128)S(1)} %get-tuple-element.17.refs_0_, ...), custom_call_target="tpu_custom_call", output_to_operand_aliasing={{0}: (3, {})} | custom-call | flops 2000000000 | bytes 6000000 | tf_op jit(solution)/shard_map/phase_4/pallas_call | solution.py:131
  32.2 0.2 collective-permute-start.15
  32.4 17.2 %collective-permute-done.7.refs_0_ = bf16[64,2048]{1,0:T(8,128)(2,1)S(1)} collective-permute-done((bf16[64,2048]{1,0:T(8,128)(2,1)S(1)}, bf16[64,2048]{1,0:T(8,128)(2,1)S(1)}, u32[]{:S(2)}, u32[]{:S(2)}) %collective-permute-start.7) | collective-permute-done | bytes 262176 | tf_op jit(solution)/shard_map/cross0/ppermute | solution.py:22
  49.6 0.0 collective-permute-start.8
  49.6 0.2 select_reduce_fusion.1
  49.8 1.8 %collective-permute-start.9 = (bf16[64,2048]{1,0:T(8,128)(2,1)S(1)}, bf16[64,2048]{1,0:T(8,128)(2,1)S(1)}, u32[]{:S(2)}, u32[]{:S(2)}) collective-permute-start(bf16[64,2048]{1,0:T(8,128)(2,1)S(1)} %collective-permute-done.7.refs_0_), channel_id=1, source_target_pairs={{0,2},{1,5},{2,0},{3,7},{4,6},{5,1},{6,4},{7,3},{8,10},{9,13},{10,... | collective-permute-start | bytes 786440 | tf_op jit(solution)/shard_map/A0/ppermute | solution.py:22
  51.6 0.0 collective-permute-start.10
  51.6 3.1 %collective-permute-done.15.refs_3_ = bf16[64,2048]{1,0:T(8,128)(2,1)S(1)} collective-permute-done((bf16[64,2048]{1,0:T(8,128)(2,1)S(1)}, bf16[64,2048]{1,0:T(8,128)(2,1)S(1)}, u32[]{:S(2)}, u32[]{:S(2)}) %collective-permute-start.15) | collective-permute-done | bytes 262176 | tf_op jit(solution)/shard_map/cross1/ppermute | solution.py:22
  54.7 1.6 %collective-permute-start.17 = (bf16[64,2048]{1,0:T(8,128)(2,1)S(1)}, bf16[64,2048]{1,0:T(8,128)(2,1)S(1)}, u32[]{:S(2)}, u32[]{:S(2)}) collective-permute-start(bf16[64,2048]{1,0:T(8,128)(2,1)S(1)} %collective-permute-done.15.refs_3_), channel_id=1, source_target_pairs={{0,2},{1,5},{2,0},{3,7},{4,6},{5,1},{6,4},{7,3},{8,10},{9,13},{10,... | collective-permute-start | bytes 786440 | tf_op jit(solution)/shard_map/A1/ppermute | solution.py:22
  56.3 0.6 collective-permute-start.18
  56.9 1.1 %phase_0.3.refs_0_ = f32[33,64,128]{2,1,0:T(8,128)S(1)} custom-call(s32[5]{0:T(128)S(1)} %select_reduce_fusion.5.starts_ref, s32[416]{0:T(512)S(1)} %broadcast_add_fusion.1.list_ref, bf16[288,128,128]{2,1,0:T(8,128)(2,1)S(1)} %bitcast.8, bf16[64,2048]{1,0:T(8,128)(2,1)S(1)} %collective-permute-done.7.refs_0_, bf16[64,2048]{1,0:T(8,128)(2,1)S(1)} %collective-permute-done.8.refs_1_), custom_call_target="tpu_custom_call" | custom-call | flops 2000000000 | bytes 6000000 | tf_op jit(solution)/shard_map/phase_0/pallas_call | solution.py:131
  58.0 0.9 %collective-permute-done.9.refs_1_ = bf16[64,2048]{1,0:T(8,128)(2,1)S(1)} collective-permute-done((bf16[64,2048]{1,0:T(8,128)(2,1)S(1)}, bf16[64,2048]{1,0:T(8,128)(2,1)S(1)}, u32[]{:S(2)}, u32[]{:S(2)}) %collective-permute-start.9) | collective-permute-done | bytes 262176 | tf_op jit(solution)/shard_map/A0/ppermute | solution.py:22
  58.9 0.8 %collective-permute-start.11 = (bf16[64,2048]{1,0:T(8,128)(2,1)S(1)}, bf16[64,2048]{1,0:T(8,128)(2,1)S(1)}, u32[]{:S(2)}, u32[]{:S(2)}) collective-permute-start(bf16[64,2048]{1,0:T(8,128)(2,1)S(1)} %collective-permute-done.9.refs_1_), channel_id=1, source_target_pairs={{0,1},{1,0},{2,3},{3,2},{4,5},{5,4},{6,7},{7,6},{8,9},{9,8},{10,11... | collective-permute-start | bytes 786440 | tf_op jit(solution)/shard_map/AC0/ppermute | solution.py:22
  59.7 1.1 %collective-permute-done.10.refs_2_ = bf16[64,2048]{1,0:T(8,128)(2,1)S(1)} collective-permute-done((bf16[64,2048]{1,0:T(8,128)(2,1)S(1)}, bf16[64,2048]{1,0:T(8,128)(2,1)S(1)}, u32[]{:S(2)}, u32[]{:S(2)}) %collective-permute-start.10) | collective-permute-done | bytes 262176 | tf_op jit(solution)/shard_map/B0/ppermute | solution.py:22
  60.8 0.0 collective-permute-start.12
  60.8 0.0 collective-permute-start.13
  60.8 3.7 %collective-permute-done.17.refs_5_ = bf16[64,2048]{1,0:T(8,128)(2,1)S(1)} collective-permute-done((bf16[64,2048]{1,0:T(8,128)(2,1)S(1)}, bf16[64,2048]{1,0:T(8,128)(2,1)S(1)}, u32[]{:S(2)}, u32[]{:S(2)}) %collective-permute-start.17) | collective-permute-done | bytes 262176 | tf_op jit(solution)/shard_map/A1/ppermute | solution.py:22
  64.5 0.1 collective-permute-start.21
  64.6 1.2 %collective-permute-done.18.refs_6_ = bf16[64,2048]{1,0:T(8,128)(2,1)S(1)} collective-permute-done((bf16[64,2048]{1,0:T(8,128)(2,1)S(1)}, bf16[64,2048]{1,0:T(8,128)(2,1)S(1)}, u32[]{:S(2)}, u32[]{:S(2)}) %collective-permute-start.18) | collective-permute-done | bytes 262176 | tf_op jit(solution)/shard_map/B1/ppermute | solution.py:22
  65.8 1.3 %collective-permute-start.16 = (bf16[64,2048]{1,0:T(8,128)(2,1)S(1)}, bf16[64,2048]{1,0:T(8,128)(2,1)S(1)}, u32[]{:S(2)}, u32[]{:S(2)}) collective-permute-start(bf16[64,2048]{1,0:T(8,128)(2,1)S(1)} %collective-permute-done.15.refs_3_), channel_id=1, source_target_pairs={{0,1},{1,0},{2,3},{3,2},{4,5},{5,4},{6,7},{7,6},{8,9},{9,8},{10,11... | collective-permute-start | bytes 786440 | tf_op jit(solution)/shard_map/CORE1/ppermute | solution.py:22
  67.1 0.1 collective-permute-start.19
  67.2 0.0 collective-permute-done.12.refs_4_
  67.2 0.4 collective-permute-start.20
  67.7 1.0 %collective-permute-done.13.refs_1_ = bf16[64,2048]{1,0:T(8,128)(2,1)S(1)} collective-permute-done((bf16[64,2048]{1,0:T(8,128)(2,1)S(1)}, bf16[64,2048]{1,0:T(8,128)(2,1)S(1)}, u32[]{:S(2)}, u32[]{:S(2)}) %collective-permute-start.13) | collective-permute-done | bytes 262176 | tf_op jit(solution)/shard_map/E0/ppermute | solution.py:22
  68.6 1.5 %phase_1.3.refs_0_ = f32[33,64,128]{2,1,0:T(8,128)S(1)} custom-call(s32[5]{0:T(128)S(1)} %select_reduce_fusion.5.starts_ref, s32[416]{0:T(512)S(1)} %broadcast_add_fusion.1.list_ref, bf16[288,128,128]{2,1,0:T(8,128)(2,1)S(1)} %bitcast.8, f32[33,64,128]{2,1,0:T(8,128)S(1)} %phase_0.3.refs_0_, ...), custom_call_target="tpu_custom_call", output_to_operand_aliasing={{}: (3, {})} | custom-call | flops 2000000000 | bytes 6000000 | tf_op jit(solution)/shard_map/phase_1/pallas_call | solution.py:131
  70.2 1.3 %collective-permute-done.21.refs_2_ = bf16[64,2048]{1,0:T(8,128)(2,1)S(1)} collective-permute-done((bf16[64,2048]{1,0:T(8,128)(2,1)S(1)}, bf16[64,2048]{1,0:T(8,128)(2,1)S(1)}, u32[]{:S(2)}, u32[]{:S(2)}) %collective-permute-start.21) | collective-permute-done | bytes 262176 | tf_op jit(solution)/shard_map/E1/ppermute | solution.py:22
  71.5 0.0 collective-permute-start.22
  71.5 2.0 %phase_2.3.refs_0_ = f32[33,64,128]{2,1,0:T(8,128)S(1)} custom-call(s32[5]{0:T(128)S(1)} %select_reduce_fusion.5.starts_ref, s32[416]{0:T(512)S(1)} %broadcast_add_fusion.1.list_ref, bf16[288,128,128]{2,1,0:T(8,128)(2,1)S(1)} %bitcast.8, f32[33,64,128]{2,1,0:T(8,128)S(1)} %phase_1.3.refs_0_, ...), custom_call_target="tpu_custom_call", output_to_operand_aliasing={{}: (3, {})} | custom-call | flops 2000000000 | bytes 6000000 | tf_op jit(solution)/shard_map/phase_2/pallas_call | solution.py:131
  73.5 0.0 collective-permute-done.22.refs_3_
  73.5 1.9 %phase_3.3 = (f32[33,64,128]{2,1,0:T(8,128)S(1)}, bf16[64,4096]{1,0:T(8,128)(2,1)}) custom-call(s32[5]{0:T(128)S(1)} %select_reduce_fusion.5.starts_ref, s32[416]{0:T(512)S(1)} %broadcast_add_fusion.1.list_ref, bf16[288,128,128]{2,1,0:T(8,128)(2,1)S(1)} %bitcast.8, f32[33,64,128]{2,1,0:T(8,128)S(1)} %phase_2.3.refs_0_, ...), custom_call_target="tpu_custom_call", output_to_operand_aliasing={{0}: (3, {})} | custom-call | flops 2000000000 | bytes 6000000 | tf_op jit(solution)/shard_map/phase_3/pallas_call | solution.py:131
  (25 shorter events, 0.1 us)
Async XLA Ops:
  0.0 8.0 %collective-permute-start = (bf16[64,4096]{1,0:T(8,128)(2,1)}, bf16[64,4096]{1,0:T(8,128)(2,1)S(1)}, u32[]{:S(2)}, u32[]{:S(2)}) collective-permute-start(bf16[64,4096]{1,0:T(8,128)(2,1)} %bitcast.9), channel_id=1, source_target_pairs={{0,1},{1,0},{2,3},{3,2},{4,5},{5,4},{6,7},{7,6},{8,9},{9,8},{10,11... | collective-permute-start | bytes 1572872 | tf_op jit(solution)/shard_map/core/ppermute | solution.py:22
  0.5 14.3 %collective-permute-start.1 = (bf16[64,4096]{1,0:T(8,128)(2,1)}, bf16[64,4096]{1,0:T(8,128)(2,1)S(1)}, u32[]{:S(2)}, u32[]{:S(2)}) collective-permute-start(bf16[64,4096]{1,0:T(8,128)(2,1)} %bitcast.10), channel_id=1, source_target_pairs={{0,2},{1,5},{2,0},{3,7},{4,6},{5,1},{6,4},{7,3},{8,10},{9,13},{10,... | collective-permute-start | bytes 1572872 | tf_op jit(solution)/shard_map/a/ppermute | solution.py:22
  2.9 12.9 %collective-permute-start.2 = (bf16[64,4096]{1,0:T(8,128)(2,1)}, bf16[64,4096]{1,0:T(8,128)(2,1)S(1)}, u32[]{:S(2)}, u32[]{:S(2)}) collective-permute-start(bf16[64,4096]{1,0:T(8,128)(2,1)} %bitcast.11), channel_id=1, source_target_pairs={{0,4},{1,3},{2,6},{3,1},{4,0},{5,7},{6,2},{7,5},{8,12},{9,11},{10,... | collective-permute-start | bytes 1572872 | tf_op jit(solution)/shard_map/b/ppermute | solution.py:22
  8.0 3.7 %copy-start = (bf16[288,128,128]{2,1,0:T(8,128)(2,1)S(1)}, bf16[288,128,128]{2,1,0:T(8,128)(2,1)}, u32[]{:S(2)}) copy-start(bf16[288,128,128]{2,1,0:T(8,128)(2,1)} %w_ref.17) | copy-start | bytes 28311556
  11.7 1.0 %copy-start.1 = (bf16[1,64,4096]{2,1,0:T(8,128)(2,1)S(1)}, bf16[1,64,4096]{2,1,0:T(8,128)(2,1)}, u32[]{:S(2)}) copy-start(bf16[1,64,4096]{2,1,0:T(8,128)(2,1)} %param.6) | copy-start | bytes 1572868
  14.8 3.3 %collective-permute-start.3 = (bf16[64,4096]{1,0:T(8,128)(2,1)S(1)}, bf16[64,4096]{1,0:T(8,128)(2,1)S(1)}, u32[]{:S(2)}, u32[]{:S(2)}) collective-permute-start(bf16[64,4096]{1,0:T(8,128)(2,1)S(1)} %collective-permute-done.1.refs_1_), channel_id=1, source_target_pairs={{0,1},{1,0},{2,3},{3,2},{4,5},{5,4},{6,7},{7,6},{8,9},{9,8},{10,11... | collective-permute-start | bytes 1572872 | tf_op jit(solution)/shard_map/ac/ppermute | solution.py:22
  15.8 2.3 %collective-permute-start.4 = (bf16[64,4096]{1,0:T(8,128)(2,1)S(1)}, bf16[64,4096]{1,0:T(8,128)(2,1)S(1)}, u32[]{:S(2)}, u32[]{:S(2)}) collective-permute-start(bf16[64,4096]{1,0:T(8,128)(2,1)S(1)} %collective-permute-done.2.refs_2_), channel_id=1, source_target_pairs={{0,1},{1,0},{2,3},{3,2},{4,5},{5,4},{6,7},{7,6},{8,9},{9,8},{10,11... | collective-permute-start | bytes 1572872 | tf_op jit(solution)/shard_map/bc/ppermute | solution.py:22
  15.9 9.3 %collective-permute-start.5 = (bf16[64,4096]{1,0:T(8,128)(2,1)S(1)}, bf16[64,4096]{1,0:T(8,128)(2,1)S(1)}, u32[]{:S(2)}, u32[]{:S(2)}) collective-permute-start(bf16[64,4096]{1,0:T(8,128)(2,1)S(1)} %collective-permute-done.1.refs_1_), channel_id=1, source_target_pairs={{0,4},{1,3},{2,6},{3,1},{4,0},{5,7},{6,2},{7,5},{8,12},{9,11},{10,... | collective-permute-start | bytes 1572872 | tf_op jit(solution)/shard_map/e/ppermute | solution.py:22
  20.1 7.1 %copy-start.2 = (f32[4096]{0:T(1024)S(1)}, f32[4096]{0:T(1024)}, u32[]{:S(2)}) copy-start(f32[4096]{0:T(1024)} %param.11) | copy-start | bytes 49156
  25.3 1.9 %collective-permute-start.6 = (bf16[64,4096]{1,0:T(8,128)(2,1)S(1)}, bf16[64,4096]{1,0:T(8,128)(2,1)S(1)}, u32[]{:S(2)}, u32[]{:S(2)}) collective-permute-start(bf16[64,4096]{1,0:T(8,128)(2,1)S(1)} %collective-permute-done.5.refs_1_), channel_id=1, source_target_pairs={{0,1},{1,0},{2,3},{3,2},{4,5},{5,4},{6,7},{7,6},{8,9},{9,8},{10,11... | collective-permute-start | bytes 1572872 | tf_op jit(solution)/shard_map/ec/ppermute | solution.py:22
  27.2 29.7 %slice-start = ((s8[9437184]{0:T(1024)(128)(4,1)}), s8[4194304]{0:T(1024)(128)(4,1)S(1)}, s32[]{:S(2)}) async-start(s8[9437184]{0:T(1024)(128)(4,1)} %bitcast.7), calls=%async_computation | async-start | bytes 8388608
  27.2 29.7 %slice-start.1 = ((s8[9437184]{0:T(1024)(128)(4,1)}), s8[4194304]{0:T(1024)(128)(4,1)S(1)}, s32[]{:S(2)}) async-start(s8[9437184]{0:T(1024)(128)(4,1)} %bitcast.7), calls=%async_computation.1 | async-start | bytes 8388608
  28.3 21.3 %collective-permute-start.7 = (bf16[64,2048]{1,0:T(8,128)(2,1)S(1)}, bf16[64,2048]{1,0:T(8,128)(2,1)S(1)}, u32[]{:S(2)}, u32[]{:S(2)}) collective-permute-start(bf16[64,2048]{1,0:T(8,128)(2,1)S(1)} %get-tuple-element.16), channel_id=1, source_target_pairs={{0,8},{1,9},{2,10},{3,11},{4,12},{5,13},{6,14},{7,15},{8,0},{9,1},... | collective-permute-start | bytes 786440 | tf_op jit(solution)/shard_map/cross0/ppermute | solution.py:22
  31.1 25.7 %slice-start.2 = ((s8[9437184]{0:T(1024)(128)(4,1)}), s8[1048576]{0:T(1024)(128)(4,1)S(1)}, s32[]{:S(2)}) async-start(s8[9437184]{0:T(1024)(128)(4,1)} %bitcast.7), calls=%async_computation.2 | async-start | bytes 2097152
  32.2 22.5 %collective-permute-start.15 = (bf16[64,2048]{1,0:T(8,128)(2,1)S(1)}, bf16[64,2048]{1,0:T(8,128)(2,1)S(1)}, u32[]{:S(2)}, u32[]{:S(2)}) collective-permute-start(bf16[64,2048]{1,0:T(8,128)(2,1)S(1)} %get-tuple-element.18), channel_id=1, source_target_pairs={{0,8},{1,9},{2,10},{3,11},{4,12},{5,13},{6,14},{7,15},{8,0},{9,1},... | collective-permute-start | bytes 786440 | tf_op jit(solution)/shard_map/cross1/ppermute | solution.py:22
  49.6 7.3 %collective-permute-start.8 = (bf16[64,2048]{1,0:T(8,128)(2,1)S(1)}, bf16[64,2048]{1,0:T(8,128)(2,1)S(1)}, u32[]{:S(2)}, u32[]{:S(2)}) collective-permute-start(bf16[64,2048]{1,0:T(8,128)(2,1)S(1)} %collective-permute-done.7.refs_0_), channel_id=1, source_target_pairs={{0,1},{1,0},{2,3},{3,2},{4,5},{5,4},{6,7},{7,6},{8,9},{9,8},{10,11... | collective-permute-start | bytes 786440 | tf_op jit(solution)/shard_map/CORE0/ppermute | solution.py:22
  49.8 9.2 %collective-permute-start.9 = (bf16[64,2048]{1,0:T(8,128)(2,1)S(1)}, bf16[64,2048]{1,0:T(8,128)(2,1)S(1)}, u32[]{:S(2)}, u32[]{:S(2)}) collective-permute-start(bf16[64,2048]{1,0:T(8,128)(2,1)S(1)} %collective-permute-done.7.refs_0_), channel_id=1, source_target_pairs={{0,2},{1,5},{2,0},{3,7},{4,6},{5,1},{6,4},{7,3},{8,10},{9,13},{10,... | collective-permute-start | bytes 786440 | tf_op jit(solution)/shard_map/A0/ppermute | solution.py:22
  51.6 9.2 %collective-permute-start.10 = (bf16[64,2048]{1,0:T(8,128)(2,1)S(1)}, bf16[64,2048]{1,0:T(8,128)(2,1)S(1)}, u32[]{:S(2)}, u32[]{:S(2)}) collective-permute-start(bf16[64,2048]{1,0:T(8,128)(2,1)S(1)} %collective-permute-done.7.refs_0_), channel_id=1, source_target_pairs={{0,4},{1,3},{2,6},{3,1},{4,0},{5,7},{6,2},{7,5},{8,12},{9,11},{10,... | collective-permute-start | bytes 786440 | tf_op jit(solution)/shard_map/B0/ppermute | solution.py:22
  54.7 9.8 %collective-permute-start.17 = (bf16[64,2048]{1,0:T(8,128)(2,1)S(1)}, bf16[64,2048]{1,0:T(8,128)(2,1)S(1)}, u32[]{:S(2)}, u32[]{:S(2)}) collective-permute-start(bf16[64,2048]{1,0:T(8,128)(2,1)S(1)} %collective-permute-done.15.refs_3_), channel_id=1, source_target_pairs={{0,2},{1,5},{2,0},{3,7},{4,6},{5,1},{6,4},{7,3},{8,10},{9,13},{10,... | collective-permute-start | bytes 786440 | tf_op jit(solution)/shard_map/A1/ppermute | solution.py:22
  56.3 9.6 %collective-permute-start.18 = (bf16[64,2048]{1,0:T(8,128)(2,1)S(1)}, bf16[64,2048]{1,0:T(8,128)(2,1)S(1)}, u32[]{:S(2)}, u32[]{:S(2)}) collective-permute-start(bf16[64,2048]{1,0:T(8,128)(2,1)S(1)} %collective-permute-done.15.refs_3_), channel_id=1, source_target_pairs={{0,4},{1,3},{2,6},{3,1},{4,0},{5,7},{6,2},{7,5},{8,12},{9,11},{10,... | collective-permute-start | bytes 786440 | tf_op jit(solution)/shard_map/B1/ppermute | solution.py:22
  58.9 8.2 %collective-permute-start.11 = (bf16[64,2048]{1,0:T(8,128)(2,1)S(1)}, bf16[64,2048]{1,0:T(8,128)(2,1)S(1)}, u32[]{:S(2)}, u32[]{:S(2)}) collective-permute-start(bf16[64,2048]{1,0:T(8,128)(2,1)S(1)} %collective-permute-done.9.refs_1_), channel_id=1, source_target_pairs={{0,1},{1,0},{2,3},{3,2},{4,5},{5,4},{6,7},{7,6},{8,9},{9,8},{10,11... | collective-permute-start | bytes 786440 | tf_op jit(solution)/shard_map/AC0/ppermute | solution.py:22
  60.8 6.4 %collective-permute-start.12 = (bf16[64,2048]{1,0:T(8,128)(2,1)S(1)}, bf16[64,2048]{1,0:T(8,128)(2,1)S(1)}, u32[]{:S(2)}, u32[]{:S(2)}) collective-permute-start(bf16[64,2048]{1,0:T(8,128)(2,1)S(1)} %collective-permute-done.10.refs_2_), channel_id=1, source_target_pairs={{0,1},{1,0},{2,3},{3,2},{4,5},{5,4},{6,7},{7,6},{8,9},{9,8},{10,11... | collective-permute-start | bytes 786440 | tf_op jit(solution)/shard_map/BC0/ppermute | solution.py:22
  60.8 7.8 %collective-permute-start.13 = (bf16[64,2048]{1,0:T(8,128)(2,1)S(1)}, bf16[64,2048]{1,0:T(8,128)(2,1)S(1)}, u32[]{:S(2)}, u32[]{:S(2)}) collective-permute-start(bf16[64,2048]{1,0:T(8,128)(2,1)S(1)} %collective-permute-done.9.refs_1_), channel_id=1, source_target_pairs={{0,4},{1,3},{2,6},{3,1},{4,0},{5,7},{6,2},{7,5},{8,12},{9,11},{10,... | collective-permute-start | bytes 786440 | tf_op jit(solution)/shard_map/E0/ppermute | solution.py:22
  64.5 6.9 %collective-permute-start.21 = (bf16[64,2048]{1,0:T(8,128)(2,1)S(1)}, bf16[64,2048]{1,0:T(8,128)(2,1)S(1)}, u32[]{:S(2)}, u32[]{:S(2)}) collective-permute-start(bf16[64,2048]{1,0:T(8,128)(2,1)S(1)} %collective-permute-done.17.refs_5_), channel_id=1, source_target_pairs={{0,4},{1,3},{2,6},{3,1},{4,0},{5,7},{6,2},{7,5},{8,12},{9,11},{10,... | collective-permute-start | bytes 786440 | tf_op jit(solution)/shard_map/E1/ppermute | solution.py:22
  65.8 5.6 %collective-permute-start.16 = (bf16[64,2048]{1,0:T(8,128)(2,1)S(1)}, bf16[64,2048]{1,0:T(8,128)(2,1)S(1)}, u32[]{:S(2)}, u32[]{:S(2)}) collective-permute-start(bf16[64,2048]{1,0:T(8,128)(2,1)S(1)} %collective-permute-done.15.refs_3_), channel_id=1, source_target_pairs={{0,1},{1,0},{2,3},{3,2},{4,5},{5,4},{6,7},{7,6},{8,9},{9,8},{10,11... | collective-permute-start | bytes 786440 | tf_op jit(solution)/shard_map/CORE1/ppermute | solution.py:22
  67.1 4.3 %collective-permute-start.19 = (bf16[64,2048]{1,0:T(8,128)(2,1)S(1)}, bf16[64,2048]{1,0:T(8,128)(2,1)S(1)}, u32[]{:S(2)}, u32[]{:S(2)}) collective-permute-start(bf16[64,2048]{1,0:T(8,128)(2,1)S(1)} %collective-permute-done.17.refs_5_), channel_id=1, source_target_pairs={{0,1},{1,0},{2,3},{3,2},{4,5},{5,4},{6,7},{7,6},{8,9},{9,8},{10,11... | collective-permute-start | bytes 786440 | tf_op jit(solution)/shard_map/AC1/ppermute | solution.py:22
  67.2 4.3 %collective-permute-start.20 = (bf16[64,2048]{1,0:T(8,128)(2,1)S(1)}, bf16[64,2048]{1,0:T(8,128)(2,1)S(1)}, u32[]{:S(2)}, u32[]{:S(2)}) collective-permute-start(bf16[64,2048]{1,0:T(8,128)(2,1)S(1)} %collective-permute-done.18.refs_6_), channel_id=1, source_target_pairs={{0,1},{1,0},{2,3},{3,2},{4,5},{5,4},{6,7},{7,6},{8,9},{9,8},{10,11... | collective-permute-start | bytes 786440 | tf_op jit(solution)/shard_map/BC1/ppermute | solution.py:22
  68.6 2.8 %collective-permute-start.14 = (bf16[64,2048]{1,0:T(8,128)(2,1)S(1)}, bf16[64,2048]{1,0:T(8,128)(2,1)S(1)}, u32[]{:S(2)}, u32[]{:S(2)}) collective-permute-start(bf16[64,2048]{1,0:T(8,128)(2,1)S(1)} %collective-permute-done.13.refs_1_), channel_id=1, source_target_pairs={{0,1},{1,0},{2,3},{3,2},{4,5},{5,4},{6,7},{7,6},{8,9},{9,8},{10,11... | collective-permute-start | bytes 786440 | tf_op jit(solution)/shard_map/EC0/ppermute | solution.py:22
  71.5 2.1 %collective-permute-start.22 = (bf16[64,2048]{1,0:T(8,128)(2,1)S(1)}, bf16[64,2048]{1,0:T(8,128)(2,1)S(1)}, u32[]{:S(2)}, u32[]{:S(2)}) collective-permute-start(bf16[64,2048]{1,0:T(8,128)(2,1)S(1)} %collective-permute-done.21.refs_2_), channel_id=1, source_target_pairs={{0,1},{1,0},{2,3},{3,2},{4,5},{5,4},{6,7},{7,6},{8,9},{9,8},{10,11... | collective-permute-start | bytes 786440 | tf_op jit(solution)/shard_map/EC1/ppermute | solution.py:22

commit v7 on v6

--- a/solution.py
+++ b/solution.py
@@ -156,8 +156,8 @@
 ) + tuple(blocks(7, columns=(k,)) for k in ALL)
 LATER_PHASES = (
     blocks((0, 0), (1, 0)),
-    blocks(*((p, 0) for p in range(2, 6))),
-    blocks((6, 0), (7, 0), *((p, 1) for p in range(6))),
+    blocks(*((p, 0) for p in range(2, 6)), (0, 1)),
+    blocks((6, 0), (7, 0), *((p, 1) for p in range(1, 6))),
     blocks((6, 1), (7, 1)),
 )
 
@@ -197,7 +197,9 @@
         if k == 0:
             a = after(a, acc)
         e = across_second(a, f"E{k}")
-        pieces = [*late, *([own, core[k]] if k else []), a, b, across_core(a, f"AC{k}"), across_core(b, f"BC{k}")]
+        pieces = [*late, *core[1:1 + k], a, b, across_core(a, f"AC{k}"), across_core(b, f"BC{k}")]
+        if k == 0:
+            pieces.append(parts[1])
         if k:
             e = after(e, acc)
         late = [e, across_core(e, f"EC{k}")]

time: 76 us -> 75.5 us (level)
  transfers between devices with their start and end apart: 23 -> 23, of which waited for: 12 -> 12; matrix products, arithmetic and copies ran while one was open for 4% -> 4% of each run, Pallas kernels for 14% -> 13%
where the time goes in v7:
time: 75.5 us; the launch traced here: 75.4 us
  waiting for transfers between devices  37.5 us (50%)
  starting transfers between devices  16.5 us (22%)
  Pallas kernels  12.9 us (17%)
  local copies, waits for them, and re-layouts  4.73 us (6%)
  other arithmetic  2.91 us (4%)
  between operations  0.86 us (1%)
    ppermute x23, waiting for transfers between devices, sent(): lax.ppermute(array, 'section', [(i, target(i, peers)) for i in range(peer...  37.5 us
    ppermute x23, starting transfers between devices, sent(): lax.ppermute(array, 'section', [(i, target(i, peers)) for i in range(peer...  16.5 us
    pallas_call x9, Pallas kernels, run_phase(): pl.pallas_call(functools.partial(phase_kernel, phase, len(pieces), first,...  12.9 us
    unnamed x12, local copies, waits for them, and re-layouts  4.73 us
  transfers between devices with their start and end apart: 23, of which 12 were waited for; matrix products, arithmetic and copies ran while one was open for 4% of the time, Pallas kernels for 13%

profile of v7, /device:TPU:0, one launch (start us, length us, event | category | flops | bytes accessed | tf_op | source)
XLA Modules:
  0.0 75.4 jit_solution(5319202463041416362)
XLA Ops:
  0.0 0.5 collective-permute-start
  0.5 2.5 %collective-permute-start.1 = (bf16[64,4096]{1,0:T(8,128)(2,1)}, bf16[64,4096]{1,0:T(8,128)(2,1)S(1)}, u32[]{:S(2)}, u32[]{:S(2)}) collective-permute-start(bf16[64,4096]{1,0:T(8,128)(2,1)} %bitcast.10), channel_id=1, source_target_pairs={{0,2},{1,5},{2,0},{3,7},{4,6},{5,1},{6,4},{7,3},{8,10},{9,13},{10,... | collective-permute-start | bytes 1572872 | tf_op jit(solution)/shard_map/a/ppermute | solution.py:22
  2.9 1.6 %collective-permute-start.2 = (bf16[64,4096]{1,0:T(8,128)(2,1)}, bf16[64,4096]{1,0:T(8,128)(2,1)S(1)}, u32[]{:S(2)}, u32[]{:S(2)}) collective-permute-start(bf16[64,4096]{1,0:T(8,128)(2,1)} %bitcast.11), channel_id=1, source_target_pairs={{0,4},{1,3},{2,6},{3,1},{4,0},{5,7},{6,2},{7,5},{8,12},{9,11},{10,... | collective-permute-start | bytes 1572872 | tf_op jit(solution)/shard_map/b/ppermute | solution.py:22
  5.2 0.7 add_add_fusion
  5.9 0.1 convert_reduce_fusion.2
  6.1 0.2 convert_reduce_fusion
  6.3 0.7 fusion.13
  7.0 0.1 convert_reduce_fusion.3
  7.2 0.2 convert_reduce_fusion.1
  7.4 0.1 select_reduce_fusion.5.starts_ref
  7.5 0.1 select_reduce_fusion.4.starts_ref
  7.6 0.1 select_reduce_fusion.2
  7.7 0.1 select_reduce_fusion.3
  7.8 0.2 select_reduce_fusion
  8.0 0.0 collective-permute-done.refs_1_
  8.0 0.0 copy-start
  8.0 3.7 %copy-done = bf16[288,128,128]{2,1,0:T(8,128)(2,1)S(1)} copy-done((bf16[288,128,128]{2,1,0:T(8,128)(2,1)S(1)}, bf16[288,128,128]{2,1,0:T(8,128)(2,1)}, u32[]{:S(2)}) %copy-start) | copy-done | bytes 9437208
  11.7 1.0 %copy-done.1 = bf16[1,64,4096]{2,1,0:T(8,128)(2,1)S(1)} copy-done((bf16[1,64,4096]{2,1,0:T(8,128)(2,1)S(1)}, bf16[1,64,4096]{2,1,0:T(8,128)(2,1)}, u32[]{:S(2)}) %copy-start.1) | copy-done | bytes 524312
  12.7 1.6 %phase_0.2.refs_0_ = f32[33,64,128]{2,1,0:T(8,128)S(1)} custom-call(s32[6]{0:T(128)S(1)} %select_reduce_fusion.4.starts_ref, s32[448]{0:T(512)S(1)} %broadcast_add_fusion.list_ref, bf16[288,128,128]{2,1,0:T(8,128)(2,1)S(1)} %copy-done, bf16[64,4096]{1,0:T(8,128)(2,1)S(1)} %bitcast.12, bf16[64,4096]{1,0:T(8,128)(2,1)S(1)} %collective-permute-done.refs_1_), custom_call_target="tpu_custom_call" | custom-call | flops 2000000000 | bytes 6000000 | tf_op jit(solution)/shard_map/phase_0/pallas_call | solution.py:131
  14.3 0.5 collective-permute-done.1.refs_1_
  14.8 0.0 collective-permute-start.3
  14.8 1.1 %collective-permute-done.2.refs_2_ = bf16[64,4096]{1,0:T(8,128)(2,1)S(1)} collective-permute-done((bf16[64,4096]{1,0:T(8,128)(2,1)}, bf16[64,4096]{1,0:T(8,128)(2,1)S(1)}, u32[]{:S(2)}, u32[]{:S(2)}) %collective-permute-start.2) | collective-permute-done | bytes 524320 | tf_op jit(solution)/shard_map/b/ppermute | solution.py:22
  15.8 0.1 collective-permute-start.4
  15.9 2.1 %collective-permute-start.5 = (bf16[64,4096]{1,0:T(8,128)(2,1)S(1)}, bf16[64,4096]{1,0:T(8,128)(2,1)S(1)}, u32[]{:S(2)}, u32[]{:S(2)}) collective-permute-start(bf16[64,4096]{1,0:T(8,128)(2,1)S(1)} %collective-permute-done.1.refs_1_), channel_id=1, source_target_pairs={{0,4},{1,3},{2,6},{3,1},{4,0},{5,7},{6,2},{7,5},{8,12},{9,11},{10,... | collective-permute-start | bytes 1572872 | tf_op jit(solution)/shard_map/e/ppermute | solution.py:22
  18.1 0.0 collective-permute-done.3.refs_3_
  18.1 0.0 collective-permute-done.4.refs_4_
  18.1 1.6 %phase_1.2.refs_0_ = f32[33,64,128]{2,1,0:T(8,128)S(1)} custom-call(s32[6]{0:T(128)S(1)} %select_reduce_fusion.4.starts_ref, s32[448]{0:T(512)S(1)} %broadcast_add_fusion.list_ref, bf16[288,128,128]{2,1,0:T(8,128)(2,1)S(1)} %copy-done, f32[33,64,128]{2,1,0:T(8,128)S(1)} %phase_0.2.refs_0_, ...), custom_call_target="tpu_custom_call", output_to_operand_aliasing={{}: (3, {})} | custom-call | flops 2000000000 | bytes 6000000 | tf_op jit(solution)/shard_map/phase_1/pallas_call | solution.py:131
  19.7 0.0 copy-start.2
  19.7 5.6 %collective-permute-done.5.refs_1_ = bf16[64,4096]{1,0:T(8,128)(2,1)S(1)} collective-permute-done((bf16[64,4096]{1,0:T(8,128)(2,1)S(1)}, bf16[64,4096]{1,0:T(8,128)(2,1)S(1)}, u32[]{:S(2)}, u32[]{:S(2)}) %collective-permute-start.5) | collective-permute-done | bytes 524320 | tf_op jit(solution)/shard_map/e/ppermute | solution.py:22
  25.3 0.0 collective-permute-start.6
  25.3 1.0 %phase_2.2.refs_0_ = f32[33,64,128]{2,1,0:T(8,128)S(1)} custom-call(s32[6]{0:T(128)S(1)} %select_reduce_fusion.4.starts_ref, s32[448]{0:T(512)S(1)} %broadcast_add_fusion.list_ref, bf16[288,128,128]{2,1,0:T(8,128)(2,1)S(1)} %copy-done, f32[33,64,128]{2,1,0:T(8,128)S(1)} %phase_1.2.refs_0_, ...), custom_call_target="tpu_custom_call", output_to_operand_aliasing={{}: (3, {})} | custom-call | flops 2000000000 | bytes 6000000 | tf_op jit(solution)/shard_map/phase_2/pallas_call | solution.py:131
  26.3 0.9 %collective-permute-done.6.refs_2_ = bf16[64,4096]{1,0:T(8,128)(2,1)S(1)} collective-permute-done((bf16[64,4096]{1,0:T(8,128)(2,1)S(1)}, bf16[64,4096]{1,0:T(8,128)(2,1)S(1)}, u32[]{:S(2)}, u32[]{:S(2)}) %collective-permute-start.6) | collective-permute-done | bytes 524320 | tf_op jit(solution)/shard_map/ec/ppermute | solution.py:22
  27.2 1.1 %phase_3.2 = (f32[33,64,128]{2,1,0:T(8,128)S(1)}, bf16[64,2048]{1,0:T(8,128)(2,1)S(1)}) custom-call(s32[6]{0:T(128)S(1)} %select_reduce_fusion.4.starts_ref, s32[448]{0:T(512)S(1)} %broadcast_add_fusion.list_ref, bf16[288,128,128]{2,1,0:T(8,128)(2,1)S(1)} %copy-done, f32[33,64,128]{2,1,0:T(8,128)S(1)} %phase_2.2.refs_0_, ...), custom_call_target="tpu_custom_call", output_to_operand_aliasing={{0}: (3, {})} | custom-call | flops 2000000000 | bytes 6000000 | tf_op jit(solution)/shard_map/phase_3/pallas_call | solution.py:131
  28.3 2.9 %collective-permute-start.7 = (bf16[64,2048]{1,0:T(8,128)(2,1)S(1)}, bf16[64,2048]{1,0:T(8,128)(2,1)S(1)}, u32[]{:S(2)}, u32[]{:S(2)}) collective-permute-start(bf16[64,2048]{1,0:T(8,128)(2,1)S(1)} %get-tuple-element.16), channel_id=1, source_target_pairs={{0,8},{1,9},{2,10},{3,11},{4,12},{5,13},{6,14},{7,15},{8,0},{9,1},... | collective-permute-start | bytes 786440 | tf_op jit(solution)/shard_map/cross0/ppermute | solution.py:22
  31.1 1.1 %phase_4.1 = (f32[33,64,128]{2,1,0:T(8,128)S(1)}, bf16[64,2048]{1,0:T(8,128)(2,1)S(1)}) custom-call(s32[6]{0:T(128)S(1)} %select_reduce_fusion.4.starts_ref, s32[448]{0:T(512)S(1)} %broadcast_add_fusion.list_ref, bf16[288,128,128]{2,1,0:T(8,128)(2,1)S(1)} %copy-done, f32[33,64,128]{2,1,0:T(8,128)S(1)} %get-tuple-element.17.refs_0_, ...), custom_call_target="tpu_custom_call", output_to_operand_aliasing={{0}: (3, {})} | custom-call | flops 2000000000 | bytes 6000000 | tf_op jit(solution)/shard_map/phase_4/pallas_call | solution.py:131
  32.2 0.2 collective-permute-start.13
  32.4 17.2 %collective-permute-done.7.refs_0_ = bf16[64,2048]{1,0:T(8,128)(2,1)S(1)} collective-permute-done((bf16[64,2048]{1,0:T(8,128)(2,1)S(1)}, bf16[64,2048]{1,0:T(8,128)(2,1)S(1)}, u32[]{:S(2)}, u32[]{:S(2)}) %collective-permute-start.7) | collective-permute-done | bytes 262176 | tf_op jit(solution)/shard_map/cross0/ppermute | solution.py:22
  49.6 0.0 collective-permute-start.8
  49.6 0.2 select_reduce_fusion.1
  49.8 1.8 %collective-permute-start.9 = (bf16[64,2048]{1,0:T(8,128)(2,1)S(1)}, bf16[64,2048]{1,0:T(8,128)(2,1)S(1)}, u32[]{:S(2)}, u32[]{:S(2)}) collective-permute-start(bf16[64,2048]{1,0:T(8,128)(2,1)S(1)} %collective-permute-done.7.refs_0_), channel_id=1, source_target_pairs={{0,2},{1,5},{2,0},{3,7},{4,6},{5,1},{6,4},{7,3},{8,10},{9,13},{10,... | collective-permute-start | bytes 786440 | tf_op jit(solution)/shard_map/A0/ppermute | solution.py:22
  51.6 3.1 %collective-permute-done.13.refs_5_ = bf16[64,2048]{1,0:T(8,128)(2,1)S(1)} collective-permute-done((bf16[64,2048]{1,0:T(8,128)(2,1)S(1)}, bf16[64,2048]{1,0:T(8,128)(2,1)S(1)}, u32[]{:S(2)}, u32[]{:S(2)}) %collective-permute-start.13) | collective-permute-done | bytes 262176 | tf_op jit(solution)/shard_map/cross1/ppermute | solution.py:22
  54.7 1.6 %collective-permute-start.17 = (bf16[64,2048]{1,0:T(8,128)(2,1)S(1)}, bf16[64,2048]{1,0:T(8,128)(2,1)S(1)}, u32[]{:S(2)}, u32[]{:S(2)}) collective-permute-start(bf16[64,2048]{1,0:T(8,128)(2,1)S(1)} %collective-permute-done.13.refs_5_), channel_id=1, source_target_pairs={{0,2},{1,5},{2,0},{3,7},{4,6},{5,1},{6,4},{7,3},{8,10},{9,13},{10,... | collective-permute-start | bytes 786440 | tf_op jit(solution)/shard_map/A1/ppermute | solution.py:22
  56.3 0.6 collective-permute-start.18
  56.9 1.1 %phase_0.3.refs_0_ = f32[33,64,128]{2,1,0:T(8,128)S(1)} custom-call(s32[5]{0:T(128)S(1)} %select_reduce_fusion.5.starts_ref, s32[416]{0:T(512)S(1)} %broadcast_add_fusion.1.list_ref, bf16[288,128,128]{2,1,0:T(8,128)(2,1)S(1)} %bitcast.8, bf16[64,2048]{1,0:T(8,128)(2,1)S(1)} %collective-permute-done.7.refs_0_, bf16[64,2048]{1,0:T(8,128)(2,1)S(1)} %collective-permute-done.8.refs_1_), custom_call_target="tpu_custom_call" | custom-call | flops 2000000000 | bytes 6000000 | tf_op jit(solution)/shard_map/phase_0/pallas_call | solution.py:131
  58.0 0.9 %collective-permute-done.9.refs_1_ = bf16[64,2048]{1,0:T(8,128)(2,1)S(1)} collective-permute-done((bf16[64,2048]{1,0:T(8,128)(2,1)S(1)}, bf16[64,2048]{1,0:T(8,128)(2,1)S(1)}, u32[]{:S(2)}, u32[]{:S(2)}) %collective-permute-start.9) | collective-permute-done | bytes 262176 | tf_op jit(solution)/shard_map/A0/ppermute | solution.py:22
  58.9 0.8 %collective-permute-start.11 = (bf16[64,2048]{1,0:T(8,128)(2,1)S(1)}, bf16[64,2048]{1,0:T(8,128)(2,1)S(1)}, u32[]{:S(2)}, u32[]{:S(2)}) collective-permute-start(bf16[64,2048]{1,0:T(8,128)(2,1)S(1)} %collective-permute-done.9.refs_1_), channel_id=1, source_target_pairs={{0,1},{1,0},{2,3},{3,2},{4,5},{5,4},{6,7},{7,6},{8,9},{9,8},{10,11... | collective-permute-start | bytes 786440 | tf_op jit(solution)/shard_map/AC0/ppermute | solution.py:22
  59.7 1.1 %collective-permute-done.10.refs_2_ = bf16[64,2048]{1,0:T(8,128)(2,1)S(1)} collective-permute-done((bf16[64,2048]{1,0:T(8,128)(2,1)S(1)}, bf16[64,2048]{1,0:T(8,128)(2,1)S(1)}, u32[]{:S(2)}, u32[]{:S(2)}) %collective-permute-start.10) | collective-permute-done | bytes 262176 | tf_op jit(solution)/shard_map/B0/ppermute | solution.py:22
  60.8 0.0 collective-permute-start.12
  60.8 0.0 collective-permute-start.14
  60.8 3.7 %collective-permute-done.17.refs_4_ = bf16[64,2048]{1,0:T(8,128)(2,1)S(1)} collective-permute-done((bf16[64,2048]{1,0:T(8,128)(2,1)S(1)}, bf16[64,2048]{1,0:T(8,128)(2,1)S(1)}, u32[]{:S(2)}, u32[]{:S(2)}) %collective-permute-start.17) | collective-permute-done | bytes 262176 | tf_op jit(solution)/shard_map/A1/ppermute | solution.py:22
  64.5 0.1 collective-permute-start.21
  64.6 1.2 %collective-permute-done.18.refs_5_ = bf16[64,2048]{1,0:T(8,128)(2,1)S(1)} collective-permute-done((bf16[64,2048]{1,0:T(8,128)(2,1)S(1)}, bf16[64,2048]{1,0:T(8,128)(2,1)S(1)}, u32[]{:S(2)}, u32[]{:S(2)}) %collective-permute-start.18) | collective-permute-done | bytes 262176 | tf_op jit(solution)/shard_map/B1/ppermute | solution.py:22
  65.8 1.3 %collective-permute-start.16 = (bf16[64,2048]{1,0:T(8,128)(2,1)S(1)}, bf16[64,2048]{1,0:T(8,128)(2,1)S(1)}, u32[]{:S(2)}, u32[]{:S(2)}) collective-permute-start(bf16[64,2048]{1,0:T(8,128)(2,1)S(1)} %collective-permute-done.13.refs_5_), channel_id=1, source_target_pairs={{0,1},{1,0},{2,3},{3,2},{4,5},{5,4},{6,7},{7,6},{8,9},{9,8},{10,11... | collective-permute-start | bytes 786440 | tf_op jit(solution)/shard_map/CORE1/ppermute | solution.py:22
  67.1 0.0 collective-permute-done.11.refs_3_
  67.2 0.1 collective-permute-start.19
  67.2 0.0 collective-permute-done.12.refs_4_
  67.2 0.4 collective-permute-start.20
  67.7 1.0 %collective-permute-done.14.refs_1_ = bf16[64,2048]{1,0:T(8,128)(2,1)S(1)} collective-permute-done((bf16[64,2048]{1,0:T(8,128)(2,1)S(1)}, bf16[64,2048]{1,0:T(8,128)(2,1)S(1)}, u32[]{:S(2)}, u32[]{:S(2)}) %collective-permute-start.14) | collective-permute-done | bytes 262176 | tf_op jit(solution)/shard_map/E0/ppermute | solution.py:22
  68.6 1.5 %phase_1.3.refs_0_ = f32[33,64,128]{2,1,0:T(8,128)S(1)} custom-call(s32[5]{0:T(128)S(1)} %select_reduce_fusion.5.starts_ref, s32[416]{0:T(512)S(1)} %broadcast_add_fusion.1.list_ref, bf16[288,128,128]{2,1,0:T(8,128)(2,1)S(1)} %bitcast.8, f32[33,64,128]{2,1,0:T(8,128)S(1)} %phase_0.3.refs_0_, ...), custom_call_target="tpu_custom_call", output_to_operand_aliasing={{}: (3, {})} | custom-call | flops 2000000000 | bytes 6000000 | tf_op jit(solution)/shard_map/phase_1/pallas_call | solution.py:131
  70.2 1.3 %collective-permute-done.21.refs_2_ = bf16[64,2048]{1,0:T(8,128)(2,1)S(1)} collective-permute-done((bf16[64,2048]{1,0:T(8,128)(2,1)S(1)}, bf16[64,2048]{1,0:T(8,128)(2,1)S(1)}, u32[]{:S(2)}, u32[]{:S(2)}) %collective-permute-start.21) | collective-permute-done | bytes 262176 | tf_op jit(solution)/shard_map/E1/ppermute | solution.py:22
  71.5 0.0 collective-permute-start.22
  71.5 2.0 %phase_2.3.refs_0_ = f32[33,64,128]{2,1,0:T(8,128)S(1)} custom-call(s32[5]{0:T(128)S(1)} %select_reduce_fusion.5.starts_ref, s32[416]{0:T(512)S(1)} %broadcast_add_fusion.1.list_ref, bf16[288,128,128]{2,1,0:T(8,128)(2,1)S(1)} %bitcast.8, f32[33,64,128]{2,1,0:T(8,128)S(1)} %phase_1.3.refs_0_, ...), custom_call_target="tpu_custom_call", output_to_operand_aliasing={{}: (3, {})} | custom-call | flops 2000000000 | bytes 6000000 | tf_op jit(solution)/shard_map/phase_2/pallas_call | solution.py:131
  73.5 0.0 collective-permute-done.22.refs_3_
  73.5 1.9 %phase_3.3 = (f32[33,64,128]{2,1,0:T(8,128)S(1)}, bf16[64,4096]{1,0:T(8,128)(2,1)}) custom-call(s32[5]{0:T(128)S(1)} %select_reduce_fusion.5.starts_ref, s32[416]{0:T(512)S(1)} %broadcast_add_fusion.1.list_ref, bf16[288,128,128]{2,1,0:T(8,128)(2,1)S(1)} %bitcast.8, f32[33,64,128]{2,1,0:T(8,128)S(1)} %phase_2.3.refs_0_, ...), custom_call_target="tpu_custom_call", output_to_operand_aliasing={{0}: (3, {})} | custom-call | flops 2000000000 | bytes 6000000 | tf_op jit(solution)/shard_map/phase_3/pallas_call | solution.py:131
  (25 shorter events, 0.1 us)
Async XLA Ops:
  0.0 8.0 %collective-permute-start = (bf16[64,4096]{1,0:T(8,128)(2,1)}, bf16[64,4096]{1,0:T(8,128)(2,1)S(1)}, u32[]{:S(2)}, u32[]{:S(2)}) collective-permute-start(bf16[64,4096]{1,0:T(8,128)(2,1)} %bitcast.9), channel_id=1, source_target_pairs={{0,1},{1,0},{2,3},{3,2},{4,5},{5,4},{6,7},{7,6},{8,9},{9,8},{10,11... | collective-permute-start | bytes 1572872 | tf_op jit(solution)/shard_map/core/ppermute | solution.py:22
  0.5 14.3 %collective-permute-start.1 = (bf16[64,4096]{1,0:T(8,128)(2,1)}, bf16[64,4096]{1,0:T(8,128)(2,1)S(1)}, u32[]{:S(2)}, u32[]{:S(2)}) collective-permute-start(bf16[64,4096]{1,0:T(8,128)(2,1)} %bitcast.10), channel_id=1, source_target_pairs={{0,2},{1,5},{2,0},{3,7},{4,6},{5,1},{6,4},{7,3},{8,10},{9,13},{10,... | collective-permute-start | bytes 1572872 | tf_op jit(solution)/shard_map/a/ppermute | solution.py:22
  2.9 12.9 %collective-permute-start.2 = (bf16[64,4096]{1,0:T(8,128)(2,1)}, bf16[64,4096]{1,0:T(8,128)(2,1)S(1)}, u32[]{:S(2)}, u32[]{:S(2)}) collective-permute-start(bf16[64,4096]{1,0:T(8,128)(2,1)} %bitcast.11), channel_id=1, source_target_pairs={{0,4},{1,3},{2,6},{3,1},{4,0},{5,7},{6,2},{7,5},{8,12},{9,11},{10,... | collective-permute-start | bytes 1572872 | tf_op jit(solution)/shard_map/b/ppermute | solution.py:22
  8.0 3.7 %copy-start = (bf16[288,128,128]{2,1,0:T(8,128)(2,1)S(1)}, bf16[288,128,128]{2,1,0:T(8,128)(2,1)}, u32[]{:S(2)}) copy-start(bf16[288,128,128]{2,1,0:T(8,128)(2,1)} %w_ref.17) | copy-start | bytes 28311556
  11.7 1.0 %copy-start.1 = (bf16[1,64,4096]{2,1,0:T(8,128)(2,1)S(1)}, bf16[1,64,4096]{2,1,0:T(8,128)(2,1)}, u32[]{:S(2)}) copy-start(bf16[1,64,4096]{2,1,0:T(8,128)(2,1)} %param.6) | copy-start | bytes 1572868
  14.8 3.3 %collective-permute-start.3 = (bf16[64,4096]{1,0:T(8,128)(2,1)S(1)}, bf16[64,4096]{1,0:T(8,128)(2,1)S(1)}, u32[]{:S(2)}, u32[]{:S(2)}) collective-permute-start(bf16[64,4096]{1,0:T(8,128)(2,1)S(1)} %collective-permute-done.1.refs_1_), channel_id=1, source_target_pairs={{0,1},{1,0},{2,3},{3,2},{4,5},{5,4},{6,7},{7,6},{8,9},{9,8},{10,11... | collective-permute-start | bytes 1572872 | tf_op jit(solution)/shard_map/ac/ppermute | solution.py:22
  15.8 2.3 %collective-permute-start.4 = (bf16[64,4096]{1,0:T(8,128)(2,1)S(1)}, bf16[64,4096]{1,0:T(8,128)(2,1)S(1)}, u32[]{:S(2)}, u32[]{:S(2)}) collective-permute-start(bf16[64,4096]{1,0:T(8,128)(2,1)S(1)} %collective-permute-done.2.refs_2_), channel_id=1, source_target_pairs={{0,1},{1,0},{2,3},{3,2},{4,5},{5,4},{6,7},{7,6},{8,9},{9,8},{10,11... | collective-permute-start | bytes 1572872 | tf_op jit(solution)/shard_map/bc/ppermute | solution.py:22
  15.9 9.3 %collective-permute-start.5 = (bf16[64,4096]{1,0:T(8,128)(2,1)S(1)}, bf16[64,4096]{1,0:T(8,128)(2,1)S(1)}, u32[]{:S(2)}, u32[]{:S(2)}) collective-permute-start(bf16[64,4096]{1,0:T(8,128)(2,1)S(1)} %collective-permute-done.1.refs_1_), channel_id=1, source_target_pairs={{0,4},{1,3},{2,6},{3,1},{4,0},{5,7},{6,2},{7,5},{8,12},{9,11},{10,... | collective-permute-start | bytes 1572872 | tf_op jit(solution)/shard_map/e/ppermute | solution.py:22
  19.7 7.5 %copy-start.2 = (f32[4096]{0:T(1024)S(1)}, f32[4096]{0:T(1024)}, u32[]{:S(2)}) copy-start(f32[4096]{0:T(1024)} %param.11) | copy-start | bytes 49156
  25.3 1.9 %collective-permute-start.6 = (bf16[64,4096]{1,0:T(8,128)(2,1)S(1)}, bf16[64,4096]{1,0:T(8,128)(2,1)S(1)}, u32[]{:S(2)}, u32[]{:S(2)}) collective-permute-start(bf16[64,4096]{1,0:T(8,128)(2,1)S(1)} %collective-permute-done.5.refs_1_), channel_id=1, source_target_pairs={{0,1},{1,0},{2,3},{3,2},{4,5},{5,4},{6,7},{7,6},{8,9},{9,8},{10,11... | collective-permute-start | bytes 1572872 | tf_op jit(solution)/shard_map/ec/ppermute | solution.py:22
  27.2 29.7 %slice-start = ((s8[9437184]{0:T(1024)(128)(4,1)}), s8[4194304]{0:T(1024)(128)(4,1)S(1)}, s32[]{:S(2)}) async-start(s8[9437184]{0:T(1024)(128)(4,1)} %bitcast.7), calls=%async_computation | async-start | bytes 8388608
  27.2 29.7 %slice-start.1 = ((s8[9437184]{0:T(1024)(128)(4,1)}), s8[4194304]{0:T(1024)(128)(4,1)S(1)}, s32[]{:S(2)}) async-start(s8[9437184]{0:T(1024)(128)(4,1)} %bitcast.7), calls=%async_computation.1 | async-start | bytes 8388608
  28.3 21.3 %collective-permute-start.7 = (bf16[64,2048]{1,0:T(8,128)(2,1)S(1)}, bf16[64,2048]{1,0:T(8,128)(2,1)S(1)}, u32[]{:S(2)}, u32[]{:S(2)}) collective-permute-start(bf16[64,2048]{1,0:T(8,128)(2,1)S(1)} %get-tuple-element.16), channel_id=1, source_target_pairs={{0,8},{1,9},{2,10},{3,11},{4,12},{5,13},{6,14},{7,15},{8,0},{9,1},... | collective-permute-start | bytes 786440 | tf_op jit(solution)/shard_map/cross0/ppermute | solution.py:22
  31.1 25.7 %slice-start.2 = ((s8[9437184]{0:T(1024)(128)(4,1)}), s8[1048576]{0:T(1024)(128)(4,1)S(1)}, s32[]{:S(2)}) async-start(s8[9437184]{0:T(1024)(128)(4,1)} %bitcast.7), calls=%async_computation.2 | async-start | bytes 2097152
  32.2 22.5 %collective-permute-start.13 = (bf16[64,2048]{1,0:T(8,128)(2,1)S(1)}, bf16[64,2048]{1,0:T(8,128)(2,1)S(1)}, u32[]{:S(2)}, u32[]{:S(2)}) collective-permute-start(bf16[64,2048]{1,0:T(8,128)(2,1)S(1)} %get-tuple-element.18), channel_id=1, source_target_pairs={{0,8},{1,9},{2,10},{3,11},{4,12},{5,13},{6,14},{7,15},{8,0},{9,1},... | collective-permute-start | bytes 786440 | tf_op jit(solution)/shard_map/cross1/ppermute | solution.py:22
  49.6 7.3 %collective-permute-start.8 = (bf16[64,2048]{1,0:T(8,128)(2,1)S(1)}, bf16[64,2048]{1,0:T(8,128)(2,1)S(1)}, u32[]{:S(2)}, u32[]{:S(2)}) collective-permute-start(bf16[64,2048]{1,0:T(8,128)(2,1)S(1)} %collective-permute-done.7.refs_0_), channel_id=1, source_target_pairs={{0,1},{1,0},{2,3},{3,2},{4,5},{5,4},{6,7},{7,6},{8,9},{9,8},{10,11... | collective-permute-start | bytes 786440 | tf_op jit(solution)/shard_map/CORE0/ppermute | solution.py:22
  49.8 9.2 %collective-permute-start.9 = (bf16[64,2048]{1,0:T(8,128)(2,1)S(1)}, bf16[64,2048]{1,0:T(8,128)(2,1)S(1)}, u32[]{:S(2)}, u32[]{:S(2)}) collective-permute-start(bf16[64,2048]{1,0:T(8,128)(2,1)S(1)} %collective-permute-done.7.refs_0_), channel_id=1, source_target_pairs={{0,2},{1,5},{2,0},{3,7},{4,6},{5,1},{6,4},{7,3},{8,10},{9,13},{10,... | collective-permute-start | bytes 786440 | tf_op jit(solution)/shard_map/A0/ppermute | solution.py:22
  51.6 9.2 %collective-permute-start.10 = (bf16[64,2048]{1,0:T(8,128)(2,1)S(1)}, bf16[64,2048]{1,0:T(8,128)(2,1)S(1)}, u32[]{:S(2)}, u32[]{:S(2)}) collective-permute-start(bf16[64,2048]{1,0:T(8,128)(2,1)S(1)} %collective-permute-done.7.refs_0_), channel_id=1, source_target_pairs={{0,4},{1,3},{2,6},{3,1},{4,0},{5,7},{6,2},{7,5},{8,12},{9,11},{10,... | collective-permute-start | bytes 786440 | tf_op jit(solution)/shard_map/B0/ppermute | solution.py:22
  54.7 9.8 %collective-permute-start.17 = (bf16[64,2048]{1,0:T(8,128)(2,1)S(1)}, bf16[64,2048]{1,0:T(8,128)(2,1)S(1)}, u32[]{:S(2)}, u32[]{:S(2)}) collective-permute-start(bf16[64,2048]{1,0:T(8,128)(2,1)S(1)} %collective-permute-done.13.refs_5_), channel_id=1, source_target_pairs={{0,2},{1,5},{2,0},{3,7},{4,6},{5,1},{6,4},{7,3},{8,10},{9,13},{10,... | collective-permute-start | bytes 786440 | tf_op jit(solution)/shard_map/A1/ppermute | solution.py:22
  56.3 9.6 %collective-permute-start.18 = (bf16[64,2048]{1,0:T(8,128)(2,1)S(1)}, bf16[64,2048]{1,0:T(8,128)(2,1)S(1)}, u32[]{:S(2)}, u32[]{:S(2)}) collective-permute-start(bf16[64,2048]{1,0:T(8,128)(2,1)S(1)} %collective-permute-done.13.refs_5_), channel_id=1, source_target_pairs={{0,4},{1,3},{2,6},{3,1},{4,0},{5,7},{6,2},{7,5},{8,12},{9,11},{10,... | collective-permute-start | bytes 786440 | tf_op jit(solution)/shard_map/B1/ppermute | solution.py:22
  58.9 8.2 %collective-permute-start.11 = (bf16[64,2048]{1,0:T(8,128)(2,1)S(1)}, bf16[64,2048]{1,0:T(8,128)(2,1)S(1)}, u32[]{:S(2)}, u32[]{:S(2)}) collective-permute-start(bf16[64,2048]{1,0:T(8,128)(2,1)S(1)} %collective-permute-done.9.refs_1_), channel_id=1, source_target_pairs={{0,1},{1,0},{2,3},{3,2},{4,5},{5,4},{6,7},{7,6},{8,9},{9,8},{10,11... | collective-permute-start | bytes 786440 | tf_op jit(solution)/shard_map/AC0/ppermute | solution.py:22
  60.8 6.4 %collective-permute-start.12 = (bf16[64,2048]{1,0:T(8,128)(2,1)S(1)}, bf16[64,2048]{1,0:T(8,128)(2,1)S(1)}, u32[]{:S(2)}, u32[]{:S(2)}) collective-permute-start(bf16[64,2048]{1,0:T(8,128)(2,1)S(1)} %collective-permute-done.10.refs_2_), channel_id=1, source_target_pairs={{0,1},{1,0},{2,3},{3,2},{4,5},{5,4},{6,7},{7,6},{8,9},{9,8},{10,11... | collective-permute-start | bytes 786440 | tf_op jit(solution)/shard_map/BC0/ppermute | solution.py:22
  60.8 7.8 %collective-permute-start.14 = (bf16[64,2048]{1,0:T(8,128)(2,1)S(1)}, bf16[64,2048]{1,0:T(8,128)(2,1)S(1)}, u32[]{:S(2)}, u32[]{:S(2)}) collective-permute-start(bf16[64,2048]{1,0:T(8,128)(2,1)S(1)} %collective-permute-done.9.refs_1_), channel_id=1, source_target_pairs={{0,4},{1,3},{2,6},{3,1},{4,0},{5,7},{6,2},{7,5},{8,12},{9,11},{10,... | collective-permute-start | bytes 786440 | tf_op jit(solution)/shard_map/E0/ppermute | solution.py:22
  64.5 6.9 %collective-permute-start.21 = (bf16[64,2048]{1,0:T(8,128)(2,1)S(1)}, bf16[64,2048]{1,0:T(8,128)(2,1)S(1)}, u32[]{:S(2)}, u32[]{:S(2)}) collective-permute-start(bf16[64,2048]{1,0:T(8,128)(2,1)S(1)} %collective-permute-done.17.refs_4_), channel_id=1, source_target_pairs={{0,4},{1,3},{2,6},{3,1},{4,0},{5,7},{6,2},{7,5},{8,12},{9,11},{10,... | collective-permute-start | bytes 786440 | tf_op jit(solution)/shard_map/E1/ppermute | solution.py:22
  65.8 5.6 %collective-permute-start.16 = (bf16[64,2048]{1,0:T(8,128)(2,1)S(1)}, bf16[64,2048]{1,0:T(8,128)(2,1)S(1)}, u32[]{:S(2)}, u32[]{:S(2)}) collective-permute-start(bf16[64,2048]{1,0:T(8,128)(2,1)S(1)} %collective-permute-done.13.refs_5_), channel_id=1, source_target_pairs={{0,1},{1,0},{2,3},{3,2},{4,5},{5,4},{6,7},{7,6},{8,9},{9,8},{10,11... | collective-permute-start | bytes 786440 | tf_op jit(solution)/shard_map/CORE1/ppermute | solution.py:22
  67.2 4.3 %collective-permute-start.19 = (bf16[64,2048]{1,0:T(8,128)(2,1)S(1)}, bf16[64,2048]{1,0:T(8,128)(2,1)S(1)}, u32[]{:S(2)}, u32[]{:S(2)}) collective-permute-start(bf16[64,2048]{1,0:T(8,128)(2,1)S(1)} %collective-permute-done.17.refs_4_), channel_id=1, source_target_pairs={{0,1},{1,0},{2,3},{3,2},{4,5},{5,4},{6,7},{7,6},{8,9},{9,8},{10,11... | collective-permute-start | bytes 786440 | tf_op jit(solution)/shard_map/AC1/ppermute | solution.py:22
  67.2 4.2 %collective-permute-start.20 = (bf16[64,2048]{1,0:T(8,128)(2,1)S(1)}, bf16[64,2048]{1,0:T(8,128)(2,1)S(1)}, u32[]{:S(2)}, u32[]{:S(2)}) collective-permute-start(bf16[64,2048]{1,0:T(8,128)(2,1)S(1)} %collective-permute-done.18.refs_5_), channel_id=1, source_target_pairs={{0,1},{1,0},{2,3},{3,2},{4,5},{5,4},{6,7},{7,6},{8,9},{9,8},{10,11... | collective-permute-start | bytes 786440 | tf_op jit(solution)/shard_map/BC1/ppermute | solution.py:22
  68.6 2.8 %collective-permute-start.15 = (bf16[64,2048]{1,0:T(8,128)(2,1)S(1)}, bf16[64,2048]{1,0:T(8,128)(2,1)S(1)}, u32[]{:S(2)}, u32[]{:S(2)}) collective-permute-start(bf16[64,2048]{1,0:T(8,128)(2,1)S(1)} %collective-permute-done.14.refs_1_), channel_id=1, source_target_pairs={{0,1},{1,0},{2,3},{3,2},{4,5},{5,4},{6,7},{7,6},{8,9},{9,8},{10,11... | collective-permute-start | bytes 786440 | tf_op jit(solution)/shard_map/EC0/ppermute | solution.py:22
  71.5 2.0 %collective-permute-start.22 = (bf16[64,2048]{1,0:T(8,128)(2,1)S(1)}, bf16[64,2048]{1,0:T(8,128)(2,1)S(1)}, u32[]{:S(2)}, u32[]{:S(2)}) collective-permute-start(bf16[64,2048]{1,0:T(8,128)(2,1)S(1)} %collective-permute-done.21.refs_2_), channel_id=1, source_target_pairs={{0,1},{1,0},{2,3},{3,2},{4,5},{5,4},{6,7},{7,6},{8,9},{9,8},{10,11... | collective-permute-start | bytes 786440 | tf_op jit(solution)/shard_map/EC1/ppermute | solution.py:22
